TPU v7x, 256 devices: a whole 4x4x8 slice. The times are simulated.
256 devices in a mesh: shuf: 4 (over y_lo, core), key: 64 (over x, z, y_hi).
Axes of the slice: x: 4, y: 4 (y_hi: 2, y_lo: 2; y = y_hi * 2 + y_lo), z: 8, core: 2. Of those that a mesh axis runs over, the one named last changes fastest.
Arguments:
- embeddings: bfloat16 [32768, 1024], P(('shuf', 'key')), may hold values from -200 to 200
- labels: int32 [32768], P(('shuf', 'key')), may hold values from 0 to 2047
- order: int32 [256, 128], P(('shuf', 'key')), may hold values from 0 to 127, each once within a row
- head_weight: bfloat16 [1024, 512], replicated, may hold values from -0.1875 to 0.1875
Outputs:
- grad_embeddings: bfloat16 [32768, 1024], P(('shuf', 'key'))
- grad_head: float32 [1024, 512], P('key')
All inputs are finite; a program needn't handle non-finite values.
Results may differ from a plain program's by a relative error of at most 0.0075.
Values may be sent and summed in bfloat16 or wider, within the bound.
No kernel may reach another device: no remote copies, remote signals or barrier semaphores. Data moves between devices by JAX's collectives and lax.ppermute only.
A program may use at most 64 MiB of HBM per device.

v0:
```python
import jax
import jax.numpy as jnp
from jax import lax
from jax.sharding import PartitionSpec as P

exponent_divisor = 0.1
loss_scale = 64.0
epsilon = 1e-06


def tile_terms(query_embeddings, anchor_labels, anchor_index, piece_keys, piece_labels):
    piece_rows = piece_keys.shape[0]
    cosine_score_table = (
        lax.dot_general(
            query_embeddings,
            piece_keys,
            (((1,), (1,)), ((), ())),
            preferred_element_type=jnp.float32,
        )
        / exponent_divisor
    )
    column = jnp.arange(piece_rows, dtype=jnp.int32)
    itself = anchor_index[:, None] == column[None, :]
    exponent = jnp.where(itself, 0.0, jnp.exp(cosine_score_table))
    positive = jnp.logical_and(
        anchor_labels[:, None] == piece_labels[None, :], jnp.logical_not(itself)
    ).astype(jnp.float32)
    return (exponent, positive)


def body(embeddings, labels, order, head_weight):
    row_count = embeddings.shape[0]
    routing = order[0]
    sent_rows = jnp.take(embeddings, routing, axis=0)
    sent_labels = jnp.take(labels, routing, axis=0)
    group_rows, group_labels = (
        lax.all_to_all(sent_rows, "shuf", split_axis=0, concat_axis=0, tiled=True),
        lax.all_to_all(sent_labels, "shuf", split_axis=0, concat_axis=0, tiled=True),
    )
    projected = jnp.dot(group_rows, head_weight, preferred_element_type=jnp.float32)
    row_norm = jnp.sqrt(jnp.sum(projected * projected, axis=1, keepdims=True) + epsilon)
    direction = projected / row_norm
    normed = direction.astype(jnp.bfloat16)
    anchor_index = lax.axis_index("key") * row_count + jnp.arange(row_count, dtype=jnp.int32)
    pieces = (
        lax.all_gather(normed, "key", axis=0, tiled=True),
        lax.all_gather(group_labels, "key", axis=0, tiled=True),
    )
    exponent, positive = tile_terms(normed, group_labels, anchor_index, pieces[0], pieces[1])
    totals = jnp.sum(exponent, axis=1)
    counts = jnp.sum(positive, axis=1)
    floor_count = jnp.maximum(counts, 1.0)
    soft_weight = loss_scale * counts / (floor_count * totals)
    pos_weight = loss_scale / floor_count
    all_soft, all_pos = (
        lax.all_gather(soft_weight, "key", axis=0, tiled=True),
        lax.all_gather(pos_weight, "key", axis=0, tiled=True),
    )
    pieces = (
        lax.all_gather(normed, "key", axis=0, tiled=True),
        lax.all_gather(group_labels, "key", axis=0, tiled=True),
    )
    exponent, positive = tile_terms(normed, group_labels, anchor_index, pieces[0], pieces[1])
    coefficient = (
        (soft_weight[:, None] + all_soft[None, :]) * exponent
        - (pos_weight[:, None] + all_pos[None, :]) * positive
    ).astype(jnp.bfloat16)
    positive_partner = jnp.dot(coefficient, pieces[0], preferred_element_type=jnp.float32)
    positive_pull_derivative = positive_partner / exponent_divisor
    along = jnp.sum(direction * positive_pull_derivative, axis=1, keepdims=True)
    slopes = ((positive_pull_derivative - direction * along) / row_norm).astype(jnp.bfloat16)
    grad_rows = lax.dot_general(
        slopes, head_weight, (((1,), (1,)), ((), ())), preferred_element_type=jnp.float32
    ).astype(jnp.bfloat16)
    returned = lax.all_to_all(grad_rows, "shuf", split_axis=0, concat_axis=0, tiled=True)
    grad_embeddings = jnp.zeros_like(embeddings).at[routing].set(returned)
    summed_all = lax.psum(
        lax.dot_general(
            group_rows, slopes, (((0,), (0,)), ((), ())), preferred_element_type=jnp.float32
        ).astype(jnp.bfloat16),
        "shuf",
    ).astype(jnp.float32)
    grad_head = lax.psum_scatter(summed_all, "key", scatter_dimension=0, tiled=True)
    return (grad_embeddings, grad_head / loss_scale)


def solution(mesh):
    return jax.shard_map(
        body,
        mesh=mesh,
        in_specs=(P(("shuf", "key"), None), P(("shuf", "key")), P(("shuf", "key"), None), P()),
        out_specs=(P(("shuf", "key"), None), P("key", None)),
        check_vma=False,
    )
```

profile of v0, /device:TPU:8, one launch (start us, length us, event | category | flops | bytes accessed | tf_op | source)
XLA Modules:
  0.0 990.7 jit_solution(10155050195612298073)
XLA Ops:
  7.2 0.0 copy-start
  7.2 0.0 copy-start.2
  7.2 0.0 copy-start.1
  7.2 0.0 all-gather.5.cloned.1.call-start
  7.2 0.7 fusion.16
  8.0 0.7 squeeze.9
  8.7 2.0 gather_fusion.1
  10.8 0.1 broadcast_select_fusion
  10.9 8.9 all_to_all.27
  19.8 0.0 copy-done
  19.8 0.4 multiply_reduce_fusion.1
  20.2 0.8 fusion.18
  21.0 0.0 all-gather.5.cloned.1.call-update
  21.0 0.5 broadcast.125
  21.5 0.0 copy-done.2
  21.5 0.6 reduce.10
  22.1 0.1 squeeze.8
  22.2 0.0 copy-done.1
  22.2 1.2 gather_fusion
  23.4 0.1 gather.13
  23.5 0.6 and_select_fusion
  24.1 4.9 all-to-all-start
  28.9 0.0 all-reduce.2.cloned.1.call-start
  28.9 1.7 all-to-all-done
  30.6 0.1 reshape.148
  30.7 0.6 reduce.11
  31.3 0.1 eq.14
  31.4 181.5 %all-gather = s32[64,1,128]{2,1,0:T(1,128)S(1)} all-gather(s32[1,1,128]{2,1,0:T(1,128)S(1)} %reshape.148), channel_id=1, replica_groups=mesh['shuf'=4,'key'=64] {'key'}, dimensions={0}, use_global_device_ids=true | all-gather | bytes 33280 | tf_op jit(solution)/shard_map/all_gather | solution.py:47
  212.8 1.4 convert_reduce_fusion
  214.2 0.0 all-gather.5.cloned.1.call-done
  214.2 0.0 copy-start.3
  214.2 6.6 fusion.19
  220.9 173.1 %all-gather.2 = f32[64,1,128]{2,1,0:T(1,128)S(1)} all-gather(f32[1,1,128]{2,1,0:T(1,128)S(1)} %bitcast.36), channel_id=1, replica_groups=mesh['shuf'=4,'key'=64] {'key'}, dimensions={0}, use_global_device_ids=true | all-gather | bytes 33280 | tf_op jit(solution)/shard_map/all_gather | solution.py:57
  394.0 176.6 %all-gather.1 = f32[64,1,128]{2,1,0:T(1,128)S(1)} all-gather(f32[1,1,128]{2,1,0:T(1,128)S(1)} %bitcast.35), channel_id=1, replica_groups=mesh['shuf'=4,'key'=64] {'key'}, dimensions={0}, use_global_device_ids=true | all-gather | bytes 33280 | tf_op jit(solution)/shard_map/all_gather | solution.py:56
  570.6 0.0 copy-done.3
  570.6 2.3 multiply_reduce_fusion
  572.9 1.5 convolution_convert_fusion
  574.4 0.0 all-reduce.2.cloned.1.call-update
  574.5 0.0 reduce-scatter.2.cloned.1.call-start
  574.5 39.0 %all-reduce.2.cloned.1.call-done = bf16[1024,512]{1,0:T(8,128)(2,1)} async-done(((bf16[1024,512]{1,0:T(8,128)(2,1)}), bf16[1024,512]{1,0:T(8,128)(2,1)}) %all-reduce.2.cloned.1.call-update) | async-done | bytes 1048592 | tf_op jit(solution)/shard_map/psum | solution.py:77
  613.5 2.9 convert_element_type.28
  616.4 0.0 reduce-scatter.2.cloned.1.call-update
  616.4 0.5 convolution_convert_fusion.1
  616.9 7.9 all_to_all.28
  624.8 1.8 scatter_custom_fusion
  626.6 356.3 %reduce-scatter.2.cloned.1.call-done = f32[16,512]{1,0:T(8,128)} async-done(((f32[1024,512]{1,0:T(8,128)}), f32[16,512]{1,0:T(8,128)}) %reduce-scatter.2.cloned.1.call-update) | async-done | bytes 32784 | tf_op jit(solution)/shard_map/reduce_scatter | solution.py:83
  982.8 1.4 broadcast_multiply_fusion
  (5 shorter events, 0.0 us)
Async XLA Ops:
  7.2 12.7 %copy-start = (bf16[1024,512]{1,0:T(8,128)(2,1)S(1)}, bf16[1024,512]{1,0:T(8,128)(2,1)}, u32[]{:S(2)}) copy-start(bf16[1024,512]{1,0:T(8,128)(2,1)} %param.7) | copy-start | bytes 3145732
  7.2 14.3 %copy-start.2 = (s32[1,128]{1,0:T(1,128)S(1)}, s32[1,128]{1,0:T(1,128)}, u32[]{:S(2)}) copy-start(s32[1,128]{1,0:T(1,128)} %param.6) | copy-start | bytes 1540
  7.2 15.0 %copy-start.1 = (s32[128]{0:T(128)S(1)}, s32[128]{0:T(128)}, u32[]{:S(2)}) copy-start(s32[128]{0:T(128)} %param.5) | copy-start | bytes 1540
  7.2 207.0 %all-gather.5.cloned.1.call-start = ((), (), s32[]{:S(2)}) async-start(), calls=%async_computation.4 | async-start | bytes 8519680 | tf_op jit(solution)/shard_map/all_gather | solution.py:46
  24.1 6.5 all-to-all-start
  28.9 584.6 %all-reduce.2.cloned.1.call-start = ((), (), s32[]{:S(2)}) async-start(), calls=%async_computation.5 | async-start | bytes 2097152 | tf_op jit(solution)/shard_map/psum | solution.py:77
  214.2 356.4 %copy-start.3 = (bf16[8192,512]{1,0:T(8,128)(2,1)S(1)}, bf16[8192,512]{1,0:T(8,128)(2,1)}, u32[]{:S(2)}) copy-start(bf16[8192,512]{1,0:T(8,128)(2,1)} %all-gather.5.cloned.1.call-done) | copy-start | bytes 25165828
  574.5 408.4 %reduce-scatter.2.cloned.1.call-start = ((), (), s32[]{:S(2)}) async-start(), calls=%async_computation.6 | async-start | bytes 2129920 | tf_op jit(solution)/shard_map/reduce_scatter | solution.py:83
Sparse Core Ops, SparseCore 0:
  21.1 148.5 all-gather.4
  574.6 38.8 all-reduce.1
  616.5 366.2 reduce-scatter.1
where the time goes:
time: 991 us
  blocking collectives  548 us (55%)
  waiting for transfers between devices  397 us (40%)
  between operations  13.8 us (1%)
  matrix products  11.3 us (1%)
    reduce_scatter x1, waiting for transfers between devices, body(): lax.psum_scatter(summed_all, 'key', scatter_dimension=0, tiled=True)  356 us
    all_gather x1, blocking collectives, body(): lax.all_gather(group_labels, 'key', axis=0, tiled=True)  181 us
    all_gather x1, blocking collectives, body(): lax.all_gather(soft_weight, 'key', axis=0, tiled=True)  177 us
    all_gather x1, blocking collectives, body(): lax.all_gather(pos_weight, 'key', axis=0, tiled=True)  173 us
    psum x1, waiting for transfers between devices, body(): lax.psum(lax.dot_general(group_rows, slopes, (((0,), (0,)), ((), ())), pr...  39 us
  transfers between devices with their start and end apart: 4, of which 3 were waited for; matrix products, arithmetic and copies ran while one was open for 1% of the time, Pallas kernels for 0%

commit v1 on v0

v1 whole, which is shorter than its diff:
```python
import jax
import jax.numpy as jnp
from jax import lax
from jax.sharding import Mesh, PartitionSpec as P

exponent_divisor = 0.1
loss_scale = 64.0
epsilon = 1e-06

AXES = ("yl", "c", "x", "zh", "zl", "yh")
KEY = ("x", "zh", "zl", "yh")
LABEL_ROWS = 16
f32 = jnp.float32
bf16 = jnp.bfloat16


def shift(value, axis, size, distance):
    distance %= size
    if distance == 0:
        return value
    return lax.ppermute(value, axis, [(i, (i + distance) % size) for i in range(size)])


def shift_y(value, distance):
    if distance % 4 == 0:
        return value
    seat = [(y % 2) * 2 + y // 2 for y in range(4)]
    return lax.ppermute(
        value, ("yl", "yh"), [(seat[y], seat[(y + distance) % 4]) for y in range(4)]
    )


def shift_yz(value, distance_y, distance_z):
    if distance_y == 0 and distance_z == 0:
        return value
    seat = lambda y, z: (y % 2) * 4 + z * 2 + y // 2
    pairs = [
        (seat(y, z), seat((y + distance_y) % 4, (z + distance_z) % 2))
        for y in range(4)
        for z in range(2)
    ]
    return lax.ppermute(value, ("yl", "zl", "yh"), pairs)


def unpack(stack, rows):
    normed = stack[:, :rows].reshape(-1, stack.shape[2])
    high = stack[:, rows, :rows].astype(jnp.int32)
    low = stack[:, rows, rows : 2 * rows].astype(jnp.int32)
    return normed, (high * 64 + low).reshape(-1)


def body(embeddings, labels, order, head_weight):
    rows, width = embeddings.shape
    proj = head_weight.shape[1]
    zh = lax.axis_index("zh")
    share = rows // 4
    doubled = jnp.concatenate([order[0], order[0]])
    routing = lax.dynamic_slice_in_dim(doubled, zh * share, rows)
    with jax.named_scope("route_out"):
        pick = (routing[:, None] == jnp.arange(rows, dtype=jnp.int32)[None, :]).astype(bf16)
        lane = jnp.arange(128, dtype=jnp.int32)[None, :]
        tag = jnp.where(
            lane == 0, (labels // 64)[:, None], jnp.where(lane == 1, (labels % 64)[:, None], 0)
        ).astype(bf16)
        tagged = jnp.concatenate([embeddings, tag], axis=1)
        sent = jnp.dot(pick, tagged, preferred_element_type=f32).astype(bf16)
        sent = sent.reshape(4, share, width + 128)
        got = jnp.concatenate([shift(sent[d], "zh", 4, d) for d in range(4)], axis=0)
    group_rows = got[:, :width]
    with jax.named_scope("project"):
        projected = jnp.dot(group_rows, head_weight, preferred_element_type=f32)
        row_norm = jnp.sqrt(jnp.sum(projected * projected, axis=1, keepdims=True) + epsilon)
        direction = projected / row_norm
        normed = direction.astype(bf16)
        label_line = jnp.concatenate(
            [got[:, width], got[:, width + 1], jnp.zeros((proj - 2 * rows,), bf16)]
        )
        label_block = jnp.broadcast_to(label_line[None, :], (LABEL_ROWS, proj))
        packet = jnp.concatenate([normed, label_block], axis=0)
    with jax.named_scope("gather_sets"):
        across_x = jnp.stack([shift(packet, "x", 4, d) for d in range(4)])
        set_b = jnp.stack([shift_yz(packet, dy, dz) for dy in range(4) for dz in range(2)])
        set_a = jnp.concatenate([across_x, shift(across_x, "c", 2, 1)], axis=0)
        normed_a, labels_a = unpack(set_a, rows)
        normed_b, labels_b = unpack(set_b, rows)
        chip_rows = lax.all_gather(group_rows, "c", axis=0, tiled=True)
    with jax.named_scope("scores"):
        total = normed_a.shape[0]
        scores = (
            lax.dot_general(
                normed_a, normed_b, (((1,), (1,)), ((), ())), preferred_element_type=f32
            )
            / exponent_divisor
        )
        row = jnp.arange(total, dtype=jnp.int32)
        itself = jnp.logical_and(row[:, None] == row[None, :], (row < rows)[:, None])
        exponent = jnp.where(itself, 0.0, jnp.exp(scores))
        positive = jnp.logical_and(
            labels_a[:, None] == labels_b[None, :], jnp.logical_not(itself)
        ).astype(f32)
        sums_a = jnp.stack([jnp.sum(exponent, axis=1), jnp.sum(positive, axis=1)])
        sums_b = jnp.stack([jnp.sum(exponent, axis=0), jnp.sum(positive, axis=0)])
    with jax.named_scope("totals"):
        sums_a = sums_a.reshape(2, 2, 4, rows)
        sums_a = sums_a + jnp.roll(shift(sums_a, "c", 2, 1), 1, axis=1)
        sums_a = sum([jnp.roll(shift(sums_a, "x", 4, d), d, axis=2) for d in range(4)])
        sums_b = sums_b.reshape(2, 4, 2, rows)
        sums_b = sums_b + jnp.roll(shift(sums_b, "zl", 2, 1), 1, axis=2)
        sums_b = sum([jnp.roll(shift_y(sums_b, d), d, axis=1) for d in range(4)])

        def weights(sums):
            totals, counts = sums.reshape(2, total)
            floor_count = jnp.maximum(counts, 1.0)
            return loss_scale * counts / (floor_count * totals), loss_scale / floor_count

        soft_a, pos_a = weights(sums_a)
        soft_b, pos_b = weights(sums_b)
    with jax.named_scope("pull"):
        coefficient = (
            (soft_a[:, None] + soft_b[None, :]) * exponent
            - (pos_a[:, None] + pos_b[None, :]) * positive
        ).astype(bf16)
        pull = jnp.dot(coefficient, normed_b, preferred_element_type=f32)
        pull = pull.reshape(2, 4, rows, proj)
        pull = pull[0] + shift(pull[1], "c", 2, 1)
        parts = [shift(pull[d].astype(bf16), "x", 4, -d).astype(f32) for d in range(1, 4)]
        pull_grad = (pull[0] + sum(parts)) / exponent_divisor
    with jax.named_scope("slopes"):
        along = jnp.sum(direction * pull_grad, axis=1, keepdims=True)
        slopes = ((pull_grad - direction * along) / row_norm).astype(bf16)
    with jax.named_scope("route_back"):
        blocks = slopes.reshape(4, share, proj)
        returned = jnp.concatenate([shift(blocks[d], "zh", 4, -d) for d in range(4)], axis=0)
        own = lax.dot_general(
            pick, returned, (((0,), (0,)), ((), ())), preferred_element_type=f32
        ).astype(bf16)
        grad_embeddings = lax.dot_general(
            own, head_weight, (((1,), (1,)), ((), ())), preferred_element_type=f32
        ).astype(bf16)
    with jax.named_scope("head"):
        chip_slopes = lax.all_gather(slopes, "c", axis=0, tiled=True)
        part = lax.dot_general(
            chip_rows, chip_slopes, (((0,), (0,)), ((), ())), preferred_element_type=f32
        ).astype(bf16)
        part = part.reshape(64, 2, width // 128, proj)
        part = lax.dynamic_index_in_dim(part, lax.axis_index("c"), axis=1, keepdims=False)
        part = part.reshape(128, width // 256, proj)
        spread = lax.all_to_all(part, KEY + ("yl",), split_axis=0, concat_axis=0, tiled=True)
        piece = jnp.sum(spread.astype(f32), axis=0)
        grad_head = lax.all_gather(piece, ("c", "yl"), axis=0, tiled=True)
    return (grad_embeddings, grad_head / loss_scale)


def solution(mesh):
    split = Mesh(mesh.devices.reshape(2, 2, 4, 4, 2, 2), AXES)
    return jax.shard_map(
        body,
        mesh=split,
        in_specs=(P(AXES, None), P(AXES), P(AXES, None), P()),
        out_specs=(P(AXES, None), P(KEY, None)),
        check_vma=False,
    )
```

time: 991 us -> 133 us (0.13)
  the two profiles are of different devices: /device:TPU:8 before, /device:TPU:1 now
where the time goes in v1:
time: 133 us; the launch traced here: 132 us
  starting transfers between devices  69.6 us (52%)
  waiting for transfers between devices  27.4 us (21%)
  blocking collectives  17.5 us (13%)
  matrix products  6.85 us (5%)
  other arithmetic  6.44 us (5%)
  local copies, waits for them, and re-layouts  3.36 us (3%)
    ppermute x19, starting transfers between devices, shift(): lax.ppermute(value, axis, [(i, (i + distance) % size) for i in range(size)])  44.4 us
    ppermute x19, waiting for transfers between devices, shift(): lax.ppermute(value, axis, [(i, (i + distance) % size) for i in range(size)])  24.5 us
    all_gather x1, blocking collectives, body(): grad_head = lax.all_gather(piece, ('c', 'yl'), axis=0, tiled=True)  12.4 us
    ppermute x7, starting transfers between devices, shift_yz(): return lax.ppermute(value, ('yl', 'zl', 'yh'), pairs)  11.4 us
    all_to_all x1, starting transfers between devices, body(): lax.all_to_all(part, KEY + ('yl',), split_axis=0, concat_axis=0, tiled=True)  9.14 us
    ppermute x3, starting transfers between devices, shift_y(): lax.ppermute(value, ('yl', 'yh'), [(seat[y], seat[(y + distance) % 4]) fo...  4.71 us
    all_gather x1, blocking collectives, body(): chip_rows = lax.all_gather(group_rows, 'c', axis=0, tiled=True)  2.73 us
  transfers between devices with their start and end apart: 30, of which 12 were waited for; matrix products, arithmetic and copies ran while one was open for 1% of the time, Pallas kernels for 0%

profile of v1, /device:TPU:1, one launch (start us, length us, event | category | flops | bytes accessed | tf_op | source)
XLA Modules:
  0.0 132.3 jit_solution(14755481514690741878)
XLA Ops:
  0.7 0.8 pad_add_fusion
  2.3 1.2 convolution_convert_fusion
  3.5 3.9 %collective-permute-start = (bf16[32,1152]{1,0:T(8,128)(2,1)S(1)}, bf16[32,1152]{1,0:T(8,128)(2,1)S(1)}, u32[]{:S(2)}, u32[]{:S(2)}) collective-permute-start(bf16[32,1152]{1,0:T(8,128)(2,1)S(1)} %get-tuple-element.18), channel_id=1, source_target_pairs={{0,4},{4,8},{8,12},{12,0},{1,5},{5,9},{9,13},{13,1},{2,6},{6,10},{... | collective-permute-start | bytes 221192 | tf_op jit(solution)/shard_map/route_out/ppermute | solution.py:21
  7.4 5.1 %collective-permute-start.1 = (bf16[32,1152]{1,0:T(8,128)(2,1)S(1)}, bf16[32,1152]{1,0:T(8,128)(2,1)S(1)}, u32[]{:S(2)}, u32[]{:S(2)}) collective-permute-start(bf16[32,1152]{1,0:T(8,128)(2,1)S(1)} %get-tuple-element.17), channel_id=1, source_target_pairs={{0,8},{4,12},{8,0},{12,4},{1,9},{5,13},{9,1},{13,5},{2,10},{6,14},... | collective-permute-start | bytes 221192 | tf_op jit(solution)/shard_map/route_out/ppermute | solution.py:21
  12.6 2.4 %collective-permute-start.2 = (bf16[32,1152]{1,0:T(8,128)(2,1)S(1)}, bf16[32,1152]{1,0:T(8,128)(2,1)S(1)}, u32[]{:S(2)}, u32[]{:S(2)}) collective-permute-start(bf16[32,1152]{1,0:T(8,128)(2,1)S(1)} %get-tuple-element.16), channel_id=1, source_target_pairs={{0,12},{4,0},{8,4},{12,8},{1,13},{5,1},{9,5},{13,9},{2,14},{6,2},{... | collective-permute-start | bytes 221192 | tf_op jit(solution)/shard_map/route_out/ppermute | solution.py:21
  14.9 2.0 %collective-permute-done.1 = bf16[32,1152]{1,0:T(8,128)(2,1)S(1)} collective-permute-done((bf16[32,1152]{1,0:T(8,128)(2,1)S(1)}, bf16[32,1152]{1,0:T(8,128)(2,1)S(1)}, u32[]{:S(2)}, u32[]{:S(2)}) %collective-permute-start.1) | collective-permute-done | bytes 73760 | tf_op jit(solution)/shard_map/route_out/ppermute | solution.py:21
  16.9 3.9 %collective-permute-done.2 = bf16[32,1152]{1,0:T(8,128)(2,1)S(1)} collective-permute-done((bf16[32,1152]{1,0:T(8,128)(2,1)S(1)}, bf16[32,1152]{1,0:T(8,128)(2,1)S(1)}, u32[]{:S(2)}, u32[]{:S(2)}) %collective-permute-start.2) | collective-permute-done | bytes 73760 | tf_op jit(solution)/shard_map/route_out/ppermute | solution.py:21
  21.8 1.3 collective-permute-start.3
  23.1 2.5 %collective-permute-start.4 = (bf16[144,512]{1,0:T(8,128)(2,1)S(1)}, bf16[144,512]{1,0:T(8,128)(2,1)S(1)}, u32[]{:S(2)}, u32[]{:S(2)}) collective-permute-start(bf16[144,512]{1,0:T(8,128)(2,1)S(1)} %get-tuple-element.20), channel_id=1, source_target_pairs={{0,32},{16,48},{32,0},{48,16},{1,33},{17,49},{33,1},{49,17},{2,34}... | collective-permute-start | bytes 442376 | tf_op jit(solution)/shard_map/gather_sets/ppermute | solution.py:21
  25.5 1.2 collective-permute-start.5
  26.7 1.3 collective-permute-start.8
  28.1 2.4 %collective-permute-start.9 = (bf16[144,512]{1,0:T(8,128)(2,1)S(1)}, bf16[144,512]{1,0:T(8,128)(2,1)S(1)}, u32[]{:S(2)}, u32[]{:S(2)}) collective-permute-start(bf16[144,512]{1,0:T(8,128)(2,1)S(1)} %get-tuple-element.20), channel_id=1, source_target_pairs={{0,130},{2,128},{128,3},{130,1},{1,131},{3,129},{129,2},{131,0},{4... | collective-permute-start | bytes 442376 | tf_op jit(solution)/shard_map/gather_sets/ppermute | solution.py:42
  30.5 1.7 %collective-permute-done.8 = bf16[144,512]{1,0:T(8,128)(2,1)S(1)} collective-permute-done((bf16[144,512]{1,0:T(8,128)(2,1)S(1)}, bf16[144,512]{1,0:T(8,128)(2,1)S(1)}, u32[]{:S(2)}, u32[]{:S(2)}) %collective-permute-start.8) | collective-permute-done | bytes 147488 | tf_op jit(solution)/shard_map/gather_sets/ppermute | solution.py:42
  32.2 1.6 %collective-permute-start.10 = (bf16[144,512]{1,0:T(8,128)(2,1)S(1)}, bf16[144,512]{1,0:T(8,128)(2,1)S(1)}, u32[]{:S(2)}, u32[]{:S(2)}) collective-permute-start(bf16[144,512]{1,0:T(8,128)(2,1)S(1)} %get-tuple-element.20), channel_id=1, source_target_pairs={{0,1},{2,3},{128,129},{130,131},{1,0},{3,2},{129,128},{131,130},{4... | collective-permute-start | bytes 442376 | tf_op jit(solution)/shard_map/gather_sets/ppermute | solution.py:42
  33.9 2.5 %collective-permute-start.11 = (bf16[144,512]{1,0:T(8,128)(2,1)S(1)}, bf16[144,512]{1,0:T(8,128)(2,1)S(1)}, u32[]{:S(2)}, u32[]{:S(2)}) collective-permute-start(bf16[144,512]{1,0:T(8,128)(2,1)S(1)} %get-tuple-element.20), channel_id=1, source_target_pairs={{0,3},{2,1},{128,131},{130,129},{1,2},{3,0},{129,130},{131,128},{4... | collective-permute-start | bytes 442376 | tf_op jit(solution)/shard_map/gather_sets/ppermute | solution.py:42
  36.4 3.4 %collective-permute-start.12 = (bf16[144,512]{1,0:T(8,128)(2,1)S(1)}, bf16[144,512]{1,0:T(8,128)(2,1)S(1)}, u32[]{:S(2)}, u32[]{:S(2)}) collective-permute-start(bf16[144,512]{1,0:T(8,128)(2,1)S(1)} %get-tuple-element.20), channel_id=1, source_target_pairs={{0,129},{2,131},{128,0},{130,2},{1,128},{3,130},{129,1},{131,3},{4... | collective-permute-start | bytes 442376 | tf_op jit(solution)/shard_map/gather_sets/ppermute | solution.py:42
  39.9 7.1 %collective-permute-start.6 = (bf16[4,144,512]{2,1,0:T(8,128)(2,1)S(1)}, bf16[4,144,512]{2,1,0:T(8,128)(2,1)S(1)}, u32[]{:S(2)}, u32[]{:S(2)}) collective-permute-start(bf16[4,144,512]{2,1,0:T(8,128)(2,1)S(1)} %pad_maximum_fusion), channel_id=1, source_target_pairs={{0,64},{64,0},{1,65},{65,1},{2,66},{66,2},{3,67},{67,3},{4,68},{68... | collective-permute-start | bytes 1769480 | tf_op jit(solution)/shard_map/gather_sets/ppermute | solution.py:21
  47.3 1.3 %collective-permute-done.6 = bf16[4,144,512]{2,1,0:T(8,128)(2,1)S(1)} collective-permute-done((bf16[4,144,512]{2,1,0:T(8,128)(2,1)S(1)}, bf16[4,144,512]{2,1,0:T(8,128)(2,1)S(1)}, u32[]{:S(2)}, u32[]{:S(2)}) %collective-permute-start.6) | collective-permute-done | bytes 589856 | tf_op jit(solution)/shard_map/gather_sets/ppermute | solution.py:21
  48.8 2.2 %convert_reduce_fusion.1 = (f32[1024]{0:T(1024)S(1)}, f32[1024]{0:T(1024)S(1)}) fusion(pred[1024]{0:T(1024)(128)(4,1)S(1)} %iota_compare_fusion.5, s32[1024]{0:T(1024)S(1)} %bitcast.89, s32[1024]{0:T(1024)S(1)} %bitcast.91), kind=kLoop, calls=%fused_computation.1 | loop fusion | flops 8386560 | bytes 17408 | tf_op jit(solution)/shard_map/scores/reduce_sum | solution.py:101
  51.0 1.6 %fusion.52 = (f32[1024]{0:T(1024)S(1)}, f32[1024]{0:T(1024)S(1)}, f32[1024,1024]{1,0:T(8,128)S(1)}) fusion(bf16[1024,512]{1,0:T(8,128)(2,1)S(1)} %bitcast.71, bf16[1024,512]{1,0:T(8,128)(2,1)S(1)} %bitcast.69, pred[1024]{0:T(1024)(128)(4,1)S(1)} %iota_compare_fusion.5), kind=kOutput, calls=%fused_computation.107 | convolution fusion | flops 1080031232 | bytes 6300672 | tf_op jit(solution)/shard_map/scores/dot_general | solution.py:90
  52.6 3.4 %collective-permute-start.14 = (f32[2,2,4,128]{3,2,1,0:T(4,128)S(1)}, f32[2,2,4,128]{3,2,1,0:T(4,128)S(1)}, u32[]{:S(2)}, u32[]{:S(2)}) collective-permute-start(f32[2,2,4,128]{3,2,1,0:T(4,128)S(1)} %pad_maximum_fusion.3), channel_id=1, source_target_pairs={{0,64},{64,0},{1,65},{65,1},{2,66},{66,2},{3,67},{67,3},{4,68},{68... | collective-permute-start | bytes 24584 | tf_op jit(solution)/shard_map/totals/ppermute | solution.py:21
  56.0 1.2 collective-permute-start.18
  57.2 1.3 collective-permute-start.16
  58.5 1.7 %collective-permute-start.17 = (f32[2,2,4,128]{3,2,1,0:T(4,128)S(1)}, f32[2,2,4,128]{3,2,1,0:T(4,128)S(1)}, u32[]{:S(2)}, u32[]{:S(2)}) collective-permute-start(f32[2,2,4,128]{3,2,1,0:T(4,128)S(1)} %maximum_add_fusion), channel_id=1, source_target_pairs={{0,48},{16,0},{32,16},{48,32},{1,49},{17,1},{33,17},{49,33},{2,50}... | collective-permute-start | bytes 24584 | tf_op jit(solution)/shard_map/totals/ppermute | solution.py:21
  60.2 2.0 %collective-permute-start.20 = (f32[2,4,2,128]{3,2,1,0:T(2,128)S(1)}, f32[2,4,2,128]{3,2,1,0:T(2,128)S(1)}, u32[]{:S(2)}, u32[]{:S(2)}) collective-permute-start(f32[2,4,2,128]{3,2,1,0:T(2,128)S(1)} %maximum_add_fusion.2), channel_id=1, source_target_pairs={{0,1},{128,129},{1,0},{129,128},{2,3},{130,131},{3,2},{131,130},{4... | collective-permute-start | bytes 24584 | tf_op jit(solution)/shard_map/totals/ppermute | solution.py:28
  62.3 1.6 %collective-permute-start.19 = (f32[2,4,2,128]{3,2,1,0:T(2,128)S(1)}, f32[2,4,2,128]{3,2,1,0:T(2,128)S(1)}, u32[]{:S(2)}, u32[]{:S(2)}) collective-permute-start(f32[2,4,2,128]{3,2,1,0:T(2,128)S(1)} %maximum_add_fusion.2), channel_id=1, source_target_pairs={{0,128},{128,1},{1,129},{129,0},{2,130},{130,3},{3,131},{131,2},{4... | collective-permute-start | bytes 24584 | tf_op jit(solution)/shard_map/totals/ppermute | solution.py:28
  63.8 1.1 collective-permute-start.21
  65.0 1.0 collective-permute-done.19
  66.4 1.8 %fusion.3 = f32[1024,512]{1,0:T(8,128)S(1)} fusion(bf16[1024,512]{1,0:T(8,128)(2,1)S(1)} %bitcast.70, f32[1024,1024]{1,0:T(8,128)S(1)} %get-tuple-element.41, f32[1024]{0:T(1024)S(1)} %bitcast.96, f32[1024]{0:T(1024)S(1)} %bitcast.94, f32[1024]{0:T(1024)S(1)} %bitcast.95, f32[1024]{0:T(1024)S(1)} %bitcast.93, s32[1024]{0:T(1024)S(1)} %bitcast.90, ...), kind=kOutput, calls=%fused_computation.9 | convolution fusion | flops 1085276160 | bytes 7365632 | tf_op jit(solution)/shard_map/pull/dot_general | solution.py:123
  68.2 1.2 fusion.54
  69.4 2.6 %collective-permute-start.22 = (f32[4,128,512]{2,1,0:T(8,128)}, f32[4,128,512]{2,1,0:T(8,128)}, u32[]{:S(2)}, u32[]{:S(2)}) collective-permute-start(f32[4,128,512]{2,1,0:T(8,128)} %bitcast.25), channel_id=1, source_target_pairs={{0,64},{64,0},{1,65},{65,1},{2,66},{66,2},{3,67},{67,3},{4,68},{68... | collective-permute-start | bytes 3145736 | tf_op jit(solution)/shard_map/pull/ppermute | solution.py:21
  72.0 2.6 %collective-permute-done.22 = f32[4,128,512]{2,1,0:T(8,128)} collective-permute-done((f32[4,128,512]{2,1,0:T(8,128)}, f32[4,128,512]{2,1,0:T(8,128)}, u32[]{:S(2)}, u32[]{:S(2)}) %collective-permute-start.22) | collective-permute-done | bytes 1048608 | tf_op jit(solution)/shard_map/pull/ppermute | solution.py:21
  74.6 1.5 %fusion.53 = (bf16[4,128,512]{2,1,0:T(8,128)(2,1)S(1)}, f32[4,128,512]{2,1,0:T(8,128)S(1)}) fusion(f32[4,128,512]{2,1,0:T(8,128)S(1)} %bitcast.67, f32[4,128,512]{2,1,0:T(8,128)} %collective-permute-done.22), kind=kLoop, calls=%fused_computation.108 | loop fusion | flops 524288 | bytes 3670016 | tf_op jit(solution)/shard_map/convert.2
  76.2 3.0 %collective-permute-start.23 = (bf16[128,512]{1,0:T(8,128)(2,1)S(1)}, bf16[128,512]{1,0:T(8,128)(2,1)S(1)}, u32[]{:S(2)}, u32[]{:S(2)}) collective-permute-start(bf16[128,512]{1,0:T(8,128)(2,1)S(1)} %get-tuple-element.12), channel_id=1, source_target_pairs={{0,48},{16,0},{32,16},{48,32},{1,49},{17,1},{33,17},{49,33},{2,50}... | collective-permute-start | bytes 393224 | tf_op jit(solution)/shard_map/pull/ppermute | solution.py:21
  79.2 0.9 collective-permute-start.25
  80.1 2.7 %all_gather.9 = bf16[256,1024]{1,0:T(8,128)(2,1)S(1)} all-gather(bf16[128,1024]{1,0:T(8,128)(2,1)S(1)} %slice-done), channel_id=1, replica_groups=mesh['yl'=2,'c'=2,'x'=4,'zh'=4,'zl'=2,'yh'=2] {'c'}, dimensions={0}, use_global_device_ids=true | all-gather | bytes 786432 | tf_op jit(solution)/shard_map/gather_sets/all_gather | solution.py:86
  82.8 1.6 %collective-permute-done.23 = bf16[128,512]{1,0:T(8,128)(2,1)S(1)} collective-permute-done((bf16[128,512]{1,0:T(8,128)(2,1)S(1)}, bf16[128,512]{1,0:T(8,128)(2,1)S(1)}, u32[]{:S(2)}, u32[]{:S(2)}) %collective-permute-start.23) | collective-permute-done | bytes 131104 | tf_op jit(solution)/shard_map/pull/ppermute | solution.py:21
  85.2 3.2 %collective-permute-done.25 = bf16[128,512]{1,0:T(8,128)(2,1)S(1)} collective-permute-done((bf16[128,512]{1,0:T(8,128)(2,1)S(1)}, bf16[128,512]{1,0:T(8,128)(2,1)S(1)}, u32[]{:S(2)}, u32[]{:S(2)}) %collective-permute-start.25) | collective-permute-done | bytes 131104 | tf_op jit(solution)/shard_map/pull/ppermute | solution.py:21
  88.7 2.4 %all_gather.10 = bf16[256,512]{1,0:T(8,128)(2,1)S(1)} all-gather(bf16[128,512]{1,0:T(8,128)(2,1)S(1)} %divide_convert_fusion), channel_id=1, replica_groups=mesh['yl'=2,'c'=2,'x'=4,'zh'=4,'zl'=2,'yh'=2] {'c'}, dimensions={0}, use_global_device_ids=true | all-gather | bytes 393216 | tf_op jit(solution)/shard_map/head/all_gather | solution.py:141
  91.6 0.9 reshape.181
  92.5 9.1 %all-to-all-start = ((bf16[128,4,512]{2,1,0:T(4,128)(2,1)}), bf16[128,4,512]{2,1,0:T(4,128)(2,1)S(1)}, u32[]{:S(2)}, u32[]{:S(2)}) async-start(bf16[128,4,512]{2,1,0:T(4,128)(2,1)} %reshape.181), calls=%async_computation | async-start | bytes 1048576 | tf_op jit(solution)/shard_map/head/all_to_all | solution.py:148
  101.7 2.8 %collective-permute-start.26 = (bf16[32,512]{1,0:T(8,128)(2,1)S(1)}, bf16[32,512]{1,0:T(8,128)(2,1)S(1)}, u32[]{:S(2)}, u32[]{:S(2)}) collective-permute-start(bf16[32,512]{1,0:T(8,128)(2,1)S(1)} %get-tuple-element.24), channel_id=1, source_target_pairs={{0,12},{4,0},{8,4},{12,8},{1,13},{5,1},{9,5},{13,9},{2,14},{6,2},{... | collective-permute-start | bytes 98312 | tf_op jit(solution)/shard_map/route_back/ppermute | solution.py:21
  104.5 2.0 %collective-permute-start.27 = (bf16[32,512]{1,0:T(8,128)(2,1)S(1)}, bf16[32,512]{1,0:T(8,128)(2,1)S(1)}, u32[]{:S(2)}, u32[]{:S(2)}) collective-permute-start(bf16[32,512]{1,0:T(8,128)(2,1)S(1)} %get-tuple-element.23), channel_id=1, source_target_pairs={{0,8},{4,12},{8,0},{12,4},{1,9},{5,13},{9,1},{13,5},{2,10},{6,14},... | collective-permute-start | bytes 98312 | tf_op jit(solution)/shard_map/route_back/ppermute | solution.py:21
  106.6 2.1 %collective-permute-start.28 = (bf16[32,512]{1,0:T(8,128)(2,1)S(1)}, bf16[32,512]{1,0:T(8,128)(2,1)S(1)}, u32[]{:S(2)}, u32[]{:S(2)}) collective-permute-start(bf16[32,512]{1,0:T(8,128)(2,1)S(1)} %get-tuple-element.22), channel_id=1, source_target_pairs={{0,4},{4,8},{8,12},{12,0},{1,5},{5,9},{9,13},{13,1},{2,6},{6,10},{... | collective-permute-start | bytes 98312 | tf_op jit(solution)/shard_map/route_back/ppermute | solution.py:21
  108.6 4.7 %collective-permute-done.26 = bf16[32,512]{1,0:T(8,128)(2,1)S(1)} collective-permute-done((bf16[32,512]{1,0:T(8,128)(2,1)S(1)}, bf16[32,512]{1,0:T(8,128)(2,1)S(1)}, u32[]{:S(2)}, u32[]{:S(2)}) %collective-permute-start.26) | collective-permute-done | bytes 32800 | tf_op jit(solution)/shard_map/route_back/ppermute | solution.py:21
  113.3 4.4 %collective-permute-done.27 = bf16[32,512]{1,0:T(8,128)(2,1)S(1)} collective-permute-done((bf16[32,512]{1,0:T(8,128)(2,1)S(1)}, bf16[32,512]{1,0:T(8,128)(2,1)S(1)}, u32[]{:S(2)}, u32[]{:S(2)}) %collective-permute-start.27) | collective-permute-done | bytes 32800 | tf_op jit(solution)/shard_map/route_back/ppermute | solution.py:21
  117.7 1.4 %convolution_convert_fusion.2 = bf16[128,1024]{1,0:T(8,128)(2,1)} fusion(bf16[1024,512]{1,0:T(8,128)(2,1)S(1)} %copy-done, bf16[32,512]{1,0:T(8,128)(2,1)S(1)} %collective-permute-done.28, bf16[32,512]{1,0:T(8,128)(2,1)S(1)} %collective-permute-done.27, bf16[32,512]{1,0:T(8,128)(2,1)S(1)} %collective-permute-done.26, ...), kind=kOutput, calls=%fused_computation.16 | convolution fusion | flops 151732224 | bytes 1442304 | tf_op jit(solution)/shard_map/route_back/dot_general | solution.py:137
  119.4 12.4 %all-gather = f32[4,4,512]{2,1,0:T(4,128)S(1)} all-gather(f32[1,4,512]{2,1,0:T(4,128)S(1)} %bitcast.87), channel_id=1, replica_groups=mesh['yl'=2,'c'=2,'x'=4,'zh'=4,'zl'=2,'yh'=2] {'c','yl'}, dimensions={0}, use_global_device_ids=true | all-gather | bytes 40960 | tf_op jit(solution)/shard_map/head/all_gather | solution.py:150
  (91 shorter events, 5.2 us)
Async XLA Ops:
  0.6 20.2 %copy-start = (bf16[1024,512]{1,0:T(8,128)(2,1)S(1)}, bf16[1024,512]{1,0:T(8,128)(2,1)}, u32[]{:S(2)}) copy-start(bf16[1024,512]{1,0:T(8,128)(2,1)} %param.7) | copy-start | bytes 3145732
  3.5 11.4 %collective-permute-start = (bf16[32,1152]{1,0:T(8,128)(2,1)S(1)}, bf16[32,1152]{1,0:T(8,128)(2,1)S(1)}, u32[]{:S(2)}, u32[]{:S(2)}) collective-permute-start(bf16[32,1152]{1,0:T(8,128)(2,1)S(1)} %get-tuple-element.18), channel_id=1, source_target_pairs={{0,4},{4,8},{8,12},{12,0},{1,5},{5,9},{9,13},{13,1},{2,6},{6,10},{... | collective-permute-start | bytes 221192 | tf_op jit(solution)/shard_map/route_out/ppermute | solution.py:21
  7.4 9.5 %collective-permute-start.1 = (bf16[32,1152]{1,0:T(8,128)(2,1)S(1)}, bf16[32,1152]{1,0:T(8,128)(2,1)S(1)}, u32[]{:S(2)}, u32[]{:S(2)}) collective-permute-start(bf16[32,1152]{1,0:T(8,128)(2,1)S(1)} %get-tuple-element.17), channel_id=1, source_target_pairs={{0,8},{4,12},{8,0},{12,4},{1,9},{5,13},{9,1},{13,5},{2,10},{6,14},... | collective-permute-start | bytes 221192 | tf_op jit(solution)/shard_map/route_out/ppermute | solution.py:21
  12.6 8.3 %collective-permute-start.2 = (bf16[32,1152]{1,0:T(8,128)(2,1)S(1)}, bf16[32,1152]{1,0:T(8,128)(2,1)S(1)}, u32[]{:S(2)}, u32[]{:S(2)}) collective-permute-start(bf16[32,1152]{1,0:T(8,128)(2,1)S(1)} %get-tuple-element.16), channel_id=1, source_target_pairs={{0,12},{4,0},{8,4},{12,8},{1,13},{5,1},{9,5},{13,9},{2,14},{6,2},{... | collective-permute-start | bytes 221192 | tf_op jit(solution)/shard_map/route_out/ppermute | solution.py:21
  20.9 51.1 %copy-start.1 = (bf16[128,1152]{1,0:T(8,128)(2,1)}, bf16[128,1152]{1,0:T(8,128)(2,1)S(1)}, u32[]{:S(2)}) copy-start(bf16[128,1152]{1,0:T(8,128)(2,1)S(1)} %pad_maximum_fusion.1) | copy-start | bytes 884740
  21.7 6.4 %collective-permute-start.7 = (bf16[144,512]{1,0:T(8,128)(2,1)S(1)}, bf16[144,512]{1,0:T(8,128)(2,1)S(1)}, u32[]{:S(2)}, u32[]{:S(2)}) collective-permute-start(bf16[144,512]{1,0:T(8,128)(2,1)S(1)} %get-tuple-element.20), channel_id=1, source_target_pairs={{0,2},{2,0},{128,130},{130,128},{1,3},{3,1},{129,131},{131,129},{4... | collective-permute-start | bytes 442376 | tf_op jit(solution)/shard_map/gather_sets/ppermute | solution.py:42
  21.8 12.1 %collective-permute-start.3 = (bf16[144,512]{1,0:T(8,128)(2,1)S(1)}, bf16[144,512]{1,0:T(8,128)(2,1)S(1)}, u32[]{:S(2)}, u32[]{:S(2)}) collective-permute-start(bf16[144,512]{1,0:T(8,128)(2,1)S(1)} %get-tuple-element.20), channel_id=1, source_target_pairs={{0,16},{16,32},{32,48},{48,0},{1,17},{17,33},{33,49},{49,1},{2,18}... | collective-permute-start | bytes 442376 | tf_op jit(solution)/shard_map/gather_sets/ppermute | solution.py:21
  23.1 13.3 %collective-permute-start.4 = (bf16[144,512]{1,0:T(8,128)(2,1)S(1)}, bf16[144,512]{1,0:T(8,128)(2,1)S(1)}, u32[]{:S(2)}, u32[]{:S(2)}) collective-permute-start(bf16[144,512]{1,0:T(8,128)(2,1)S(1)} %get-tuple-element.20), channel_id=1, source_target_pairs={{0,32},{16,48},{32,0},{48,16},{1,33},{17,49},{33,1},{49,17},{2,34}... | collective-permute-start | bytes 442376 | tf_op jit(solution)/shard_map/gather_sets/ppermute | solution.py:21
  25.5 14.3 %collective-permute-start.5 = (bf16[144,512]{1,0:T(8,128)(2,1)S(1)}, bf16[144,512]{1,0:T(8,128)(2,1)S(1)}, u32[]{:S(2)}, u32[]{:S(2)}) collective-permute-start(bf16[144,512]{1,0:T(8,128)(2,1)S(1)} %get-tuple-element.20), channel_id=1, source_target_pairs={{0,48},{16,0},{32,16},{48,32},{1,49},{17,1},{33,17},{49,33},{2,50}... | collective-permute-start | bytes 442376 | tf_op jit(solution)/shard_map/gather_sets/ppermute | solution.py:21
  26.7 5.6 %collective-permute-start.8 = (bf16[144,512]{1,0:T(8,128)(2,1)S(1)}, bf16[144,512]{1,0:T(8,128)(2,1)S(1)}, u32[]{:S(2)}, u32[]{:S(2)}) collective-permute-start(bf16[144,512]{1,0:T(8,128)(2,1)S(1)} %get-tuple-element.20), channel_id=1, source_target_pairs={{0,128},{2,130},{128,1},{130,3},{1,129},{3,131},{129,0},{131,2},{4... | collective-permute-start | bytes 442376 | tf_op jit(solution)/shard_map/gather_sets/ppermute | solution.py:42
  28.1 11.8 %collective-permute-start.9 = (bf16[144,512]{1,0:T(8,128)(2,1)S(1)}, bf16[144,512]{1,0:T(8,128)(2,1)S(1)}, u32[]{:S(2)}, u32[]{:S(2)}) collective-permute-start(bf16[144,512]{1,0:T(8,128)(2,1)S(1)} %get-tuple-element.20), channel_id=1, source_target_pairs={{0,130},{2,128},{128,3},{130,1},{1,131},{3,129},{129,2},{131,0},{4... | collective-permute-start | bytes 442376 | tf_op jit(solution)/shard_map/gather_sets/ppermute | solution.py:42
  32.2 14.8 %collective-permute-start.10 = (bf16[144,512]{1,0:T(8,128)(2,1)S(1)}, bf16[144,512]{1,0:T(8,128)(2,1)S(1)}, u32[]{:S(2)}, u32[]{:S(2)}) collective-permute-start(bf16[144,512]{1,0:T(8,128)(2,1)S(1)} %get-tuple-element.20), channel_id=1, source_target_pairs={{0,1},{2,3},{128,129},{130,131},{1,0},{3,2},{129,128},{131,130},{4... | collective-permute-start | bytes 442376 | tf_op jit(solution)/shard_map/gather_sets/ppermute | solution.py:42
  33.9 13.2 %collective-permute-start.11 = (bf16[144,512]{1,0:T(8,128)(2,1)S(1)}, bf16[144,512]{1,0:T(8,128)(2,1)S(1)}, u32[]{:S(2)}, u32[]{:S(2)}) collective-permute-start(bf16[144,512]{1,0:T(8,128)(2,1)S(1)} %get-tuple-element.20), channel_id=1, source_target_pairs={{0,3},{2,1},{128,131},{130,129},{1,2},{3,0},{129,130},{131,128},{4... | collective-permute-start | bytes 442376 | tf_op jit(solution)/shard_map/gather_sets/ppermute | solution.py:42
  36.4 10.7 %collective-permute-start.12 = (bf16[144,512]{1,0:T(8,128)(2,1)S(1)}, bf16[144,512]{1,0:T(8,128)(2,1)S(1)}, u32[]{:S(2)}, u32[]{:S(2)}) collective-permute-start(bf16[144,512]{1,0:T(8,128)(2,1)S(1)} %get-tuple-element.20), channel_id=1, source_target_pairs={{0,129},{2,131},{128,0},{130,2},{1,128},{3,130},{129,1},{131,3},{4... | collective-permute-start | bytes 442376 | tf_op jit(solution)/shard_map/gather_sets/ppermute | solution.py:42
  39.8 7.3 %collective-permute-start.13 = (bf16[144,512]{1,0:T(8,128)(2,1)S(1)}, bf16[144,512]{1,0:T(8,128)(2,1)S(1)}, u32[]{:S(2)}, u32[]{:S(2)}) collective-permute-start(bf16[144,512]{1,0:T(8,128)(2,1)S(1)} %get-tuple-element.20), channel_id=1, source_target_pairs={{0,131},{2,129},{128,2},{130,0},{1,130},{3,128},{129,3},{131,1},{4... | collective-permute-start | bytes 442376 | tf_op jit(solution)/shard_map/gather_sets/ppermute | solution.py:42
  39.9 8.8 %collective-permute-start.6 = (bf16[4,144,512]{2,1,0:T(8,128)(2,1)S(1)}, bf16[4,144,512]{2,1,0:T(8,128)(2,1)S(1)}, u32[]{:S(2)}, u32[]{:S(2)}) collective-permute-start(bf16[4,144,512]{2,1,0:T(8,128)(2,1)S(1)} %pad_maximum_fusion), channel_id=1, source_target_pairs={{0,64},{64,0},{1,65},{65,1},{2,66},{66,2},{3,67},{67,3},{4,68},{68... | collective-permute-start | bytes 1769480 | tf_op jit(solution)/shard_map/gather_sets/ppermute | solution.py:21
  52.6 4.6 %collective-permute-start.14 = (f32[2,2,4,128]{3,2,1,0:T(4,128)S(1)}, f32[2,2,4,128]{3,2,1,0:T(4,128)S(1)}, u32[]{:S(2)}, u32[]{:S(2)}) collective-permute-start(f32[2,2,4,128]{3,2,1,0:T(4,128)S(1)} %pad_maximum_fusion.3), channel_id=1, source_target_pairs={{0,64},{64,0},{1,65},{65,1},{2,66},{66,2},{3,67},{67,3},{4,68},{68... | collective-permute-start | bytes 24584 | tf_op jit(solution)/shard_map/totals/ppermute | solution.py:21
  56.0 4.2 %collective-permute-start.18 = (f32[2,4,2,128]{3,2,1,0:T(2,128)S(1)}, f32[2,4,2,128]{3,2,1,0:T(2,128)S(1)}, u32[]{:S(2)}, u32[]{:S(2)}) collective-permute-start(f32[2,4,2,128]{3,2,1,0:T(2,128)S(1)} %pad_maximum_fusion.4), channel_id=1, source_target_pairs={{0,2},{2,0},{1,3},{3,1},{4,6},{6,4},{5,7},{7,5},{8,10},{10,8},{9,1... | collective-permute-start | bytes 24584 | tf_op jit(solution)/shard_map/totals/ppermute | solution.py:21
  57.2 6.6 %collective-permute-start.16 = (f32[2,2,4,128]{3,2,1,0:T(4,128)S(1)}, f32[2,2,4,128]{3,2,1,0:T(4,128)S(1)}, u32[]{:S(2)}, u32[]{:S(2)}) collective-permute-start(f32[2,2,4,128]{3,2,1,0:T(4,128)S(1)} %maximum_add_fusion), channel_id=1, source_target_pairs={{0,32},{16,48},{32,0},{48,16},{1,33},{17,49},{33,1},{49,17},{2,34}... | collective-permute-start | bytes 24584 | tf_op jit(solution)/shard_map/totals/ppermute | solution.py:21
  58.5 6.4 %collective-permute-start.17 = (f32[2,2,4,128]{3,2,1,0:T(4,128)S(1)}, f32[2,2,4,128]{3,2,1,0:T(4,128)S(1)}, u32[]{:S(2)}, u32[]{:S(2)}) collective-permute-start(f32[2,2,4,128]{3,2,1,0:T(4,128)S(1)} %maximum_add_fusion), channel_id=1, source_target_pairs={{0,48},{16,0},{32,16},{48,32},{1,49},{17,1},{33,17},{49,33},{2,50}... | collective-permute-start | bytes 24584 | tf_op jit(solution)/shard_map/totals/ppermute | solution.py:21
  60.2 4.8 %collective-permute-start.15 = (f32[2,2,4,128]{3,2,1,0:T(4,128)S(1)}, f32[2,2,4,128]{3,2,1,0:T(4,128)S(1)}, u32[]{:S(2)}, u32[]{:S(2)}) collective-permute-start(f32[2,2,4,128]{3,2,1,0:T(4,128)S(1)} %maximum_add_fusion), channel_id=1, source_target_pairs={{0,16},{16,32},{32,48},{48,0},{1,17},{17,33},{33,49},{49,1},{2,18}... | collective-permute-start | bytes 24584 | tf_op jit(solution)/shard_map/totals/ppermute | solution.py:21
  60.2 6.1 %collective-permute-start.20 = (f32[2,4,2,128]{3,2,1,0:T(2,128)S(1)}, f32[2,4,2,128]{3,2,1,0:T(2,128)S(1)}, u32[]{:S(2)}, u32[]{:S(2)}) collective-permute-start(f32[2,4,2,128]{3,2,1,0:T(2,128)S(1)} %maximum_add_fusion.2), channel_id=1, source_target_pairs={{0,1},{128,129},{1,0},{129,128},{2,3},{130,131},{3,2},{131,130},{4... | collective-permute-start | bytes 24584 | tf_op jit(solution)/shard_map/totals/ppermute | solution.py:28
  62.3 3.8 %collective-permute-start.19 = (f32[2,4,2,128]{3,2,1,0:T(2,128)S(1)}, f32[2,4,2,128]{3,2,1,0:T(2,128)S(1)}, u32[]{:S(2)}, u32[]{:S(2)}) collective-permute-start(f32[2,4,2,128]{3,2,1,0:T(2,128)S(1)} %maximum_add_fusion.2), channel_id=1, source_target_pairs={{0,128},{128,1},{1,129},{129,0},{2,130},{130,3},{3,131},{131,2},{4... | collective-permute-start | bytes 24584 | tf_op jit(solution)/shard_map/totals/ppermute | solution.py:28
  63.8 2.5 %collective-permute-start.21 = (f32[2,4,2,128]{3,2,1,0:T(2,128)S(1)}, f32[2,4,2,128]{3,2,1,0:T(2,128)S(1)}, u32[]{:S(2)}, u32[]{:S(2)}) collective-permute-start(f32[2,4,2,128]{3,2,1,0:T(2,128)S(1)} %maximum_add_fusion.2), channel_id=1, source_target_pairs={{0,129},{128,0},{1,128},{129,1},{2,131},{130,2},{3,130},{131,3},{4... | collective-permute-start | bytes 24584 | tf_op jit(solution)/shard_map/totals/ppermute | solution.py:28
  69.4 5.2 %collective-permute-start.22 = (f32[4,128,512]{2,1,0:T(8,128)}, f32[4,128,512]{2,1,0:T(8,128)}, u32[]{:S(2)}, u32[]{:S(2)}) collective-permute-start(f32[4,128,512]{2,1,0:T(8,128)} %bitcast.25), channel_id=1, source_target_pairs={{0,64},{64,0},{1,65},{65,1},{2,66},{66,2},{3,67},{67,3},{4,68},{68... | collective-permute-start | bytes 3145736 | tf_op jit(solution)/shard_map/pull/ppermute | solution.py:21
  74.6 5.5 %slice-start = ((bf16[128,1152]{1,0:T(8,128)(2,1)}), bf16[128,1024]{1,0:T(8,128)(2,1)S(1)}, s32[]{:S(2)}) async-start(bf16[128,1152]{1,0:T(8,128)(2,1)} %copy-done.1), calls=%async_computation.1 | async-start | bytes 524288 | tf_op jit(solution)/shard_map/slice | solution.py:69
  76.2 8.3 %collective-permute-start.23 = (bf16[128,512]{1,0:T(8,128)(2,1)S(1)}, bf16[128,512]{1,0:T(8,128)(2,1)S(1)}, u32[]{:S(2)}, u32[]{:S(2)}) collective-permute-start(bf16[128,512]{1,0:T(8,128)(2,1)S(1)} %get-tuple-element.12), channel_id=1, source_target_pairs={{0,48},{16,0},{32,16},{48,32},{1,49},{17,1},{33,17},{49,33},{2,50}... | collective-permute-start | bytes 393224 | tf_op jit(solution)/shard_map/pull/ppermute | solution.py:21
  79.2 6.0 %collective-permute-start.24 = (bf16[128,512]{1,0:T(8,128)(2,1)S(1)}, bf16[128,512]{1,0:T(8,128)(2,1)S(1)}, u32[]{:S(2)}, u32[]{:S(2)}) collective-permute-start(bf16[128,512]{1,0:T(8,128)(2,1)S(1)} %get-tuple-element.14), channel_id=1, source_target_pairs={{0,32},{16,48},{32,0},{48,16},{1,33},{17,49},{33,1},{49,17},{2,34}... | collective-permute-start | bytes 393224 | tf_op jit(solution)/shard_map/pull/ppermute | solution.py:21
  79.2 9.1 %collective-permute-start.25 = (bf16[128,512]{1,0:T(8,128)(2,1)S(1)}, bf16[128,512]{1,0:T(8,128)(2,1)S(1)}, u32[]{:S(2)}, u32[]{:S(2)}) collective-permute-start(bf16[128,512]{1,0:T(8,128)(2,1)S(1)} %get-tuple-element.13), channel_id=1, source_target_pairs={{0,16},{16,32},{32,48},{48,0},{1,17},{17,33},{33,49},{49,1},{2,18}... | collective-permute-start | bytes 393224 | tf_op jit(solution)/shard_map/pull/ppermute | solution.py:21
  92.5 26.5 %all-to-all-start = ((bf16[128,4,512]{2,1,0:T(4,128)(2,1)}), bf16[128,4,512]{2,1,0:T(4,128)(2,1)S(1)}, u32[]{:S(2)}, u32[]{:S(2)}) async-start(bf16[128,4,512]{2,1,0:T(4,128)(2,1)} %reshape.181), calls=%async_computation | async-start | bytes 1048576 | tf_op jit(solution)/shard_map/head/all_to_all | solution.py:148
  101.7 11.6 %collective-permute-start.26 = (bf16[32,512]{1,0:T(8,128)(2,1)S(1)}, bf16[32,512]{1,0:T(8,128)(2,1)S(1)}, u32[]{:S(2)}, u32[]{:S(2)}) collective-permute-start(bf16[32,512]{1,0:T(8,128)(2,1)S(1)} %get-tuple-element.24), channel_id=1, source_target_pairs={{0,12},{4,0},{8,4},{12,8},{1,13},{5,1},{9,5},{13,9},{2,14},{6,2},{... | collective-permute-start | bytes 98312 | tf_op jit(solution)/shard_map/route_back/ppermute | solution.py:21
  104.5 13.2 %collective-permute-start.27 = (bf16[32,512]{1,0:T(8,128)(2,1)S(1)}, bf16[32,512]{1,0:T(8,128)(2,1)S(1)}, u32[]{:S(2)}, u32[]{:S(2)}) collective-permute-start(bf16[32,512]{1,0:T(8,128)(2,1)S(1)} %get-tuple-element.23), channel_id=1, source_target_pairs={{0,8},{4,12},{8,0},{12,4},{1,9},{5,13},{9,1},{13,5},{2,10},{6,14},... | collective-permute-start | bytes 98312 | tf_op jit(solution)/shard_map/route_back/ppermute | solution.py:21
  106.6 11.1 %collective-permute-start.28 = (bf16[32,512]{1,0:T(8,128)(2,1)S(1)}, bf16[32,512]{1,0:T(8,128)(2,1)S(1)}, u32[]{:S(2)}, u32[]{:S(2)}) collective-permute-start(bf16[32,512]{1,0:T(8,128)(2,1)S(1)} %get-tuple-element.22), channel_id=1, source_target_pairs={{0,4},{4,8},{8,12},{12,0},{1,5},{5,9},{9,13},{13,1},{2,6},{6,10},{... | collective-permute-start | bytes 98312 | tf_op jit(solution)/shard_map/route_back/ppermute | solution.py:21

commit v2 on v1

--- a/solution.py
+++ b/solution.py
@@ -128,16 +128,9 @@
     with jax.named_scope("slopes"):
         along = jnp.sum(direction * pull_grad, axis=1, keepdims=True)
         slopes = ((pull_grad - direction * along) / row_norm).astype(bf16)
-    with jax.named_scope("route_back"):
+    with jax.named_scope("head_part"):
         blocks = slopes.reshape(4, share, proj)
-        returned = jnp.concatenate([shift(blocks[d], "zh", 4, -d) for d in range(4)], axis=0)
-        own = lax.dot_general(
-            pick, returned, (((0,), (0,)), ((), ())), preferred_element_type=f32
-        ).astype(bf16)
-        grad_embeddings = lax.dot_general(
-            own, head_weight, (((1,), (1,)), ((), ())), preferred_element_type=f32
-        ).astype(bf16)
-    with jax.named_scope("head"):
+        returned = [shift(blocks[d], "zh", 4, -d) for d in range(4)]
         chip_slopes = lax.all_gather(slopes, "c", axis=0, tiled=True)
         part = lax.dot_general(
             chip_rows, chip_slopes, (((0,), (0,)), ((), ())), preferred_element_type=f32
@@ -145,9 +138,24 @@
         part = part.reshape(64, 2, width // 128, proj)
         part = lax.dynamic_index_in_dim(part, lax.axis_index("c"), axis=1, keepdims=False)
         part = part.reshape(128, width // 256, proj)
+        part, *returned = lax.optimization_barrier((part, *returned))
+    with jax.named_scope("head"):
         spread = lax.all_to_all(part, KEY + ("yl",), split_axis=0, concat_axis=0, tiled=True)
         piece = jnp.sum(spread.astype(f32), axis=0)
-        grad_head = lax.all_gather(piece, ("c", "yl"), axis=0, tiled=True)
+        other = shift(piece, "yl", 2, 1)
+        first = lax.axis_index("yl") == 0
+        pair = jnp.concatenate([jnp.where(first, piece, other), jnp.where(first, other, piece)])
+        grad_head = lax.all_gather(pair, "c", axis=0, tiled=True)
+    with jax.named_scope("route_back"):
+        own = lax.dot_general(
+            pick,
+            jnp.concatenate(returned, axis=0),
+            (((0,), (0,)), ((), ())),
+            preferred_element_type=f32,
+        ).astype(bf16)
+        grad_embeddings = lax.dot_general(
+            own, head_weight, (((1,), (1,)), ((), ())), preferred_element_type=f32
+        ).astype(bf16)
     return (grad_embeddings, grad_head / loss_scale)
 
 

time: 133 us -> 137 us (1.030)
  waiting for transfers between devices: 27.4 us -> 37.8 us
  blocking collectives: 17.5 us -> 12.5 us
    all_to_all x1, waiting for transfers between devices: 0.01 us -> 15.3 us  [body(): lax.all_to_all(part, KEY + ('yl',), split_axis=0, concat_axis=0, tiled=True)]
    ppermute x19 -> x20, waiting for transfers between devices: 24.5 us -> 19.4 us  [shift(): lax.ppermute(value, axis, [(i, (i + distance) % size) for i in range(size)])]
    all_gather x1, blocking collectives: 12.4 us -> 7.36 us  [body(): grad_head = lax.all_gather(pair, 'c', axis=0, tiled=True)]
    ppermute x19 -> x20, starting transfers between devices: 44.4 us -> 43.6 us  [shift(): lax.ppermute(value, axis, [(i, (i + distance) % size) for i in range(size)])]
  transfers between devices with their start and end apart: 30 -> 31, of which waited for: 12 -> 13; matrix products, arithmetic and copies ran while one was open for 1% -> 2% of each run, Pallas kernels for 0% -> 0%
where the time goes in v2:
time: 137 us
  starting transfers between devices  69 us (50%)
  waiting for transfers between devices  37.8 us (28%)
  blocking collectives  12.5 us (9%)
  other arithmetic  7.07 us (5%)
  matrix products  6.84 us (5%)
  local copies, waits for them, and re-layouts  2.74 us (2%)
    ppermute x20, starting transfers between devices, shift(): lax.ppermute(value, axis, [(i, (i + distance) % size) for i in range(size)])  43.6 us
    ppermute x20, waiting for transfers between devices, shift(): lax.ppermute(value, axis, [(i, (i + distance) % size) for i in range(size)])  19.4 us
    all_to_all x1, waiting for transfers between devices, body(): lax.all_to_all(part, KEY + ('yl',), split_axis=0, concat_axis=0, tiled=True)  15.3 us
    ppermute x7, starting transfers between devices, shift_yz(): return lax.ppermute(value, ('yl', 'zl', 'yh'), pairs)  11.4 us
    all_to_all x1, starting transfers between devices, body(): lax.all_to_all(part, KEY + ('yl',), split_axis=0, concat_axis=0, tiled=True)  9.33 us
    all_gather x1, blocking collectives, body(): grad_head = lax.all_gather(pair, 'c', axis=0, tiled=True)  7.36 us
    ppermute x3, starting transfers between devices, shift_y(): lax.ppermute(value, ('yl', 'yh'), [(seat[y], seat[(y + distance) % 4]) fo...  4.71 us
  transfers between devices with their start and end apart: 31, of which 13 were waited for; matrix products, arithmetic and copies ran while one was open for 2% of the time, Pallas kernels for 0%

profile of v2, /device:TPU:1, one launch (start us, length us, event | category | flops | bytes accessed | tf_op | source)
XLA Modules:
  0.0 137.1 jit_solution(2901276366963597830)
XLA Ops:
  0.7 0.8 pad_add_fusion
  2.3 1.2 convolution_convert_fusion
  3.5 3.9 %collective-permute-start = (bf16[32,1152]{1,0:T(8,128)(2,1)S(1)}, bf16[32,1152]{1,0:T(8,128)(2,1)S(1)}, u32[]{:S(2)}, u32[]{:S(2)}) collective-permute-start(bf16[32,1152]{1,0:T(8,128)(2,1)S(1)} %get-tuple-element.28), channel_id=1, source_target_pairs={{0,4},{4,8},{8,12},{12,0},{1,5},{5,9},{9,13},{13,1},{2,6},{6,10},{... | collective-permute-start | bytes 221192 | tf_op jit(solution)/shard_map/route_out/ppermute | solution.py:21
  7.4 5.1 %collective-permute-start.1 = (bf16[32,1152]{1,0:T(8,128)(2,1)S(1)}, bf16[32,1152]{1,0:T(8,128)(2,1)S(1)}, u32[]{:S(2)}, u32[]{:S(2)}) collective-permute-start(bf16[32,1152]{1,0:T(8,128)(2,1)S(1)} %get-tuple-element.27), channel_id=1, source_target_pairs={{0,8},{4,12},{8,0},{12,4},{1,9},{5,13},{9,1},{13,5},{2,10},{6,14},... | collective-permute-start | bytes 221192 | tf_op jit(solution)/shard_map/route_out/ppermute | solution.py:21
  12.6 2.4 %collective-permute-start.2 = (bf16[32,1152]{1,0:T(8,128)(2,1)S(1)}, bf16[32,1152]{1,0:T(8,128)(2,1)S(1)}, u32[]{:S(2)}, u32[]{:S(2)}) collective-permute-start(bf16[32,1152]{1,0:T(8,128)(2,1)S(1)} %get-tuple-element.26), channel_id=1, source_target_pairs={{0,12},{4,0},{8,4},{12,8},{1,13},{5,1},{9,5},{13,9},{2,14},{6,2},{... | collective-permute-start | bytes 221192 | tf_op jit(solution)/shard_map/route_out/ppermute | solution.py:21
  14.9 2.0 %collective-permute-done.1 = bf16[32,1152]{1,0:T(8,128)(2,1)S(1)} collective-permute-done((bf16[32,1152]{1,0:T(8,128)(2,1)S(1)}, bf16[32,1152]{1,0:T(8,128)(2,1)S(1)}, u32[]{:S(2)}, u32[]{:S(2)}) %collective-permute-start.1) | collective-permute-done | bytes 73760 | tf_op jit(solution)/shard_map/route_out/ppermute | solution.py:21
  16.9 3.9 %collective-permute-done.2 = bf16[32,1152]{1,0:T(8,128)(2,1)S(1)} collective-permute-done((bf16[32,1152]{1,0:T(8,128)(2,1)S(1)}, bf16[32,1152]{1,0:T(8,128)(2,1)S(1)}, u32[]{:S(2)}, u32[]{:S(2)}) %collective-permute-start.2) | collective-permute-done | bytes 73760 | tf_op jit(solution)/shard_map/route_out/ppermute | solution.py:21
  21.8 1.3 collective-permute-start.3
  23.1 2.5 %collective-permute-start.4 = (bf16[144,512]{1,0:T(8,128)(2,1)S(1)}, bf16[144,512]{1,0:T(8,128)(2,1)S(1)}, u32[]{:S(2)}, u32[]{:S(2)}) collective-permute-start(bf16[144,512]{1,0:T(8,128)(2,1)S(1)} %get-tuple-element.30), channel_id=1, source_target_pairs={{0,32},{16,48},{32,0},{48,16},{1,33},{17,49},{33,1},{49,17},{2,34}... | collective-permute-start | bytes 442376 | tf_op jit(solution)/shard_map/gather_sets/ppermute | solution.py:21
  25.5 1.2 collective-permute-start.5
  26.7 1.3 collective-permute-start.8
  28.1 2.4 %collective-permute-start.9 = (bf16[144,512]{1,0:T(8,128)(2,1)S(1)}, bf16[144,512]{1,0:T(8,128)(2,1)S(1)}, u32[]{:S(2)}, u32[]{:S(2)}) collective-permute-start(bf16[144,512]{1,0:T(8,128)(2,1)S(1)} %get-tuple-element.30), channel_id=1, source_target_pairs={{0,130},{2,128},{128,3},{130,1},{1,131},{3,129},{129,2},{131,0},{4... | collective-permute-start | bytes 442376 | tf_op jit(solution)/shard_map/gather_sets/ppermute | solution.py:42
  30.5 1.7 %collective-permute-done.8 = bf16[144,512]{1,0:T(8,128)(2,1)S(1)} collective-permute-done((bf16[144,512]{1,0:T(8,128)(2,1)S(1)}, bf16[144,512]{1,0:T(8,128)(2,1)S(1)}, u32[]{:S(2)}, u32[]{:S(2)}) %collective-permute-start.8) | collective-permute-done | bytes 147488 | tf_op jit(solution)/shard_map/gather_sets/ppermute | solution.py:42
  32.2 1.6 %collective-permute-start.10 = (bf16[144,512]{1,0:T(8,128)(2,1)S(1)}, bf16[144,512]{1,0:T(8,128)(2,1)S(1)}, u32[]{:S(2)}, u32[]{:S(2)}) collective-permute-start(bf16[144,512]{1,0:T(8,128)(2,1)S(1)} %get-tuple-element.30), channel_id=1, source_target_pairs={{0,1},{2,3},{128,129},{130,131},{1,0},{3,2},{129,128},{131,130},{4... | collective-permute-start | bytes 442376 | tf_op jit(solution)/shard_map/gather_sets/ppermute | solution.py:42
  33.9 2.5 %collective-permute-start.11 = (bf16[144,512]{1,0:T(8,128)(2,1)S(1)}, bf16[144,512]{1,0:T(8,128)(2,1)S(1)}, u32[]{:S(2)}, u32[]{:S(2)}) collective-permute-start(bf16[144,512]{1,0:T(8,128)(2,1)S(1)} %get-tuple-element.30), channel_id=1, source_target_pairs={{0,3},{2,1},{128,131},{130,129},{1,2},{3,0},{129,130},{131,128},{4... | collective-permute-start | bytes 442376 | tf_op jit(solution)/shard_map/gather_sets/ppermute | solution.py:42
  36.4 3.4 %collective-permute-start.12 = (bf16[144,512]{1,0:T(8,128)(2,1)S(1)}, bf16[144,512]{1,0:T(8,128)(2,1)S(1)}, u32[]{:S(2)}, u32[]{:S(2)}) collective-permute-start(bf16[144,512]{1,0:T(8,128)(2,1)S(1)} %get-tuple-element.30), channel_id=1, source_target_pairs={{0,129},{2,131},{128,0},{130,2},{1,128},{3,130},{129,1},{131,3},{4... | collective-permute-start | bytes 442376 | tf_op jit(solution)/shard_map/gather_sets/ppermute | solution.py:42
  39.9 7.1 %collective-permute-start.6 = (bf16[4,144,512]{2,1,0:T(8,128)(2,1)S(1)}, bf16[4,144,512]{2,1,0:T(8,128)(2,1)S(1)}, u32[]{:S(2)}, u32[]{:S(2)}) collective-permute-start(bf16[4,144,512]{2,1,0:T(8,128)(2,1)S(1)} %pad_maximum_fusion), channel_id=1, source_target_pairs={{0,64},{64,0},{1,65},{65,1},{2,66},{66,2},{3,67},{67,3},{4,68},{68... | collective-permute-start | bytes 1769480 | tf_op jit(solution)/shard_map/gather_sets/ppermute | solution.py:21
  47.3 1.3 collective-permute-done.6
  48.8 2.2 %convert_reduce_fusion.1 = (f32[1024]{0:T(1024)S(1)}, f32[1024]{0:T(1024)S(1)}) fusion(pred[1024]{0:T(1024)(128)(4,1)S(1)} %iota_compare_fusion.5, s32[1024]{0:T(1024)S(1)} %bitcast.87, s32[1024]{0:T(1024)S(1)} %bitcast.89), kind=kLoop, calls=%fused_computation.1 | loop fusion | flops 8386560 | bytes 17408 | tf_op jit(solution)/shard_map/scores/reduce_sum | solution.py:101
  51.0 1.6 %fusion.52 = (f32[1024]{0:T(1024)S(1)}, f32[1024]{0:T(1024)S(1)}, f32[1024,1024]{1,0:T(8,128)S(1)}) fusion(bf16[1024,512]{1,0:T(8,128)(2,1)S(1)} %bitcast.70, bf16[1024,512]{1,0:T(8,128)(2,1)S(1)} %bitcast.68, pred[1024]{0:T(1024)(128)(4,1)S(1)} %iota_compare_fusion.5), kind=kOutput, calls=%fused_computation.110 | convolution fusion | flops 1080031232 | bytes 6300672 | tf_op jit(solution)/shard_map/scores/dot_general | solution.py:90
  52.6 3.4 %collective-permute-start.14 = (f32[2,2,4,128]{3,2,1,0:T(4,128)S(1)}, f32[2,2,4,128]{3,2,1,0:T(4,128)S(1)}, u32[]{:S(2)}, u32[]{:S(2)}) collective-permute-start(f32[2,2,4,128]{3,2,1,0:T(4,128)S(1)} %pad_maximum_fusion.4), channel_id=1, source_target_pairs={{0,64},{64,0},{1,65},{65,1},{2,66},{66,2},{3,67},{67,3},{4,68},{68... | collective-permute-start | bytes 24584 | tf_op jit(solution)/shard_map/totals/ppermute | solution.py:21
  56.0 1.2 collective-permute-start.18
  57.2 1.3 collective-permute-start.16
  58.5 1.7 %collective-permute-start.17 = (f32[2,2,4,128]{3,2,1,0:T(4,128)S(1)}, f32[2,2,4,128]{3,2,1,0:T(4,128)S(1)}, u32[]{:S(2)}, u32[]{:S(2)}) collective-permute-start(f32[2,2,4,128]{3,2,1,0:T(4,128)S(1)} %maximum_add_fusion), channel_id=1, source_target_pairs={{0,48},{16,0},{32,16},{48,32},{1,49},{17,1},{33,17},{49,33},{2,50}... | collective-permute-start | bytes 24584 | tf_op jit(solution)/shard_map/totals/ppermute | solution.py:21
  60.2 2.0 %collective-permute-start.20 = (f32[2,4,2,128]{3,2,1,0:T(2,128)S(1)}, f32[2,4,2,128]{3,2,1,0:T(2,128)S(1)}, u32[]{:S(2)}, u32[]{:S(2)}) collective-permute-start(f32[2,4,2,128]{3,2,1,0:T(2,128)S(1)} %maximum_add_fusion.2), channel_id=1, source_target_pairs={{0,1},{128,129},{1,0},{129,128},{2,3},{130,131},{3,2},{131,130},{4... | collective-permute-start | bytes 24584 | tf_op jit(solution)/shard_map/totals/ppermute | solution.py:28
  62.3 1.6 %collective-permute-start.19 = (f32[2,4,2,128]{3,2,1,0:T(2,128)S(1)}, f32[2,4,2,128]{3,2,1,0:T(2,128)S(1)}, u32[]{:S(2)}, u32[]{:S(2)}) collective-permute-start(f32[2,4,2,128]{3,2,1,0:T(2,128)S(1)} %maximum_add_fusion.2), channel_id=1, source_target_pairs={{0,128},{128,1},{1,129},{129,0},{2,130},{130,3},{3,131},{131,2},{4... | collective-permute-start | bytes 24584 | tf_op jit(solution)/shard_map/totals/ppermute | solution.py:28
  63.8 1.1 collective-permute-start.21
  65.0 1.0 collective-permute-done.19
  66.4 1.8 %fusion.3 = f32[1024,512]{1,0:T(8,128)S(1)} fusion(bf16[1024,512]{1,0:T(8,128)(2,1)S(1)} %bitcast.69, f32[1024,1024]{1,0:T(8,128)S(1)} %get-tuple-element.53, f32[1024]{0:T(1024)S(1)} %bitcast.94, f32[1024]{0:T(1024)S(1)} %bitcast.92, f32[1024]{0:T(1024)S(1)} %bitcast.93, f32[1024]{0:T(1024)S(1)} %bitcast.91, s32[1024]{0:T(1024)S(1)} %bitcast.88, ...), kind=kOutput, calls=%fused_computation.9 | convolution fusion | flops 1085276160 | bytes 7365632 | tf_op jit(solution)/shard_map/pull/dot_general | solution.py:123
  68.2 1.2 fusion.54
  69.4 2.6 %collective-permute-start.22 = (f32[4,128,512]{2,1,0:T(8,128)}, f32[4,128,512]{2,1,0:T(8,128)}, u32[]{:S(2)}, u32[]{:S(2)}) collective-permute-start(f32[4,128,512]{2,1,0:T(8,128)} %bitcast.25), channel_id=1, source_target_pairs={{0,64},{64,0},{1,65},{65,1},{2,66},{66,2},{3,67},{67,3},{4,68},{68... | collective-permute-start | bytes 3145736 | tf_op jit(solution)/shard_map/pull/ppermute | solution.py:21
  72.0 2.6 %collective-permute-done.22 = f32[4,128,512]{2,1,0:T(8,128)} collective-permute-done((f32[4,128,512]{2,1,0:T(8,128)}, f32[4,128,512]{2,1,0:T(8,128)}, u32[]{:S(2)}, u32[]{:S(2)}) %collective-permute-start.22) | collective-permute-done | bytes 1048608 | tf_op jit(solution)/shard_map/pull/ppermute | solution.py:21
  74.6 1.5 %fusion.53 = (bf16[4,128,512]{2,1,0:T(8,128)(2,1)S(1)}, f32[4,128,512]{2,1,0:T(8,128)S(1)}) fusion(f32[4,128,512]{2,1,0:T(8,128)S(1)} %bitcast.66, f32[4,128,512]{2,1,0:T(8,128)} %collective-permute-done.22), kind=kLoop, calls=%fused_computation.111 | loop fusion | flops 524288 | bytes 3670016 | tf_op jit(solution)/shard_map/convert.2
  76.2 3.0 %collective-permute-start.23 = (bf16[128,512]{1,0:T(8,128)(2,1)S(1)}, bf16[128,512]{1,0:T(8,128)(2,1)S(1)}, u32[]{:S(2)}, u32[]{:S(2)}) collective-permute-start(bf16[128,512]{1,0:T(8,128)(2,1)S(1)} %get-tuple-element.22), channel_id=1, source_target_pairs={{0,48},{16,0},{32,16},{48,32},{1,49},{17,1},{33,17},{49,33},{2,50}... | collective-permute-start | bytes 393224 | tf_op jit(solution)/shard_map/pull/ppermute | solution.py:21
  79.2 0.9 collective-permute-start.25
  80.1 2.7 %all_gather.9 = bf16[256,1024]{1,0:T(8,128)(2,1)S(1)} all-gather(bf16[128,1024]{1,0:T(8,128)(2,1)S(1)} %slice-done), channel_id=1, replica_groups=mesh['yl'=2,'c'=2,'x'=4,'zh'=4,'zl'=2,'yh'=2] {'c'}, dimensions={0}, use_global_device_ids=true | all-gather | bytes 786432 | tf_op jit(solution)/shard_map/gather_sets/all_gather | solution.py:86
  82.8 1.6 %collective-permute-done.23 = bf16[128,512]{1,0:T(8,128)(2,1)S(1)} collective-permute-done((bf16[128,512]{1,0:T(8,128)(2,1)S(1)}, bf16[128,512]{1,0:T(8,128)(2,1)S(1)}, u32[]{:S(2)}, u32[]{:S(2)}) %collective-permute-start.23) | collective-permute-done | bytes 131104 | tf_op jit(solution)/shard_map/pull/ppermute | solution.py:21
  85.2 3.2 %collective-permute-done.25 = bf16[128,512]{1,0:T(8,128)(2,1)S(1)} collective-permute-done((bf16[128,512]{1,0:T(8,128)(2,1)S(1)}, bf16[128,512]{1,0:T(8,128)(2,1)S(1)}, u32[]{:S(2)}, u32[]{:S(2)}) %collective-permute-start.25) | collective-permute-done | bytes 131104 | tf_op jit(solution)/shard_map/pull/ppermute | solution.py:21
  88.7 2.4 %all_gather.10 = bf16[256,512]{1,0:T(8,128)(2,1)S(1)} all-gather(bf16[128,512]{1,0:T(8,128)(2,1)S(1)} %divide_convert_fusion), channel_id=1, replica_groups=mesh['yl'=2,'c'=2,'x'=4,'zh'=4,'zl'=2,'yh'=2] {'c'}, dimensions={0}, use_global_device_ids=true | all-gather | bytes 393216 | tf_op jit(solution)/shard_map/head_part/all_gather | solution.py:134
  91.1 3.1 %collective-permute-start.26 = (bf16[32,512]{1,0:T(8,128)(2,1)S(1)}, bf16[32,512]{1,0:T(8,128)(2,1)S(1)}, u32[]{:S(2)}, u32[]{:S(2)}) collective-permute-start(bf16[32,512]{1,0:T(8,128)(2,1)S(1)} %get-tuple-element.33), channel_id=1, source_target_pairs={{0,12},{4,0},{8,4},{12,8},{1,13},{5,1},{9,5},{13,9},{2,14},{6,2},{... | collective-permute-start | bytes 98312 | tf_op jit(solution)/shard_map/head_part/ppermute | solution.py:21
  94.2 2.2 %collective-permute-start.28 = (bf16[32,512]{1,0:T(8,128)(2,1)S(1)}, bf16[32,512]{1,0:T(8,128)(2,1)S(1)}, u32[]{:S(2)}, u32[]{:S(2)}) collective-permute-start(bf16[32,512]{1,0:T(8,128)(2,1)S(1)} %get-tuple-element.31), channel_id=1, source_target_pairs={{0,4},{4,8},{8,12},{12,0},{1,5},{5,9},{9,13},{13,1},{2,6},{6,10},{... | collective-permute-start | bytes 98312 | tf_op jit(solution)/shard_map/head_part/ppermute | solution.py:21
  96.9 0.9 reshape.181
  97.9 3.4 %collective-permute-done.27 = bf16[32,512]{1,0:T(8,128)(2,1)S(1)} collective-permute-done((bf16[32,512]{1,0:T(8,128)(2,1)S(1)}, bf16[32,512]{1,0:T(8,128)(2,1)S(1)}, u32[]{:S(2)}, u32[]{:S(2)}) %collective-permute-start.27) | collective-permute-done | bytes 32800 | tf_op jit(solution)/shard_map/head_part/ppermute | solution.py:21
  101.2 9.3 %all-to-all-start = ((bf16[128,4,512]{2,1,0:T(4,128)(2,1)}), bf16[128,4,512]{2,1,0:T(4,128)(2,1)S(1)}, u32[]{:S(2)}, u32[]{:S(2)}) async-start(bf16[128,4,512]{2,1,0:T(4,128)(2,1)} %reshape.181), calls=%async_computation | async-start | bytes 1048576 | tf_op jit(solution)/shard_map/head/all_to_all | solution.py:143
  110.6 15.3 %all-to-all-done = bf16[128,4,512]{2,1,0:T(4,128)(2,1)S(1)} async-done(((bf16[128,4,512]{2,1,0:T(4,128)(2,1)}), bf16[128,4,512]{2,1,0:T(4,128)(2,1)S(1)}, u32[]{:S(2)}, u32[]{:S(2)}) %all-to-all-start) | async-done | bytes 524320 | tf_op jit(solution)/shard_map/head/all_to_all | solution.py:143
  126.2 0.8 collective-permute-start.29
  127.0 1.4 convolution_convert_fusion.2
  129.1 7.4 %all_gather.11 = f32[16,512]{1,0:T(8,128)S(1)} all-gather(f32[8,512]{1,0:T(8,128)S(1)} %pad_maximum_fusion.3), channel_id=1, replica_groups=mesh['yl'=2,'c'=2,'x'=4,'zh'=4,'zl'=2,'yh'=2] {'c'}, dimensions={0}, use_global_device_ids=true | all-gather | bytes 49152 | tf_op jit(solution)/shard_map/head/all_gather | solution.py:148
  (94 shorter events, 5.9 us)
Async XLA Ops:
  0.6 20.2 %copy-start = (bf16[1024,512]{1,0:T(8,128)(2,1)S(1)}, bf16[1024,512]{1,0:T(8,128)(2,1)}, u32[]{:S(2)}) copy-start(bf16[1024,512]{1,0:T(8,128)(2,1)} %param.7) | copy-start | bytes 3145732
  3.5 11.4 %collective-permute-start = (bf16[32,1152]{1,0:T(8,128)(2,1)S(1)}, bf16[32,1152]{1,0:T(8,128)(2,1)S(1)}, u32[]{:S(2)}, u32[]{:S(2)}) collective-permute-start(bf16[32,1152]{1,0:T(8,128)(2,1)S(1)} %get-tuple-element.28), channel_id=1, source_target_pairs={{0,4},{4,8},{8,12},{12,0},{1,5},{5,9},{9,13},{13,1},{2,6},{6,10},{... | collective-permute-start | bytes 221192 | tf_op jit(solution)/shard_map/route_out/ppermute | solution.py:21
  7.4 9.5 %collective-permute-start.1 = (bf16[32,1152]{1,0:T(8,128)(2,1)S(1)}, bf16[32,1152]{1,0:T(8,128)(2,1)S(1)}, u32[]{:S(2)}, u32[]{:S(2)}) collective-permute-start(bf16[32,1152]{1,0:T(8,128)(2,1)S(1)} %get-tuple-element.27), channel_id=1, source_target_pairs={{0,8},{4,12},{8,0},{12,4},{1,9},{5,13},{9,1},{13,5},{2,10},{6,14},... | collective-permute-start | bytes 221192 | tf_op jit(solution)/shard_map/route_out/ppermute | solution.py:21
  12.6 8.3 %collective-permute-start.2 = (bf16[32,1152]{1,0:T(8,128)(2,1)S(1)}, bf16[32,1152]{1,0:T(8,128)(2,1)S(1)}, u32[]{:S(2)}, u32[]{:S(2)}) collective-permute-start(bf16[32,1152]{1,0:T(8,128)(2,1)S(1)} %get-tuple-element.26), channel_id=1, source_target_pairs={{0,12},{4,0},{8,4},{12,8},{1,13},{5,1},{9,5},{13,9},{2,14},{6,2},{... | collective-permute-start | bytes 221192 | tf_op jit(solution)/shard_map/route_out/ppermute | solution.py:21
  20.9 51.1 %copy-start.1 = (bf16[128,1152]{1,0:T(8,128)(2,1)}, bf16[128,1152]{1,0:T(8,128)(2,1)S(1)}, u32[]{:S(2)}) copy-start(bf16[128,1152]{1,0:T(8,128)(2,1)S(1)} %pad_maximum_fusion.1) | copy-start | bytes 884740
  21.7 6.4 %collective-permute-start.7 = (bf16[144,512]{1,0:T(8,128)(2,1)S(1)}, bf16[144,512]{1,0:T(8,128)(2,1)S(1)}, u32[]{:S(2)}, u32[]{:S(2)}) collective-permute-start(bf16[144,512]{1,0:T(8,128)(2,1)S(1)} %get-tuple-element.30), channel_id=1, source_target_pairs={{0,2},{2,0},{128,130},{130,128},{1,3},{3,1},{129,131},{131,129},{4... | collective-permute-start | bytes 442376 | tf_op jit(solution)/shard_map/gather_sets/ppermute | solution.py:42
  21.8 12.1 %collective-permute-start.3 = (bf16[144,512]{1,0:T(8,128)(2,1)S(1)}, bf16[144,512]{1,0:T(8,128)(2,1)S(1)}, u32[]{:S(2)}, u32[]{:S(2)}) collective-permute-start(bf16[144,512]{1,0:T(8,128)(2,1)S(1)} %get-tuple-element.30), channel_id=1, source_target_pairs={{0,16},{16,32},{32,48},{48,0},{1,17},{17,33},{33,49},{49,1},{2,18}... | collective-permute-start | bytes 442376 | tf_op jit(solution)/shard_map/gather_sets/ppermute | solution.py:21
  23.1 13.3 %collective-permute-start.4 = (bf16[144,512]{1,0:T(8,128)(2,1)S(1)}, bf16[144,512]{1,0:T(8,128)(2,1)S(1)}, u32[]{:S(2)}, u32[]{:S(2)}) collective-permute-start(bf16[144,512]{1,0:T(8,128)(2,1)S(1)} %get-tuple-element.30), channel_id=1, source_target_pairs={{0,32},{16,48},{32,0},{48,16},{1,33},{17,49},{33,1},{49,17},{2,34}... | collective-permute-start | bytes 442376 | tf_op jit(solution)/shard_map/gather_sets/ppermute | solution.py:21
  25.5 14.3 %collective-permute-start.5 = (bf16[144,512]{1,0:T(8,128)(2,1)S(1)}, bf16[144,512]{1,0:T(8,128)(2,1)S(1)}, u32[]{:S(2)}, u32[]{:S(2)}) collective-permute-start(bf16[144,512]{1,0:T(8,128)(2,1)S(1)} %get-tuple-element.30), channel_id=1, source_target_pairs={{0,48},{16,0},{32,16},{48,32},{1,49},{17,1},{33,17},{49,33},{2,50}... | collective-permute-start | bytes 442376 | tf_op jit(solution)/shard_map/gather_sets/ppermute | solution.py:21
  26.7 5.6 %collective-permute-start.8 = (bf16[144,512]{1,0:T(8,128)(2,1)S(1)}, bf16[144,512]{1,0:T(8,128)(2,1)S(1)}, u32[]{:S(2)}, u32[]{:S(2)}) collective-permute-start(bf16[144,512]{1,0:T(8,128)(2,1)S(1)} %get-tuple-element.30), channel_id=1, source_target_pairs={{0,128},{2,130},{128,1},{130,3},{1,129},{3,131},{129,0},{131,2},{4... | collective-permute-start | bytes 442376 | tf_op jit(solution)/shard_map/gather_sets/ppermute | solution.py:42
  28.1 11.8 %collective-permute-start.9 = (bf16[144,512]{1,0:T(8,128)(2,1)S(1)}, bf16[144,512]{1,0:T(8,128)(2,1)S(1)}, u32[]{:S(2)}, u32[]{:S(2)}) collective-permute-start(bf16[144,512]{1,0:T(8,128)(2,1)S(1)} %get-tuple-element.30), channel_id=1, source_target_pairs={{0,130},{2,128},{128,3},{130,1},{1,131},{3,129},{129,2},{131,0},{4... | collective-permute-start | bytes 442376 | tf_op jit(solution)/shard_map/gather_sets/ppermute | solution.py:42
  32.2 14.8 %collective-permute-start.10 = (bf16[144,512]{1,0:T(8,128)(2,1)S(1)}, bf16[144,512]{1,0:T(8,128)(2,1)S(1)}, u32[]{:S(2)}, u32[]{:S(2)}) collective-permute-start(bf16[144,512]{1,0:T(8,128)(2,1)S(1)} %get-tuple-element.30), channel_id=1, source_target_pairs={{0,1},{2,3},{128,129},{130,131},{1,0},{3,2},{129,128},{131,130},{4... | collective-permute-start | bytes 442376 | tf_op jit(solution)/shard_map/gather_sets/ppermute | solution.py:42
  33.9 13.2 %collective-permute-start.11 = (bf16[144,512]{1,0:T(8,128)(2,1)S(1)}, bf16[144,512]{1,0:T(8,128)(2,1)S(1)}, u32[]{:S(2)}, u32[]{:S(2)}) collective-permute-start(bf16[144,512]{1,0:T(8,128)(2,1)S(1)} %get-tuple-element.30), channel_id=1, source_target_pairs={{0,3},{2,1},{128,131},{130,129},{1,2},{3,0},{129,130},{131,128},{4... | collective-permute-start | bytes 442376 | tf_op jit(solution)/shard_map/gather_sets/ppermute | solution.py:42
  36.4 10.7 %collective-permute-start.12 = (bf16[144,512]{1,0:T(8,128)(2,1)S(1)}, bf16[144,512]{1,0:T(8,128)(2,1)S(1)}, u32[]{:S(2)}, u32[]{:S(2)}) collective-permute-start(bf16[144,512]{1,0:T(8,128)(2,1)S(1)} %get-tuple-element.30), channel_id=1, source_target_pairs={{0,129},{2,131},{128,0},{130,2},{1,128},{3,130},{129,1},{131,3},{4... | collective-permute-start | bytes 442376 | tf_op jit(solution)/shard_map/gather_sets/ppermute | solution.py:42
  39.8 7.3 %collective-permute-start.13 = (bf16[144,512]{1,0:T(8,128)(2,1)S(1)}, bf16[144,512]{1,0:T(8,128)(2,1)S(1)}, u32[]{:S(2)}, u32[]{:S(2)}) collective-permute-start(bf16[144,512]{1,0:T(8,128)(2,1)S(1)} %get-tuple-element.30), channel_id=1, source_target_pairs={{0,131},{2,129},{128,2},{130,0},{1,130},{3,128},{129,3},{131,1},{4... | collective-permute-start | bytes 442376 | tf_op jit(solution)/shard_map/gather_sets/ppermute | solution.py:42
  39.9 8.8 %collective-permute-start.6 = (bf16[4,144,512]{2,1,0:T(8,128)(2,1)S(1)}, bf16[4,144,512]{2,1,0:T(8,128)(2,1)S(1)}, u32[]{:S(2)}, u32[]{:S(2)}) collective-permute-start(bf16[4,144,512]{2,1,0:T(8,128)(2,1)S(1)} %pad_maximum_fusion), channel_id=1, source_target_pairs={{0,64},{64,0},{1,65},{65,1},{2,66},{66,2},{3,67},{67,3},{4,68},{68... | collective-permute-start | bytes 1769480 | tf_op jit(solution)/shard_map/gather_sets/ppermute | solution.py:21
  52.6 4.6 %collective-permute-start.14 = (f32[2,2,4,128]{3,2,1,0:T(4,128)S(1)}, f32[2,2,4,128]{3,2,1,0:T(4,128)S(1)}, u32[]{:S(2)}, u32[]{:S(2)}) collective-permute-start(f32[2,2,4,128]{3,2,1,0:T(4,128)S(1)} %pad_maximum_fusion.4), channel_id=1, source_target_pairs={{0,64},{64,0},{1,65},{65,1},{2,66},{66,2},{3,67},{67,3},{4,68},{68... | collective-permute-start | bytes 24584 | tf_op jit(solution)/shard_map/totals/ppermute | solution.py:21
  56.0 4.2 %collective-permute-start.18 = (f32[2,4,2,128]{3,2,1,0:T(2,128)S(1)}, f32[2,4,2,128]{3,2,1,0:T(2,128)S(1)}, u32[]{:S(2)}, u32[]{:S(2)}) collective-permute-start(f32[2,4,2,128]{3,2,1,0:T(2,128)S(1)} %pad_maximum_fusion.5), channel_id=1, source_target_pairs={{0,2},{2,0},{1,3},{3,1},{4,6},{6,4},{5,7},{7,5},{8,10},{10,8},{9,1... | collective-permute-start | bytes 24584 | tf_op jit(solution)/shard_map/totals/ppermute | solution.py:21
  57.2 6.6 %collective-permute-start.16 = (f32[2,2,4,128]{3,2,1,0:T(4,128)S(1)}, f32[2,2,4,128]{3,2,1,0:T(4,128)S(1)}, u32[]{:S(2)}, u32[]{:S(2)}) collective-permute-start(f32[2,2,4,128]{3,2,1,0:T(4,128)S(1)} %maximum_add_fusion), channel_id=1, source_target_pairs={{0,32},{16,48},{32,0},{48,16},{1,33},{17,49},{33,1},{49,17},{2,34}... | collective-permute-start | bytes 24584 | tf_op jit(solution)/shard_map/totals/ppermute | solution.py:21
  58.5 6.4 %collective-permute-start.17 = (f32[2,2,4,128]{3,2,1,0:T(4,128)S(1)}, f32[2,2,4,128]{3,2,1,0:T(4,128)S(1)}, u32[]{:S(2)}, u32[]{:S(2)}) collective-permute-start(f32[2,2,4,128]{3,2,1,0:T(4,128)S(1)} %maximum_add_fusion), channel_id=1, source_target_pairs={{0,48},{16,0},{32,16},{48,32},{1,49},{17,1},{33,17},{49,33},{2,50}... | collective-permute-start | bytes 24584 | tf_op jit(solution)/shard_map/totals/ppermute | solution.py:21
  60.2 4.8 %collective-permute-start.15 = (f32[2,2,4,128]{3,2,1,0:T(4,128)S(1)}, f32[2,2,4,128]{3,2,1,0:T(4,128)S(1)}, u32[]{:S(2)}, u32[]{:S(2)}) collective-permute-start(f32[2,2,4,128]{3,2,1,0:T(4,128)S(1)} %maximum_add_fusion), channel_id=1, source_target_pairs={{0,16},{16,32},{32,48},{48,0},{1,17},{17,33},{33,49},{49,1},{2,18}... | collective-permute-start | bytes 24584 | tf_op jit(solution)/shard_map/totals/ppermute | solution.py:21
  60.2 6.1 %collective-permute-start.20 = (f32[2,4,2,128]{3,2,1,0:T(2,128)S(1)}, f32[2,4,2,128]{3,2,1,0:T(2,128)S(1)}, u32[]{:S(2)}, u32[]{:S(2)}) collective-permute-start(f32[2,4,2,128]{3,2,1,0:T(2,128)S(1)} %maximum_add_fusion.2), channel_id=1, source_target_pairs={{0,1},{128,129},{1,0},{129,128},{2,3},{130,131},{3,2},{131,130},{4... | collective-permute-start | bytes 24584 | tf_op jit(solution)/shard_map/totals/ppermute | solution.py:28
  62.3 3.8 %collective-permute-start.19 = (f32[2,4,2,128]{3,2,1,0:T(2,128)S(1)}, f32[2,4,2,128]{3,2,1,0:T(2,128)S(1)}, u32[]{:S(2)}, u32[]{:S(2)}) collective-permute-start(f32[2,4,2,128]{3,2,1,0:T(2,128)S(1)} %maximum_add_fusion.2), channel_id=1, source_target_pairs={{0,128},{128,1},{1,129},{129,0},{2,130},{130,3},{3,131},{131,2},{4... | collective-permute-start | bytes 24584 | tf_op jit(solution)/shard_map/totals/ppermute | solution.py:28
  63.8 2.5 %collective-permute-start.21 = (f32[2,4,2,128]{3,2,1,0:T(2,128)S(1)}, f32[2,4,2,128]{3,2,1,0:T(2,128)S(1)}, u32[]{:S(2)}, u32[]{:S(2)}) collective-permute-start(f32[2,4,2,128]{3,2,1,0:T(2,128)S(1)} %maximum_add_fusion.2), channel_id=1, source_target_pairs={{0,129},{128,0},{1,128},{129,1},{2,131},{130,2},{3,130},{131,3},{4... | collective-permute-start | bytes 24584 | tf_op jit(solution)/shard_map/totals/ppermute | solution.py:28
  69.4 5.2 %collective-permute-start.22 = (f32[4,128,512]{2,1,0:T(8,128)}, f32[4,128,512]{2,1,0:T(8,128)}, u32[]{:S(2)}, u32[]{:S(2)}) collective-permute-start(f32[4,128,512]{2,1,0:T(8,128)} %bitcast.25), channel_id=1, source_target_pairs={{0,64},{64,0},{1,65},{65,1},{2,66},{66,2},{3,67},{67,3},{4,68},{68... | collective-permute-start | bytes 3145736 | tf_op jit(solution)/shard_map/pull/ppermute | solution.py:21
  74.6 5.5 %slice-start = ((bf16[128,1152]{1,0:T(8,128)(2,1)}), bf16[128,1024]{1,0:T(8,128)(2,1)S(1)}, s32[]{:S(2)}) async-start(bf16[128,1152]{1,0:T(8,128)(2,1)} %copy-done.1), calls=%async_computation.1 | async-start | bytes 524288 | tf_op jit(solution)/shard_map/slice | solution.py:69
  76.2 8.3 %collective-permute-start.23 = (bf16[128,512]{1,0:T(8,128)(2,1)S(1)}, bf16[128,512]{1,0:T(8,128)(2,1)S(1)}, u32[]{:S(2)}, u32[]{:S(2)}) collective-permute-start(bf16[128,512]{1,0:T(8,128)(2,1)S(1)} %get-tuple-element.22), channel_id=1, source_target_pairs={{0,48},{16,0},{32,16},{48,32},{1,49},{17,1},{33,17},{49,33},{2,50}... | collective-permute-start | bytes 393224 | tf_op jit(solution)/shard_map/pull/ppermute | solution.py:21
  79.2 6.0 %collective-permute-start.24 = (bf16[128,512]{1,0:T(8,128)(2,1)S(1)}, bf16[128,512]{1,0:T(8,128)(2,1)S(1)}, u32[]{:S(2)}, u32[]{:S(2)}) collective-permute-start(bf16[128,512]{1,0:T(8,128)(2,1)S(1)} %get-tuple-element.24), channel_id=1, source_target_pairs={{0,32},{16,48},{32,0},{48,16},{1,33},{17,49},{33,1},{49,17},{2,34}... | collective-permute-start | bytes 393224 | tf_op jit(solution)/shard_map/pull/ppermute | solution.py:21
  79.2 9.1 %collective-permute-start.25 = (bf16[128,512]{1,0:T(8,128)(2,1)S(1)}, bf16[128,512]{1,0:T(8,128)(2,1)S(1)}, u32[]{:S(2)}, u32[]{:S(2)}) collective-permute-start(bf16[128,512]{1,0:T(8,128)(2,1)S(1)} %get-tuple-element.23), channel_id=1, source_target_pairs={{0,16},{16,32},{32,48},{48,0},{1,17},{17,33},{33,49},{49,1},{2,18}... | collective-permute-start | bytes 393224 | tf_op jit(solution)/shard_map/pull/ppermute | solution.py:21
  91.1 6.8 %collective-permute-start.26 = (bf16[32,512]{1,0:T(8,128)(2,1)S(1)}, bf16[32,512]{1,0:T(8,128)(2,1)S(1)}, u32[]{:S(2)}, u32[]{:S(2)}) collective-permute-start(bf16[32,512]{1,0:T(8,128)(2,1)S(1)} %get-tuple-element.33), channel_id=1, source_target_pairs={{0,12},{4,0},{8,4},{12,8},{1,13},{5,1},{9,5},{13,9},{2,14},{6,2},{... | collective-permute-start | bytes 98312 | tf_op jit(solution)/shard_map/head_part/ppermute | solution.py:21
  94.2 7.0 %collective-permute-start.27 = (bf16[32,512]{1,0:T(8,128)(2,1)S(1)}, bf16[32,512]{1,0:T(8,128)(2,1)S(1)}, u32[]{:S(2)}, u32[]{:S(2)}) collective-permute-start(bf16[32,512]{1,0:T(8,128)(2,1)S(1)} %get-tuple-element.32), channel_id=1, source_target_pairs={{0,8},{4,12},{8,0},{12,4},{1,9},{5,13},{9,1},{13,5},{2,10},{6,14},... | collective-permute-start | bytes 98312 | tf_op jit(solution)/shard_map/head_part/ppermute | solution.py:21
  94.2 7.0 %collective-permute-start.28 = (bf16[32,512]{1,0:T(8,128)(2,1)S(1)}, bf16[32,512]{1,0:T(8,128)(2,1)S(1)}, u32[]{:S(2)}, u32[]{:S(2)}) collective-permute-start(bf16[32,512]{1,0:T(8,128)(2,1)S(1)} %get-tuple-element.31), channel_id=1, source_target_pairs={{0,4},{4,8},{8,12},{12,0},{1,5},{5,9},{9,13},{13,1},{2,6},{6,10},{... | collective-permute-start | bytes 98312 | tf_op jit(solution)/shard_map/head_part/ppermute | solution.py:21
  101.2 24.7 %all-to-all-start = ((bf16[128,4,512]{2,1,0:T(4,128)(2,1)}), bf16[128,4,512]{2,1,0:T(4,128)(2,1)S(1)}, u32[]{:S(2)}, u32[]{:S(2)}) async-start(bf16[128,4,512]{2,1,0:T(4,128)(2,1)} %reshape.181), calls=%async_computation | async-start | bytes 1048576 | tf_op jit(solution)/shard_map/head/all_to_all | solution.py:143
  126.2 2.9 %collective-permute-start.29 = (f32[4,512]{1,0:T(4,128)S(1)}, f32[4,512]{1,0:T(4,128)S(1)}, u32[]{:S(2)}, u32[]{:S(2)}) collective-permute-start(f32[4,512]{1,0:T(4,128)S(1)} %convert_reduce_fusion.2), channel_id=1, source_target_pairs={{0,128},{128,0},{1,129},{129,1},{2,130},{130,2},{3,131},{131,3},{4... | collective-permute-start | bytes 24584 | tf_op jit(solution)/shard_map/head/ppermute | solution.py:21

commit v3 on v1

--- a/solution.py
+++ b/solution.py
@@ -28,18 +28,6 @@
     return lax.ppermute(
         value, ("yl", "yh"), [(seat[y], seat[(y + distance) % 4]) for y in range(4)]
     )
-
-
-def shift_yz(value, distance_y, distance_z):
-    if distance_y == 0 and distance_z == 0:
-        return value
-    seat = lambda y, z: (y % 2) * 4 + z * 2 + y // 2
-    pairs = [
-        (seat(y, z), seat((y + distance_y) % 4, (z + distance_z) % 2))
-        for y in range(4)
-        for z in range(2)
-    ]
-    return lax.ppermute(value, ("yl", "zl", "yh"), pairs)
 
 
 def unpack(stack, rows):
@@ -79,7 +67,8 @@
         packet = jnp.concatenate([normed, label_block], axis=0)
     with jax.named_scope("gather_sets"):
         across_x = jnp.stack([shift(packet, "x", 4, d) for d in range(4)])
-        set_b = jnp.stack([shift_yz(packet, dy, dz) for dy in range(4) for dz in range(2)])
+        across_y = [shift_y(packet, d) for d in range(4)]
+        set_b = jnp.stack([shift(block, "zl", 2, dz) for block in across_y for dz in range(2)])
         set_a = jnp.concatenate([across_x, shift(across_x, "c", 2, 1)], axis=0)
         normed_a, labels_a = unpack(set_a, rows)
         normed_b, labels_b = unpack(set_b, rows)
@@ -116,13 +105,19 @@
         soft_a, pos_a = weights(sums_a)
         soft_b, pos_b = weights(sums_b)
     with jax.named_scope("pull"):
-        coefficient = (
-            (soft_a[:, None] + soft_b[None, :]) * exponent
-            - (pos_a[:, None] + pos_b[None, :]) * positive
-        ).astype(bf16)
-        pull = jnp.dot(coefficient, normed_b, preferred_element_type=f32)
-        pull = pull.reshape(2, 4, rows, proj)
-        pull = pull[0] + shift(pull[1], "c", 2, 1)
+        half = total // 2
+
+        def pull_rows(start):
+            take = slice(start, start + half)
+            coefficient = (
+                (soft_a[take, None] + soft_b[None, :]) * exponent[take]
+                - (pos_a[take, None] + pos_b[None, :]) * positive[take]
+            ).astype(bf16)
+            part = jnp.dot(coefficient, normed_b, preferred_element_type=f32)
+            return part.reshape(4, rows, proj)
+
+        crossing = shift(pull_rows(half), "c", 2, 1)
+        pull = lax.optimization_barrier(pull_rows(0)) + crossing
         parts = [shift(pull[d].astype(bf16), "x", 4, -d).astype(f32) for d in range(1, 4)]
         pull_grad = (pull[0] + sum(parts)) / exponent_divisor
     with jax.named_scope("slopes"):
@@ -144,10 +139,10 @@
         ).astype(bf16)
         part = part.reshape(64, 2, width // 128, proj)
         part = lax.dynamic_index_in_dim(part, lax.axis_index("c"), axis=1, keepdims=False)
-        part = part.reshape(128, width // 256, proj)
-        spread = lax.all_to_all(part, KEY + ("yl",), split_axis=0, concat_axis=0, tiled=True)
+        spread = lax.all_to_all(part, KEY, split_axis=0, concat_axis=0, tiled=True)
         piece = jnp.sum(spread.astype(f32), axis=0)
-        grad_head = lax.all_gather(piece, ("c", "yl"), axis=0, tiled=True)
+        piece = piece + shift(piece, "yl", 2, 1)
+        grad_head = lax.all_gather(piece, "c", axis=0, tiled=True)
     return (grad_embeddings, grad_head / loss_scale)
 
 

time: 133 us -> 126 us (0.947)
  starting transfers between devices: 69.6 us -> 54.8 us
  waiting for transfers between devices: 27.4 us -> 39.2 us
  blocking collectives: 17.5 us -> 12 us
  other arithmetic: 6.44 us -> 8.55 us
  local copies, waits for them, and re-layouts: 3.36 us -> 1.45 us
  matrix products: 6.85 us -> 8.65 us
    ppermute x7 -> x0, starting transfers between devices: 11.4 us -> none  [shift_yz(): return lax.ppermute(value, ('yl', 'zl', 'yh'), pairs)]
    all_to_all x1, waiting for transfers between devices: 0.01 us -> 10.2 us  [body(): spread = lax.all_to_all(part, KEY, split_axis=0, concat_axis=0, tiled=True)]
    ppermute x19 -> x24, starting transfers between devices: 44.4 us -> 38.9 us  [shift(): lax.ppermute(value, axis, [(i, (i + distance) % size) for i in range(size)])]
    all_gather x1, blocking collectives: 12.4 us -> 7.18 us  [body(): grad_head = lax.all_gather(piece, 'c', axis=0, tiled=True)]
    ppermute x3 -> x6, starting transfers between devices: 4.71 us -> 9.7 us  [shift_y(): lax.ppermute(value, ('yl', 'yh'), [(seat[y], seat[(y + distance) % 4]) fo...]
    ppermute x19 -> x24, waiting for transfers between devices: 24.5 us -> 29 us  [shift(): lax.ppermute(value, axis, [(i, (i + distance) % size) for i in range(size)])]
    all_to_all x1, starting transfers between devices: 9.14 us -> 6.25 us  [body(): spread = lax.all_to_all(part, KEY, split_axis=0, concat_axis=0, tiled=True)]
    dot_general x1 -> x2, matrix products: 1.77 us -> 3.6 us  [pull_rows(): part = jnp.dot(coefficient, normed_b, preferred_element_type=f32)]
  transfers between devices with their start and end apart: 30 -> 31, of which waited for: 12 -> 16; matrix products, arithmetic and copies ran while one was open for 1% -> 3% of each run, Pallas kernels for 0% -> 0%
where the time goes in v3:
time: 126 us
  starting transfers between devices  54.8 us (43%)
  waiting for transfers between devices  39.2 us (31%)
  blocking collectives  12 us (10%)
  matrix products  8.65 us (7%)
  other arithmetic  8.55 us (7%)
  local copies, waits for them, and re-layouts  1.45 us (1%)
    ppermute x24, starting transfers between devices, shift(): lax.ppermute(value, axis, [(i, (i + distance) % size) for i in range(size)])  38.9 us
    ppermute x24, waiting for transfers between devices, shift(): lax.ppermute(value, axis, [(i, (i + distance) % size) for i in range(size)])  29 us
    all_to_all x1, waiting for transfers between devices, body(): spread = lax.all_to_all(part, KEY, split_axis=0, concat_axis=0, tiled=True)  10.2 us
    ppermute x6, starting transfers between devices, shift_y(): lax.ppermute(value, ('yl', 'yh'), [(seat[y], seat[(y + distance) % 4]) fo...  9.7 us
    all_gather x1, blocking collectives, body(): grad_head = lax.all_gather(piece, 'c', axis=0, tiled=True)  7.18 us
    all_to_all x1, starting transfers between devices, body(): spread = lax.all_to_all(part, KEY, split_axis=0, concat_axis=0, tiled=True)  6.25 us
    dot_general x2, matrix products, pull_rows(): part = jnp.dot(coefficient, normed_b, preferred_element_type=f32)  3.6 us
    all_gather x1, blocking collectives, body(): chip_rows = lax.all_gather(group_rows, 'c', axis=0, tiled=True)  2.73 us
  transfers between devices with their start and end apart: 31, of which 16 were waited for; matrix products, arithmetic and copies ran while one was open for 3% of the time, Pallas kernels for 0%

profile of v3, /device:TPU:1, one launch (start us, length us, event | category | flops | bytes accessed | tf_op | source)
XLA Modules:
  0.0 125.9 jit_solution(6568072583042534108)
XLA Ops:
  0.7 0.8 pad_add_fusion
  2.3 1.2 convolution_convert_fusion
  3.5 3.9 %collective-permute-start = (bf16[32,1152]{1,0:T(8,128)(2,1)S(1)}, bf16[32,1152]{1,0:T(8,128)(2,1)S(1)}, u32[]{:S(2)}, u32[]{:S(2)}) collective-permute-start(bf16[32,1152]{1,0:T(8,128)(2,1)S(1)} %get-tuple-element.18), channel_id=1, source_target_pairs={{0,4},{4,8},{8,12},{12,0},{1,5},{5,9},{9,13},{13,1},{2,6},{6,10},{... | collective-permute-start | bytes 221192 | tf_op jit(solution)/shard_map/route_out/ppermute | solution.py:21
  7.4 5.1 %collective-permute-start.1 = (bf16[32,1152]{1,0:T(8,128)(2,1)S(1)}, bf16[32,1152]{1,0:T(8,128)(2,1)S(1)}, u32[]{:S(2)}, u32[]{:S(2)}) collective-permute-start(bf16[32,1152]{1,0:T(8,128)(2,1)S(1)} %get-tuple-element.17), channel_id=1, source_target_pairs={{0,8},{4,12},{8,0},{12,4},{1,9},{5,13},{9,1},{13,5},{2,10},{6,14},... | collective-permute-start | bytes 221192 | tf_op jit(solution)/shard_map/route_out/ppermute | solution.py:21
  12.6 2.4 %collective-permute-start.2 = (bf16[32,1152]{1,0:T(8,128)(2,1)S(1)}, bf16[32,1152]{1,0:T(8,128)(2,1)S(1)}, u32[]{:S(2)}, u32[]{:S(2)}) collective-permute-start(bf16[32,1152]{1,0:T(8,128)(2,1)S(1)} %get-tuple-element.16), channel_id=1, source_target_pairs={{0,12},{4,0},{8,4},{12,8},{1,13},{5,1},{9,5},{13,9},{2,14},{6,2},{... | collective-permute-start | bytes 221192 | tf_op jit(solution)/shard_map/route_out/ppermute | solution.py:21
  14.9 2.0 %collective-permute-done.1 = bf16[32,1152]{1,0:T(8,128)(2,1)S(1)} collective-permute-done((bf16[32,1152]{1,0:T(8,128)(2,1)S(1)}, bf16[32,1152]{1,0:T(8,128)(2,1)S(1)}, u32[]{:S(2)}, u32[]{:S(2)}) %collective-permute-start.1) | collective-permute-done | bytes 73760 | tf_op jit(solution)/shard_map/route_out/ppermute | solution.py:21
  16.9 3.9 %collective-permute-done.2 = bf16[32,1152]{1,0:T(8,128)(2,1)S(1)} collective-permute-done((bf16[32,1152]{1,0:T(8,128)(2,1)S(1)}, bf16[32,1152]{1,0:T(8,128)(2,1)S(1)}, u32[]{:S(2)}, u32[]{:S(2)}) %collective-permute-start.2) | collective-permute-done | bytes 73760 | tf_op jit(solution)/shard_map/route_out/ppermute | solution.py:21
  21.7 1.3 %collective-permute-start.3 = (bf16[144,512]{1,0:T(8,128)(2,1)S(1)}, bf16[144,512]{1,0:T(8,128)(2,1)S(1)}, u32[]{:S(2)}, u32[]{:S(2)}) collective-permute-start(bf16[144,512]{1,0:T(8,128)(2,1)S(1)} %get-tuple-element.20), channel_id=1, source_target_pairs={{0,16},{16,32},{32,48},{48,0},{1,17},{17,33},{33,49},{49,1},{2,18}... | collective-permute-start | bytes 442376 | tf_op jit(solution)/shard_map/gather_sets/ppermute | solution.py:21
  22.9 2.5 %collective-permute-start.4 = (bf16[144,512]{1,0:T(8,128)(2,1)S(1)}, bf16[144,512]{1,0:T(8,128)(2,1)S(1)}, u32[]{:S(2)}, u32[]{:S(2)}) collective-permute-start(bf16[144,512]{1,0:T(8,128)(2,1)S(1)} %get-tuple-element.20), channel_id=1, source_target_pairs={{0,32},{16,48},{32,0},{48,16},{1,33},{17,49},{33,1},{49,17},{2,34}... | collective-permute-start | bytes 442376 | tf_op jit(solution)/shard_map/gather_sets/ppermute | solution.py:21
  25.4 1.2 collective-permute-start.5
  26.6 1.3 %collective-permute-start.8 = (bf16[144,512]{1,0:T(8,128)(2,1)S(1)}, bf16[144,512]{1,0:T(8,128)(2,1)S(1)}, u32[]{:S(2)}, u32[]{:S(2)}) collective-permute-start(bf16[144,512]{1,0:T(8,128)(2,1)S(1)} %get-tuple-element.20), channel_id=1, source_target_pairs={{0,128},{128,1},{1,129},{129,0},{2,130},{130,3},{3,131},{131,2},{4... | collective-permute-start | bytes 442376 | tf_op jit(solution)/shard_map/gather_sets/ppermute | solution.py:28
  28.0 2.8 %collective-permute-start.10 = (bf16[144,512]{1,0:T(8,128)(2,1)S(1)}, bf16[144,512]{1,0:T(8,128)(2,1)S(1)}, u32[]{:S(2)}, u32[]{:S(2)}) collective-permute-start(bf16[144,512]{1,0:T(8,128)(2,1)S(1)} %get-tuple-element.20), channel_id=1, source_target_pairs={{0,1},{128,129},{1,0},{129,128},{2,3},{130,131},{3,2},{131,130},{4... | collective-permute-start | bytes 442376 | tf_op jit(solution)/shard_map/gather_sets/ppermute | solution.py:28
  30.8 1.2 collective-permute-done.4
  32.0 2.7 %collective-permute-start.12 = (bf16[144,512]{1,0:T(8,128)(2,1)S(1)}, bf16[144,512]{1,0:T(8,128)(2,1)S(1)}, u32[]{:S(2)}, u32[]{:S(2)}) collective-permute-start(bf16[144,512]{1,0:T(8,128)(2,1)S(1)} %get-tuple-element.20), channel_id=1, source_target_pairs={{0,129},{128,0},{1,128},{129,1},{2,131},{130,2},{3,130},{131,3},{4... | collective-permute-start | bytes 442376 | tf_op jit(solution)/shard_map/gather_sets/ppermute | solution.py:28
  34.8 1.7 %collective-permute-start.6 = (bf16[4,144,512]{2,1,0:T(8,128)(2,1)S(1)}, bf16[4,144,512]{2,1,0:T(8,128)(2,1)S(1)}, u32[]{:S(2)}, u32[]{:S(2)}) collective-permute-start(bf16[4,144,512]{2,1,0:T(8,128)(2,1)S(1)} %pad_maximum_fusion), channel_id=1, source_target_pairs={{0,64},{64,0},{1,65},{65,1},{2,66},{66,2},{3,67},{67,3},{4,68},{68... | collective-permute-start | bytes 1769480 | tf_op jit(solution)/shard_map/gather_sets/ppermute | solution.py:21
  36.7 1.5 %collective-permute-start.11 = (bf16[144,512]{1,0:T(8,128)(2,1)S(1)}, bf16[144,512]{1,0:T(8,128)(2,1)S(1)}, u32[]{:S(2)}, u32[]{:S(2)}) collective-permute-start(bf16[144,512]{1,0:T(8,128)(2,1)S(1)} %collective-permute-done.10), channel_id=1, source_target_pairs={{0,2},{2,0},{1,3},{3,1},{4,6},{6,4},{5,7},{7,5},{8,10},{10,8},{9,1... | collective-permute-start | bytes 442376 | tf_op jit(solution)/shard_map/gather_sets/ppermute | solution.py:21
  38.6 3.5 %collective-permute-done.9 = bf16[144,512]{1,0:T(8,128)(2,1)S(1)} collective-permute-done((bf16[144,512]{1,0:T(8,128)(2,1)S(1)}, bf16[144,512]{1,0:T(8,128)(2,1)S(1)}, u32[]{:S(2)}, u32[]{:S(2)}) %collective-permute-start.9) | collective-permute-done | bytes 147488 | tf_op jit(solution)/shard_map/gather_sets/ppermute | solution.py:21
  42.1 3.1 %collective-permute-done.11 = bf16[144,512]{1,0:T(8,128)(2,1)S(1)} collective-permute-done((bf16[144,512]{1,0:T(8,128)(2,1)S(1)}, bf16[144,512]{1,0:T(8,128)(2,1)S(1)}, u32[]{:S(2)}, u32[]{:S(2)}) %collective-permute-start.11) | collective-permute-done | bytes 147488 | tf_op jit(solution)/shard_map/gather_sets/ppermute | solution.py:21
  45.3 3.1 %collective-permute-done.13 = bf16[144,512]{1,0:T(8,128)(2,1)S(1)} collective-permute-done((bf16[144,512]{1,0:T(8,128)(2,1)S(1)}, bf16[144,512]{1,0:T(8,128)(2,1)S(1)}, u32[]{:S(2)}, u32[]{:S(2)}) %collective-permute-start.13) | collective-permute-done | bytes 147488 | tf_op jit(solution)/shard_map/gather_sets/ppermute | solution.py:21
  48.7 2.2 %fusion.9 = (f32[1024]{0:T(1024)S(1)}, f32[1024]{0:T(1024)S(1)}) fusion(pred[1024]{0:T(1024)(128)(4,1)S(1)} %iota_compare_fusion.5, s32[1024]{0:T(1024)S(1)} %bitcast.101, s32[1024]{0:T(1024)S(1)} %bitcast.103), kind=kLoop, calls=%fused_computation.16 | loop fusion | flops 8386560 | bytes 17408 | tf_op jit(solution)/shard_map/scores/reduce_sum | solution.py:90
  51.6 1.6 %fusion.51 = (f32[1024]{0:T(1024)S(1)}, f32[1024]{0:T(1024)S(1)}, f32[1024,1024]{1,0:T(8,128)S(1)}) fusion(bf16[1024,512]{1,0:T(8,128)(2,1)S(1)} %bitcast.83, bf16[1024,512]{1,0:T(8,128)(2,1)S(1)} %bitcast.80, pred[1024]{0:T(1024)(128)(4,1)S(1)} %iota_compare_fusion.5), kind=kOutput, calls=%fused_computation.112 | convolution fusion | flops 1080031232 | bytes 6300672 | tf_op jit(solution)/shard_map/scores/dot_general | solution.py:79
  53.4 1.1 collective-permute-start.14
  54.4 1.4 %collective-permute-done.18 = f32[2,4,2,128]{3,2,1,0:T(2,128)S(1)} collective-permute-done((f32[2,4,2,128]{3,2,1,0:T(2,128)S(1)}, f32[2,4,2,128]{3,2,1,0:T(2,128)S(1)}, u32[]{:S(2)}, u32[]{:S(2)}) %collective-permute-start.18) | collective-permute-done | bytes 8224 | tf_op jit(solution)/shard_map/totals/ppermute | solution.py:21
  56.0 1.0 collective-permute-start.19
  57.0 1.7 %collective-permute-start.21 = (f32[2,4,2,128]{3,2,1,0:T(2,128)S(1)}, f32[2,4,2,128]{3,2,1,0:T(2,128)S(1)}, u32[]{:S(2)}, u32[]{:S(2)}) collective-permute-start(f32[2,4,2,128]{3,2,1,0:T(2,128)S(1)} %maximum_add_fusion.2), channel_id=1, source_target_pairs={{0,129},{128,0},{1,128},{129,1},{2,131},{130,2},{3,130},{131,3},{4... | collective-permute-start | bytes 24584 | tf_op jit(solution)/shard_map/totals/ppermute | solution.py:28
  58.7 1.8 %collective-permute-start.16 = (f32[2,2,4,128]{3,2,1,0:T(4,128)S(1)}, f32[2,2,4,128]{3,2,1,0:T(4,128)S(1)}, u32[]{:S(2)}, u32[]{:S(2)}) collective-permute-start(f32[2,2,4,128]{3,2,1,0:T(4,128)S(1)} %maximum_add_fusion), channel_id=1, source_target_pairs={{0,32},{16,48},{32,0},{48,16},{1,33},{17,49},{33,1},{49,17},{2,34}... | collective-permute-start | bytes 24584 | tf_op jit(solution)/shard_map/totals/ppermute | solution.py:21
  61.1 1.0 collective-permute-start.15
  62.1 0.7 collective-permute-done.16
  63.1 1.7 %collective-permute-done.15 = f32[2,2,4,128]{3,2,1,0:T(4,128)S(1)} collective-permute-done((f32[2,2,4,128]{3,2,1,0:T(4,128)S(1)}, f32[2,2,4,128]{3,2,1,0:T(4,128)S(1)}, u32[]{:S(2)}, u32[]{:S(2)}) %collective-permute-start.15) | collective-permute-done | bytes 8224 | tf_op jit(solution)/shard_map/totals/ppermute | solution.py:21
  64.8 1.0 fusion.5
  65.9 1.7 %fusion.60 = f32[4,128,512]{2,1,0:T(8,128)} fusion(bf16[4,128,1024]{2,1,0:T(8,128)(2,1)S(1)} %bitcast.79, bf16[1024,512,1]{1,0,2:T(8,128)(2,1)S(1)} %bitcast.81), kind=kOutput, calls=%fused_computation.121 | convolution fusion | flops 536870912 | bytes 3145728 | tf_op jit(solution)/shard_map/pull/dot_general | solution.py:116
  67.5 5.5 %collective-permute-start.22 = (f32[4,128,512]{2,1,0:T(8,128)}, f32[4,128,512]{2,1,0:T(8,128)}, u32[]{:S(2)}, u32[]{:S(2)}) collective-permute-start(f32[4,128,512]{2,1,0:T(8,128)} %fusion.60), channel_id=1, source_target_pairs={{0,64},{64,0},{1,65},{65,1},{2,66},{66,2},{3,67},{67,3},{4,68},{68... | collective-permute-start | bytes 3145736 | tf_op jit(solution)/shard_map/pull/ppermute | solution.py:21
  73.1 1.9 %fusion.59 = f32[4,128,512]{2,1,0:T(8,128)S(1)} fusion(bf16[4,128,1024]{2,1,0:T(8,128)(2,1)S(1)} %bitcast.78, bf16[1024,512,1]{1,0,2:T(8,128)(2,1)} %bitcast.82), kind=kOutput, calls=%fused_computation.120 | convolution fusion | flops 536870912 | bytes 3145728 | tf_op jit(solution)/shard_map/pull/dot_general | solution.py:116
  75.7 1.5 %fusion.52 = (bf16[4,128,512]{2,1,0:T(8,128)(2,1)S(1)}, f32[4,128,512]{2,1,0:T(8,128)S(1)}) fusion(f32[4,128,512]{2,1,0:T(8,128)S(1)} %fusion.59, f32[4,128,512]{2,1,0:T(8,128)} %collective-permute-done.22), kind=kLoop, calls=%fused_computation.113 | loop fusion | flops 524288 | bytes 3670016 | tf_op jit(solution)/shard_map/convert.2
  77.3 1.0 collective-permute-start.24
  78.8 2.7 %all_gather.9 = bf16[256,1024]{1,0:T(8,128)(2,1)S(1)} all-gather(bf16[128,1024]{1,0:T(8,128)(2,1)S(1)} %slice-done), channel_id=1, replica_groups=mesh['yl'=2,'c'=2,'x'=4,'zh'=4,'zl'=2,'yh'=2] {'c'}, dimensions={0}, use_global_device_ids=true | all-gather | bytes 786432 | tf_op jit(solution)/shard_map/gather_sets/all_gather | solution.py:75
  82.0 1.8 %collective-permute-done.24 = bf16[128,512]{1,0:T(8,128)(2,1)S(1)} collective-permute-done((bf16[128,512]{1,0:T(8,128)(2,1)S(1)}, bf16[128,512]{1,0:T(8,128)(2,1)S(1)}, u32[]{:S(2)}, u32[]{:S(2)}) %collective-permute-start.24) | collective-permute-done | bytes 131104 | tf_op jit(solution)/shard_map/pull/ppermute | solution.py:21
  83.9 3.5 %collective-permute-done.25 = bf16[128,512]{1,0:T(8,128)(2,1)S(1)} collective-permute-done((bf16[128,512]{1,0:T(8,128)(2,1)S(1)}, bf16[128,512]{1,0:T(8,128)(2,1)S(1)}, u32[]{:S(2)}, u32[]{:S(2)}) %collective-permute-start.25) | collective-permute-done | bytes 131104 | tf_op jit(solution)/shard_map/pull/ppermute | solution.py:21
  87.7 2.1 %all_gather.10 = bf16[256,512]{1,0:T(8,128)(2,1)S(1)} all-gather(bf16[128,512]{1,0:T(8,128)(2,1)S(1)} %divide_convert_fusion), channel_id=1, replica_groups=mesh['yl'=2,'c'=2,'x'=4,'zh'=4,'zl'=2,'yh'=2] {'c'}, dimensions={0}, use_global_device_ids=true | all-gather | bytes 393216 | tf_op jit(solution)/shard_map/head/all_gather | solution.py:136
  90.3 0.9 dynamic-slice_bitcast_fusion
  91.2 6.3 %all-to-all-start = ((bf16[64,8,512]{2,1,0:T(8,128)(2,1)}), bf16[64,8,512]{2,1,0:T(8,128)(2,1)S(1)}, u32[]{:S(2)}, u32[]{:S(2)}) async-start(bf16[64,8,512]{2,1,0:T(8,128)(2,1)} %dynamic-slice_bitcast_fusion), calls=%async_computation | async-start | bytes 1048576 | tf_op jit(solution)/shard_map/head/all_to_all | solution.py:142
  97.5 3.2 %collective-permute-start.26 = (bf16[32,512]{1,0:T(8,128)(2,1)S(1)}, bf16[32,512]{1,0:T(8,128)(2,1)S(1)}, u32[]{:S(2)}, u32[]{:S(2)}) collective-permute-start(bf16[32,512]{1,0:T(8,128)(2,1)S(1)} %get-tuple-element.24), channel_id=1, source_target_pairs={{0,12},{4,0},{8,4},{12,8},{1,13},{5,1},{9,5},{13,9},{2,14},{6,2},{... | collective-permute-start | bytes 98312 | tf_op jit(solution)/shard_map/route_back/ppermute | solution.py:21
  100.7 2.1 %collective-permute-start.27 = (bf16[32,512]{1,0:T(8,128)(2,1)S(1)}, bf16[32,512]{1,0:T(8,128)(2,1)S(1)}, u32[]{:S(2)}, u32[]{:S(2)}) collective-permute-start(bf16[32,512]{1,0:T(8,128)(2,1)S(1)} %get-tuple-element.23), channel_id=1, source_target_pairs={{0,8},{4,12},{8,0},{12,4},{1,9},{5,13},{9,1},{13,5},{2,10},{6,14},... | collective-permute-start | bytes 98312 | tf_op jit(solution)/shard_map/route_back/ppermute | solution.py:21
  102.7 2.1 %collective-permute-start.28 = (bf16[32,512]{1,0:T(8,128)(2,1)S(1)}, bf16[32,512]{1,0:T(8,128)(2,1)S(1)}, u32[]{:S(2)}, u32[]{:S(2)}) collective-permute-start(bf16[32,512]{1,0:T(8,128)(2,1)S(1)} %get-tuple-element.22), channel_id=1, source_target_pairs={{0,4},{4,8},{8,12},{12,0},{1,5},{5,9},{9,13},{13,1},{2,6},{6,10},{... | collective-permute-start | bytes 98312 | tf_op jit(solution)/shard_map/route_back/ppermute | solution.py:21
  104.8 10.2 %all-to-all-done = bf16[64,8,512]{2,1,0:T(8,128)(2,1)S(1)} async-done(((bf16[64,8,512]{2,1,0:T(8,128)(2,1)}), bf16[64,8,512]{2,1,0:T(8,128)(2,1)S(1)}, u32[]{:S(2)}, u32[]{:S(2)}) %all-to-all-start) | async-done | bytes 524320 | tf_op jit(solution)/shard_map/head/all_to_all | solution.py:142
  115.2 1.4 %convolution_convert_fusion.2 = bf16[128,1024]{1,0:T(8,128)(2,1)} fusion(bf16[1024,512]{1,0:T(8,128)(2,1)S(1)} %copy-done, bf16[32,512]{1,0:T(8,128)(2,1)S(1)} %collective-permute-done.28, bf16[32,512]{1,0:T(8,128)(2,1)S(1)} %collective-permute-done.27, bf16[32,512]{1,0:T(8,128)(2,1)S(1)} %collective-permute-done.26, ...), kind=kOutput, calls=%fused_computation.18 | convolution fusion | flops 151732224 | bytes 1442304 | tf_op jit(solution)/shard_map/route_back/dot_general | solution.py:132
  116.6 1.5 %collective-permute-done.29 = f32[8,512]{1,0:T(8,128)S(1)} collective-permute-done((f32[8,512]{1,0:T(8,128)S(1)}, f32[8,512]{1,0:T(8,128)S(1)}, u32[]{:S(2)}, u32[]{:S(2)}) %collective-permute-start.29) | collective-permute-done | bytes 16416 | tf_op jit(solution)/shard_map/head/ppermute | solution.py:21
  118.1 7.2 %all_gather.11 = f32[16,512]{1,0:T(8,128)S(1)} all-gather(f32[8,512]{1,0:T(8,128)S(1)} %add.163), channel_id=1, replica_groups=mesh['yl'=2,'c'=2,'x'=4,'zh'=4,'zl'=2,'yh'=2] {'c'}, dimensions={0}, use_global_device_ids=true | all-gather | bytes 49152 | tf_op jit(solution)/shard_map/head/all_gather | solution.py:145
  (98 shorter events, 7.7 us)
Async XLA Ops:
  0.6 20.2 %copy-start = (bf16[1024,512]{1,0:T(8,128)(2,1)S(1)}, bf16[1024,512]{1,0:T(8,128)(2,1)}, u32[]{:S(2)}) copy-start(bf16[1024,512]{1,0:T(8,128)(2,1)} %param.7) | copy-start | bytes 3145732
  3.5 11.4 %collective-permute-start = (bf16[32,1152]{1,0:T(8,128)(2,1)S(1)}, bf16[32,1152]{1,0:T(8,128)(2,1)S(1)}, u32[]{:S(2)}, u32[]{:S(2)}) collective-permute-start(bf16[32,1152]{1,0:T(8,128)(2,1)S(1)} %get-tuple-element.18), channel_id=1, source_target_pairs={{0,4},{4,8},{8,12},{12,0},{1,5},{5,9},{9,13},{13,1},{2,6},{6,10},{... | collective-permute-start | bytes 221192 | tf_op jit(solution)/shard_map/route_out/ppermute | solution.py:21
  7.4 9.5 %collective-permute-start.1 = (bf16[32,1152]{1,0:T(8,128)(2,1)S(1)}, bf16[32,1152]{1,0:T(8,128)(2,1)S(1)}, u32[]{:S(2)}, u32[]{:S(2)}) collective-permute-start(bf16[32,1152]{1,0:T(8,128)(2,1)S(1)} %get-tuple-element.17), channel_id=1, source_target_pairs={{0,8},{4,12},{8,0},{12,4},{1,9},{5,13},{9,1},{13,5},{2,10},{6,14},... | collective-permute-start | bytes 221192 | tf_op jit(solution)/shard_map/route_out/ppermute | solution.py:21
  12.6 8.3 %collective-permute-start.2 = (bf16[32,1152]{1,0:T(8,128)(2,1)S(1)}, bf16[32,1152]{1,0:T(8,128)(2,1)S(1)}, u32[]{:S(2)}, u32[]{:S(2)}) collective-permute-start(bf16[32,1152]{1,0:T(8,128)(2,1)S(1)} %get-tuple-element.16), channel_id=1, source_target_pairs={{0,12},{4,0},{8,4},{12,8},{1,13},{5,1},{9,5},{13,9},{2,14},{6,2},{... | collective-permute-start | bytes 221192 | tf_op jit(solution)/shard_map/route_out/ppermute | solution.py:21
  20.9 52.2 %copy-start.1 = (bf16[128,1152]{1,0:T(8,128)(2,1)}, bf16[128,1152]{1,0:T(8,128)(2,1)S(1)}, u32[]{:S(2)}) copy-start(bf16[128,1152]{1,0:T(8,128)(2,1)S(1)} %pad_maximum_fusion.1) | copy-start | bytes 884740
  21.7 6.3 %collective-permute-start.3 = (bf16[144,512]{1,0:T(8,128)(2,1)S(1)}, bf16[144,512]{1,0:T(8,128)(2,1)S(1)}, u32[]{:S(2)}, u32[]{:S(2)}) collective-permute-start(bf16[144,512]{1,0:T(8,128)(2,1)S(1)} %get-tuple-element.20), channel_id=1, source_target_pairs={{0,16},{16,32},{32,48},{48,0},{1,17},{17,33},{33,49},{49,1},{2,18}... | collective-permute-start | bytes 442376 | tf_op jit(solution)/shard_map/gather_sets/ppermute | solution.py:21
  22.9 9.1 %collective-permute-start.4 = (bf16[144,512]{1,0:T(8,128)(2,1)S(1)}, bf16[144,512]{1,0:T(8,128)(2,1)S(1)}, u32[]{:S(2)}, u32[]{:S(2)}) collective-permute-start(bf16[144,512]{1,0:T(8,128)(2,1)S(1)} %get-tuple-element.20), channel_id=1, source_target_pairs={{0,32},{16,48},{32,0},{48,16},{1,33},{17,49},{33,1},{49,17},{2,34}... | collective-permute-start | bytes 442376 | tf_op jit(solution)/shard_map/gather_sets/ppermute | solution.py:21
  25.4 9.4 %collective-permute-start.5 = (bf16[144,512]{1,0:T(8,128)(2,1)S(1)}, bf16[144,512]{1,0:T(8,128)(2,1)S(1)}, u32[]{:S(2)}, u32[]{:S(2)}) collective-permute-start(bf16[144,512]{1,0:T(8,128)(2,1)S(1)} %get-tuple-element.20), channel_id=1, source_target_pairs={{0,48},{16,0},{32,16},{48,32},{1,49},{17,1},{33,17},{49,33},{2,50}... | collective-permute-start | bytes 442376 | tf_op jit(solution)/shard_map/gather_sets/ppermute | solution.py:21
  26.6 11.7 %collective-permute-start.7 = (bf16[144,512]{1,0:T(8,128)(2,1)S(1)}, bf16[144,512]{1,0:T(8,128)(2,1)S(1)}, u32[]{:S(2)}, u32[]{:S(2)}) collective-permute-start(bf16[144,512]{1,0:T(8,128)(2,1)S(1)} %get-tuple-element.20), channel_id=1, source_target_pairs={{0,2},{2,0},{1,3},{3,1},{4,6},{6,4},{5,7},{7,5},{8,10},{10,8},{9,1... | collective-permute-start | bytes 442376 | tf_op jit(solution)/shard_map/gather_sets/ppermute | solution.py:21
  26.6 10.0 %collective-permute-start.8 = (bf16[144,512]{1,0:T(8,128)(2,1)S(1)}, bf16[144,512]{1,0:T(8,128)(2,1)S(1)}, u32[]{:S(2)}, u32[]{:S(2)}) collective-permute-start(bf16[144,512]{1,0:T(8,128)(2,1)S(1)} %get-tuple-element.20), channel_id=1, source_target_pairs={{0,128},{128,1},{1,129},{129,0},{2,130},{130,3},{3,131},{131,2},{4... | collective-permute-start | bytes 442376 | tf_op jit(solution)/shard_map/gather_sets/ppermute | solution.py:28
  28.0 8.7 %collective-permute-start.10 = (bf16[144,512]{1,0:T(8,128)(2,1)S(1)}, bf16[144,512]{1,0:T(8,128)(2,1)S(1)}, u32[]{:S(2)}, u32[]{:S(2)}) collective-permute-start(bf16[144,512]{1,0:T(8,128)(2,1)S(1)} %get-tuple-element.20), channel_id=1, source_target_pairs={{0,1},{128,129},{1,0},{129,128},{2,3},{130,131},{3,2},{131,130},{4... | collective-permute-start | bytes 442376 | tf_op jit(solution)/shard_map/gather_sets/ppermute | solution.py:28
  32.0 6.3 %collective-permute-start.12 = (bf16[144,512]{1,0:T(8,128)(2,1)S(1)}, bf16[144,512]{1,0:T(8,128)(2,1)S(1)}, u32[]{:S(2)}, u32[]{:S(2)}) collective-permute-start(bf16[144,512]{1,0:T(8,128)(2,1)S(1)} %get-tuple-element.20), channel_id=1, source_target_pairs={{0,129},{128,0},{1,128},{129,1},{2,131},{130,2},{3,130},{131,3},{4... | collective-permute-start | bytes 442376 | tf_op jit(solution)/shard_map/gather_sets/ppermute | solution.py:28
  34.8 13.7 %collective-permute-start.6 = (bf16[4,144,512]{2,1,0:T(8,128)(2,1)S(1)}, bf16[4,144,512]{2,1,0:T(8,128)(2,1)S(1)}, u32[]{:S(2)}, u32[]{:S(2)}) collective-permute-start(bf16[4,144,512]{2,1,0:T(8,128)(2,1)S(1)} %pad_maximum_fusion), channel_id=1, source_target_pairs={{0,64},{64,0},{1,65},{65,1},{2,66},{66,2},{3,67},{67,3},{4,68},{68... | collective-permute-start | bytes 1769480 | tf_op jit(solution)/shard_map/gather_sets/ppermute | solution.py:21
  36.6 5.5 %collective-permute-start.9 = (bf16[144,512]{1,0:T(8,128)(2,1)S(1)}, bf16[144,512]{1,0:T(8,128)(2,1)S(1)}, u32[]{:S(2)}, u32[]{:S(2)}) collective-permute-start(bf16[144,512]{1,0:T(8,128)(2,1)S(1)} %collective-permute-done.8), channel_id=1, source_target_pairs={{0,2},{2,0},{1,3},{3,1},{4,6},{6,4},{5,7},{7,5},{8,10},{10,8},{9,1... | collective-permute-start | bytes 442376 | tf_op jit(solution)/shard_map/gather_sets/ppermute | solution.py:21
  36.7 8.6 %collective-permute-start.11 = (bf16[144,512]{1,0:T(8,128)(2,1)S(1)}, bf16[144,512]{1,0:T(8,128)(2,1)S(1)}, u32[]{:S(2)}, u32[]{:S(2)}) collective-permute-start(bf16[144,512]{1,0:T(8,128)(2,1)S(1)} %collective-permute-done.10), channel_id=1, source_target_pairs={{0,2},{2,0},{1,3},{3,1},{4,6},{6,4},{5,7},{7,5},{8,10},{10,8},{9,1... | collective-permute-start | bytes 442376 | tf_op jit(solution)/shard_map/gather_sets/ppermute | solution.py:21
  38.3 10.2 %collective-permute-start.13 = (bf16[144,512]{1,0:T(8,128)(2,1)S(1)}, bf16[144,512]{1,0:T(8,128)(2,1)S(1)}, u32[]{:S(2)}, u32[]{:S(2)}) collective-permute-start(bf16[144,512]{1,0:T(8,128)(2,1)S(1)} %collective-permute-done.12), channel_id=1, source_target_pairs={{0,2},{2,0},{1,3},{3,1},{4,6},{6,4},{5,7},{7,5},{8,10},{10,8},{9,1... | collective-permute-start | bytes 442376 | tf_op jit(solution)/shard_map/gather_sets/ppermute | solution.py:21
  48.5 17.3 %copy-start.2 = (bf16[8,128,512]{2,1,0:T(8,128)(2,1)}, bf16[8,128,512]{2,1,0:T(8,128)(2,1)S(1)}, u32[]{:S(2)}) copy-start(bf16[8,128,512]{2,1,0:T(8,128)(2,1)S(1)} %slice.233) | copy-start | bytes 3145732
  53.2 2.6 %collective-permute-start.18 = (f32[2,4,2,128]{3,2,1,0:T(2,128)S(1)}, f32[2,4,2,128]{3,2,1,0:T(2,128)S(1)}, u32[]{:S(2)}, u32[]{:S(2)}) collective-permute-start(f32[2,4,2,128]{3,2,1,0:T(2,128)S(1)} %pad_maximum_fusion.4), channel_id=1, source_target_pairs={{0,2},{2,0},{1,3},{3,1},{4,6},{6,4},{5,7},{7,5},{8,10},{10,8},{9,1... | collective-permute-start | bytes 24584 | tf_op jit(solution)/shard_map/totals/ppermute | solution.py:21
  53.4 5.4 %collective-permute-start.14 = (f32[2,2,4,128]{3,2,1,0:T(4,128)S(1)}, f32[2,2,4,128]{3,2,1,0:T(4,128)S(1)}, u32[]{:S(2)}, u32[]{:S(2)}) collective-permute-start(f32[2,2,4,128]{3,2,1,0:T(4,128)S(1)} %pad_maximum_fusion.3), channel_id=1, source_target_pairs={{0,64},{64,0},{1,65},{65,1},{2,66},{66,2},{3,67},{67,3},{4,68},{68... | collective-permute-start | bytes 24584 | tf_op jit(solution)/shard_map/totals/ppermute | solution.py:21
  55.9 6.2 %collective-permute-start.20 = (f32[2,4,2,128]{3,2,1,0:T(2,128)S(1)}, f32[2,4,2,128]{3,2,1,0:T(2,128)S(1)}, u32[]{:S(2)}, u32[]{:S(2)}) collective-permute-start(f32[2,4,2,128]{3,2,1,0:T(2,128)S(1)} %maximum_add_fusion.2), channel_id=1, source_target_pairs={{0,1},{128,129},{1,0},{129,128},{2,3},{130,131},{3,2},{131,130},{4... | collective-permute-start | bytes 24584 | tf_op jit(solution)/shard_map/totals/ppermute | solution.py:28
  56.0 5.1 %collective-permute-start.19 = (f32[2,4,2,128]{3,2,1,0:T(2,128)S(1)}, f32[2,4,2,128]{3,2,1,0:T(2,128)S(1)}, u32[]{:S(2)}, u32[]{:S(2)}) collective-permute-start(f32[2,4,2,128]{3,2,1,0:T(2,128)S(1)} %maximum_add_fusion.2), channel_id=1, source_target_pairs={{0,128},{128,1},{1,129},{129,0},{2,130},{130,3},{3,131},{131,2},{4... | collective-permute-start | bytes 24584 | tf_op jit(solution)/shard_map/totals/ppermute | solution.py:28
  57.0 5.1 %collective-permute-start.21 = (f32[2,4,2,128]{3,2,1,0:T(2,128)S(1)}, f32[2,4,2,128]{3,2,1,0:T(2,128)S(1)}, u32[]{:S(2)}, u32[]{:S(2)}) collective-permute-start(f32[2,4,2,128]{3,2,1,0:T(2,128)S(1)} %maximum_add_fusion.2), channel_id=1, source_target_pairs={{0,129},{128,0},{1,128},{129,1},{2,131},{130,2},{3,130},{131,3},{4... | collective-permute-start | bytes 24584 | tf_op jit(solution)/shard_map/totals/ppermute | solution.py:28
  58.7 4.1 %collective-permute-start.16 = (f32[2,2,4,128]{3,2,1,0:T(4,128)S(1)}, f32[2,2,4,128]{3,2,1,0:T(4,128)S(1)}, u32[]{:S(2)}, u32[]{:S(2)}) collective-permute-start(f32[2,2,4,128]{3,2,1,0:T(4,128)S(1)} %maximum_add_fusion), channel_id=1, source_target_pairs={{0,32},{16,48},{32,0},{48,16},{1,33},{17,49},{33,1},{49,17},{2,34}... | collective-permute-start | bytes 24584 | tf_op jit(solution)/shard_map/totals/ppermute | solution.py:21
  60.6 2.5 %collective-permute-start.17 = (f32[2,2,4,128]{3,2,1,0:T(4,128)S(1)}, f32[2,2,4,128]{3,2,1,0:T(4,128)S(1)}, u32[]{:S(2)}, u32[]{:S(2)}) collective-permute-start(f32[2,2,4,128]{3,2,1,0:T(4,128)S(1)} %maximum_add_fusion), channel_id=1, source_target_pairs={{0,48},{16,0},{32,16},{48,32},{1,49},{17,1},{33,17},{49,33},{2,50}... | collective-permute-start | bytes 24584 | tf_op jit(solution)/shard_map/totals/ppermute | solution.py:21
  61.1 3.7 %collective-permute-start.15 = (f32[2,2,4,128]{3,2,1,0:T(4,128)S(1)}, f32[2,2,4,128]{3,2,1,0:T(4,128)S(1)}, u32[]{:S(2)}, u32[]{:S(2)}) collective-permute-start(f32[2,2,4,128]{3,2,1,0:T(4,128)S(1)} %maximum_add_fusion), channel_id=1, source_target_pairs={{0,16},{16,32},{32,48},{48,0},{1,17},{17,33},{33,49},{49,1},{2,18}... | collective-permute-start | bytes 24584 | tf_op jit(solution)/shard_map/totals/ppermute | solution.py:21
  67.5 8.2 %collective-permute-start.22 = (f32[4,128,512]{2,1,0:T(8,128)}, f32[4,128,512]{2,1,0:T(8,128)}, u32[]{:S(2)}, u32[]{:S(2)}) collective-permute-start(f32[4,128,512]{2,1,0:T(8,128)} %fusion.60), channel_id=1, source_target_pairs={{0,64},{64,0},{1,65},{65,1},{2,66},{66,2},{3,67},{67,3},{4,68},{68... | collective-permute-start | bytes 3145736 | tf_op jit(solution)/shard_map/pull/ppermute | solution.py:21
  75.0 3.8 %slice-start = ((bf16[128,1152]{1,0:T(8,128)(2,1)}), bf16[128,1024]{1,0:T(8,128)(2,1)S(1)}, s32[]{:S(2)}) async-start(bf16[128,1152]{1,0:T(8,128)(2,1)} %copy-done.1), calls=%async_computation.1 | async-start | bytes 524288 | tf_op jit(solution)/shard_map/slice | solution.py:57
  77.2 4.8 %collective-permute-start.23 = (bf16[128,512]{1,0:T(8,128)(2,1)S(1)}, bf16[128,512]{1,0:T(8,128)(2,1)S(1)}, u32[]{:S(2)}, u32[]{:S(2)}) collective-permute-start(bf16[128,512]{1,0:T(8,128)(2,1)S(1)} %get-tuple-element.12), channel_id=1, source_target_pairs={{0,48},{16,0},{32,16},{48,32},{1,49},{17,1},{33,17},{49,33},{2,50}... | collective-permute-start | bytes 393224 | tf_op jit(solution)/shard_map/pull/ppermute | solution.py:21
  77.3 6.5 %collective-permute-start.24 = (bf16[128,512]{1,0:T(8,128)(2,1)S(1)}, bf16[128,512]{1,0:T(8,128)(2,1)S(1)}, u32[]{:S(2)}, u32[]{:S(2)}) collective-permute-start(bf16[128,512]{1,0:T(8,128)(2,1)S(1)} %get-tuple-element.14), channel_id=1, source_target_pairs={{0,32},{16,48},{32,0},{48,16},{1,33},{17,49},{33,1},{49,17},{2,34}... | collective-permute-start | bytes 393224 | tf_op jit(solution)/shard_map/pull/ppermute | solution.py:21
  78.3 9.1 %collective-permute-start.25 = (bf16[128,512]{1,0:T(8,128)(2,1)S(1)}, bf16[128,512]{1,0:T(8,128)(2,1)S(1)}, u32[]{:S(2)}, u32[]{:S(2)}) collective-permute-start(bf16[128,512]{1,0:T(8,128)(2,1)S(1)} %get-tuple-element.13), channel_id=1, source_target_pairs={{0,16},{16,32},{32,48},{48,0},{1,17},{17,33},{33,49},{49,1},{2,18}... | collective-permute-start | bytes 393224 | tf_op jit(solution)/shard_map/pull/ppermute | solution.py:21
  91.2 23.8 %all-to-all-start = ((bf16[64,8,512]{2,1,0:T(8,128)(2,1)}), bf16[64,8,512]{2,1,0:T(8,128)(2,1)S(1)}, u32[]{:S(2)}, u32[]{:S(2)}) async-start(bf16[64,8,512]{2,1,0:T(8,128)(2,1)} %dynamic-slice_bitcast_fusion), calls=%async_computation | async-start | bytes 1048576 | tf_op jit(solution)/shard_map/head/all_to_all | solution.py:142
  97.5 17.7 %collective-permute-start.26 = (bf16[32,512]{1,0:T(8,128)(2,1)S(1)}, bf16[32,512]{1,0:T(8,128)(2,1)S(1)}, u32[]{:S(2)}, u32[]{:S(2)}) collective-permute-start(bf16[32,512]{1,0:T(8,128)(2,1)S(1)} %get-tuple-element.24), channel_id=1, source_target_pairs={{0,12},{4,0},{8,4},{12,8},{1,13},{5,1},{9,5},{13,9},{2,14},{6,2},{... | collective-permute-start | bytes 98312 | tf_op jit(solution)/shard_map/route_back/ppermute | solution.py:21
  100.7 14.5 %collective-permute-start.27 = (bf16[32,512]{1,0:T(8,128)(2,1)S(1)}, bf16[32,512]{1,0:T(8,128)(2,1)S(1)}, u32[]{:S(2)}, u32[]{:S(2)}) collective-permute-start(bf16[32,512]{1,0:T(8,128)(2,1)S(1)} %get-tuple-element.23), channel_id=1, source_target_pairs={{0,8},{4,12},{8,0},{12,4},{1,9},{5,13},{9,1},{13,5},{2,10},{6,14},... | collective-permute-start | bytes 98312 | tf_op jit(solution)/shard_map/route_back/ppermute | solution.py:21
  102.7 12.5 %collective-permute-start.28 = (bf16[32,512]{1,0:T(8,128)(2,1)S(1)}, bf16[32,512]{1,0:T(8,128)(2,1)S(1)}, u32[]{:S(2)}, u32[]{:S(2)}) collective-permute-start(bf16[32,512]{1,0:T(8,128)(2,1)S(1)} %get-tuple-element.22), channel_id=1, source_target_pairs={{0,4},{4,8},{8,12},{12,0},{1,5},{5,9},{9,13},{13,1},{2,6},{6,10},{... | collective-permute-start | bytes 98312 | tf_op jit(solution)/shard_map/route_back/ppermute | solution.py:21
  115.1 3.0 %collective-permute-start.29 = (f32[8,512]{1,0:T(8,128)S(1)}, f32[8,512]{1,0:T(8,128)S(1)}, u32[]{:S(2)}, u32[]{:S(2)}) collective-permute-start(f32[8,512]{1,0:T(8,128)S(1)} %convert_reduce_fusion), channel_id=1, source_target_pairs={{0,128},{128,0},{1,129},{129,1},{2,130},{130,2},{3,131},{131,3},{4... | collective-permute-start | bytes 49160 | tf_op jit(solution)/shard_map/head/ppermute | solution.py:21

commit v4 on v3

--- a/solution.py
+++ b/solution.py
@@ -55,10 +55,14 @@
         sent = sent.reshape(4, share, width + 128)
         got = jnp.concatenate([shift(sent[d], "zh", 4, d) for d in range(4)], axis=0)
     group_rows = got[:, :width]
+
+    def project(values):
+        projected = jnp.dot(values, head_weight, preferred_element_type=f32)
+        norm = jnp.sqrt(jnp.sum(projected * projected, axis=1, keepdims=True) + epsilon)
+        return projected / norm, norm
+
     with jax.named_scope("project"):
-        projected = jnp.dot(group_rows, head_weight, preferred_element_type=f32)
-        row_norm = jnp.sqrt(jnp.sum(projected * projected, axis=1, keepdims=True) + epsilon)
-        direction = projected / row_norm
+        direction, row_norm = project(group_rows)
         normed = direction.astype(bf16)
         label_line = jnp.concatenate(
             [got[:, width], got[:, width + 1], jnp.zeros((proj - 2 * rows,), bf16)]
@@ -66,13 +70,17 @@
         label_block = jnp.broadcast_to(label_line[None, :], (LABEL_ROWS, proj))
         packet = jnp.concatenate([normed, label_block], axis=0)
     with jax.named_scope("gather_sets"):
-        across_x = jnp.stack([shift(packet, "x", 4, d) for d in range(4)])
+        across_x = jnp.stack([shift(got, "x", 4, d) for d in range(4)])
         across_y = [shift_y(packet, d) for d in range(4)]
         set_b = jnp.stack([shift(block, "zl", 2, dz) for block in across_y for dz in range(2)])
+        normed_b, labels_b = unpack(set_b, rows)
         set_a = jnp.concatenate([across_x, shift(across_x, "c", 2, 1)], axis=0)
-        normed_a, labels_a = unpack(set_a, rows)
-        normed_b, labels_b = unpack(set_b, rows)
-        chip_rows = lax.all_gather(group_rows, "c", axis=0, tiled=True)
+        set_a = set_a.reshape(-1, width + 128)
+        rows_a = set_a[:, :width]
+        high = set_a[:, width].astype(jnp.int32)
+        labels_a = high * 64 + set_a[:, width + 1].astype(jnp.int32)
+        direction_a, norm_a = project(rows_a)
+        normed_a = direction_a.astype(bf16)
     with jax.named_scope("scores"):
         total = normed_a.shape[0]
         scores = (
@@ -116,13 +124,34 @@
             part = jnp.dot(coefficient, normed_b, preferred_element_type=f32)
             return part.reshape(4, rows, proj)
 
-        crossing = shift(pull_rows(half), "c", 2, 1)
-        pull = lax.optimization_barrier(pull_rows(0)) + crossing
+        pull_far = pull_rows(half)
+        crossing = shift(pull_far, "c", 2, 1)
+        pull_near = lax.optimization_barrier(pull_rows(0))
+
+    def to_slopes(pull_grad, unit, norm):
+        along = jnp.sum(unit * pull_grad, axis=1, keepdims=True)
+        return ((pull_grad - unit * along) / norm).astype(bf16)
+
+    with jax.named_scope("head"):
+        pull_part = jnp.concatenate([pull_near, pull_far]).reshape(total, proj)
+        slopes_part = to_slopes(pull_part / exponent_divisor, direction_a, norm_a)
+        part = lax.dot_general(
+            rows_a, slopes_part, (((0,), (0,)), ((), ())), preferred_element_type=f32
+        )
+        part = part.reshape(64, 2, width // 128, proj)
+        core = lax.axis_index("c")
+        kept = lax.dynamic_index_in_dim(part, core, axis=1, keepdims=False)
+        given = lax.dynamic_index_in_dim(part, 1 - core, axis=1, keepdims=False)
+        part = (kept + shift(given.astype(bf16), "c", 2, 1).astype(f32)).astype(bf16)
+        spread = lax.all_to_all(part, KEY, split_axis=0, concat_axis=0, tiled=True)
+        piece = jnp.sum(spread.astype(f32), axis=0)
+        piece = piece + shift(piece, "yl", 2, 1)
+        grad_head = lax.all_gather(piece, "c", axis=0, tiled=True)
+    with jax.named_scope("slopes"):
+        pull = pull_near + crossing
         parts = [shift(pull[d].astype(bf16), "x", 4, -d).astype(f32) for d in range(1, 4)]
         pull_grad = (pull[0] + sum(parts)) / exponent_divisor
-    with jax.named_scope("slopes"):
-        along = jnp.sum(direction * pull_grad, axis=1, keepdims=True)
-        slopes = ((pull_grad - direction * along) / row_norm).astype(bf16)
+        slopes = to_slopes(pull_grad, direction, row_norm)
     with jax.named_scope("route_back"):
         blocks = slopes.reshape(4, share, proj)
         returned = jnp.concatenate([shift(blocks[d], "zh", 4, -d) for d in range(4)], axis=0)
@@ -132,17 +161,6 @@
         grad_embeddings = lax.dot_general(
             own, head_weight, (((1,), (1,)), ((), ())), preferred_element_type=f32
         ).astype(bf16)
-    with jax.named_scope("head"):
-        chip_slopes = lax.all_gather(slopes, "c", axis=0, tiled=True)
-        part = lax.dot_general(
-            chip_rows, chip_slopes, (((0,), (0,)), ((), ())), preferred_element_type=f32
-        ).astype(bf16)
-        part = part.reshape(64, 2, width // 128, proj)
-        part = lax.dynamic_index_in_dim(part, lax.axis_index("c"), axis=1, keepdims=False)
-        spread = lax.all_to_all(part, KEY, split_axis=0, concat_axis=0, tiled=True)
-        piece = jnp.sum(spread.astype(f32), axis=0)
-        piece = piece + shift(piece, "yl", 2, 1)
-        grad_head = lax.all_gather(piece, "c", axis=0, tiled=True)
     return (grad_embeddings, grad_head / loss_scale)
 
 

time: 126 us -> 138 us (1.095)
  blocking collectives: 12 us -> 3.59 us
  local copies, waits for them, and re-layouts: 1.45 us -> 9.25 us
  other arithmetic: 8.55 us -> 15.6 us
  starting transfers between devices: 54.8 us -> 60.9 us
  waiting for transfers between devices: 39.2 us -> 35.1 us
  matrix products: 8.65 us -> 11.6 us
    all_to_all x1, waiting for transfers between devices: 10.2 us -> 0.01 us  [body(): spread = lax.all_to_all(part, KEY, split_axis=0, concat_axis=0, tiled=True)]
    ppermute x24 -> x25, starting transfers between devices: 38.9 us -> 45.5 us  [shift(): lax.ppermute(value, axis, [(i, (i + distance) % size) for i in range(size)])]
    all_gather x2 -> x0, blocking collectives: 4.86 us -> none  [the longest x1 2.73 us: body(): chip_rows = lax.all_gather(group_rows, 'c', axis=0, tiled=True)]
    unnamed x16 -> x27, local copies, waits for them, and re-layouts: 0.2 us -> 4.58 us
    dot_general x2 -> x3, matrix products: 0.85 us -> 4.63 us  [the longest x1 2.93 us: body(): lax.dot_general(rows_a, slopes_part, (((0,), (0,)), ((), ())), preferred_...]
    ppermute x6, waiting for transfers between devices: 0.02 us -> 3.67 us  [shift_y(): lax.ppermute(value, ('yl', 'yh'), [(seat[y], seat[(y + distance) % 4]) fo...]
    all_gather x1, blocking collectives: 7.18 us -> 3.59 us  [body(): grad_head = lax.all_gather(piece, 'c', axis=0, tiled=True)]
    div x0 -> x1, other arithmetic: none -> 2.84 us  [body(): slopes_part = to_slopes(pull_part / exponent_divisor, direction_a, norm_a)]
  transfers between devices with their start and end apart: 31 -> 32, of which waited for: 16 -> 13; matrix products, arithmetic and copies ran while one was open for 3% -> 13% of each run, Pallas kernels for 0% -> 0%
where the time goes in v4:
time: 138 us; the launch traced here: 137 us
  starting transfers between devices  60.9 us (44%)
  waiting for transfers between devices  35.1 us (25%)
  other arithmetic  15.6 us (11%)
  matrix products  11.6 us (8%)
  local copies, waits for them, and re-layouts  9.25 us (7%)
  blocking collectives  3.59 us (3%)
    ppermute x25, starting transfers between devices, shift(): lax.ppermute(value, axis, [(i, (i + distance) % size) for i in range(size)])  45.5 us
    ppermute x25, waiting for transfers between devices, shift(): lax.ppermute(value, axis, [(i, (i + distance) % size) for i in range(size)])  31.4 us
    ppermute x6, starting transfers between devices, shift_y(): lax.ppermute(value, ('yl', 'yh'), [(seat[y], seat[(y + distance) % 4]) fo...  10 us
    all_to_all x1, starting transfers between devices, body(): spread = lax.all_to_all(part, KEY, split_axis=0, concat_axis=0, tiled=True)  5.33 us
    unnamed x27, local copies, waits for them, and re-layouts  4.58 us
    ppermute x6, waiting for transfers between devices, shift_y(): lax.ppermute(value, ('yl', 'yh'), [(seat[y], seat[(y + distance) % 4]) fo...  3.67 us
    all_gather x1, blocking collectives, body(): grad_head = lax.all_gather(piece, 'c', axis=0, tiled=True)  3.59 us
    dot_general x1, matrix products, body(): lax.dot_general(rows_a, slopes_part, (((0,), (0,)), ((), ())), preferred_...  2.93 us
  transfers between devices with their start and end apart: 32, of which 13 were waited for; matrix products, arithmetic and copies ran while one was open for 13% of the time, Pallas kernels for 0%

profile of v4, /device:TPU:1, one launch (start us, length us, event | category | flops | bytes accessed | tf_op | source)
XLA Modules:
  0.0 137.2 jit_solution(9923911454990041922)
XLA Ops:
  2.3 1.2 convolution_convert_fusion
  3.5 3.9 %collective-permute-start = (bf16[32,1152]{1,0:T(8,128)(2,1)S(1)}, bf16[32,1152]{1,0:T(8,128)(2,1)S(1)}, u32[]{:S(2)}, u32[]{:S(2)}) collective-permute-start(bf16[32,1152]{1,0:T(8,128)(2,1)S(1)} %get-tuple-element.22), channel_id=1, source_target_pairs={{0,4},{4,8},{8,12},{12,0},{1,5},{5,9},{9,13},{13,1},{2,6},{6,10},{... | collective-permute-start | bytes 221192 | tf_op jit(solution)/shard_map/route_out/ppermute | solution.py:21
  7.4 5.1 %collective-permute-start.1 = (bf16[32,1152]{1,0:T(8,128)(2,1)S(1)}, bf16[32,1152]{1,0:T(8,128)(2,1)S(1)}, u32[]{:S(2)}, u32[]{:S(2)}) collective-permute-start(bf16[32,1152]{1,0:T(8,128)(2,1)S(1)} %get-tuple-element.21), channel_id=1, source_target_pairs={{0,8},{4,12},{8,0},{12,4},{1,9},{5,13},{9,1},{13,5},{2,10},{6,14},... | collective-permute-start | bytes 221192 | tf_op jit(solution)/shard_map/route_out/ppermute | solution.py:21
  12.6 2.4 %collective-permute-start.2 = (bf16[32,1152]{1,0:T(8,128)(2,1)S(1)}, bf16[32,1152]{1,0:T(8,128)(2,1)S(1)}, u32[]{:S(2)}, u32[]{:S(2)}) collective-permute-start(bf16[32,1152]{1,0:T(8,128)(2,1)S(1)} %get-tuple-element.20), channel_id=1, source_target_pairs={{0,12},{4,0},{8,4},{12,8},{1,13},{5,1},{9,5},{13,9},{2,14},{6,2},{... | collective-permute-start | bytes 221192 | tf_op jit(solution)/shard_map/route_out/ppermute | solution.py:21
  14.9 2.0 %collective-permute-done.1 = bf16[32,1152]{1,0:T(8,128)(2,1)S(1)} collective-permute-done((bf16[32,1152]{1,0:T(8,128)(2,1)S(1)}, bf16[32,1152]{1,0:T(8,128)(2,1)S(1)}, u32[]{:S(2)}, u32[]{:S(2)}) %collective-permute-start.1) | collective-permute-done | bytes 73760 | tf_op jit(solution)/shard_map/route_out/ppermute | solution.py:21
  16.9 3.9 %collective-permute-done.2 = bf16[32,1152]{1,0:T(8,128)(2,1)S(1)} collective-permute-done((bf16[32,1152]{1,0:T(8,128)(2,1)S(1)}, bf16[32,1152]{1,0:T(8,128)(2,1)S(1)}, u32[]{:S(2)}, u32[]{:S(2)}) %collective-permute-start.2) | collective-permute-done | bytes 73760 | tf_op jit(solution)/shard_map/route_out/ppermute | solution.py:21
  20.9 1.3 collective-permute-start.3
  22.2 2.5 %collective-permute-start.4 = (bf16[128,1152]{1,0:T(8,128)(2,1)S(1)}, bf16[128,1152]{1,0:T(8,128)(2,1)S(1)}, u32[]{:S(2)}, u32[]{:S(2)}) collective-permute-start(bf16[128,1152]{1,0:T(8,128)(2,1)S(1)} %get-tuple-element.18), channel_id=1, source_target_pairs={{0,32},{16,48},{32,0},{48,16},{1,33},{17,49},{33,1},{49,17},{2,34}... | collective-permute-start | bytes 884744 | tf_op jit(solution)/shard_map/gather_sets/ppermute | solution.py:21
  24.6 1.2 collective-permute-start.5
  26.6 1.4 %collective-permute-start.8 = (bf16[144,512]{1,0:T(8,128)(2,1)S(1)}, bf16[144,512]{1,0:T(8,128)(2,1)S(1)}, u32[]{:S(2)}, u32[]{:S(2)}) collective-permute-start(bf16[144,512]{1,0:T(8,128)(2,1)S(1)} %pad_maximum_fusion.2), channel_id=1, source_target_pairs={{0,128},{128,1},{1,129},{129,0},{2,130},{130,3},{3,131},{131,2},{4... | collective-permute-start | bytes 442376 | tf_op jit(solution)/shard_map/gather_sets/ppermute | solution.py:28
  28.1 2.9 %collective-permute-done.7 = bf16[144,512]{1,0:T(8,128)(2,1)S(1)} collective-permute-done((bf16[144,512]{1,0:T(8,128)(2,1)S(1)}, bf16[144,512]{1,0:T(8,128)(2,1)S(1)}, u32[]{:S(2)}, u32[]{:S(2)}) %collective-permute-start.7) | collective-permute-done | bytes 147488 | tf_op jit(solution)/shard_map/gather_sets/ppermute | solution.py:21
  30.9 2.9 %collective-permute-start.10 = (bf16[144,512]{1,0:T(8,128)(2,1)S(1)}, bf16[144,512]{1,0:T(8,128)(2,1)S(1)}, u32[]{:S(2)}, u32[]{:S(2)}) collective-permute-start(bf16[144,512]{1,0:T(8,128)(2,1)S(1)} %pad_maximum_fusion.2), channel_id=1, source_target_pairs={{0,1},{128,129},{1,0},{129,128},{2,3},{130,131},{3,2},{131,130},{4... | collective-permute-start | bytes 442376 | tf_op jit(solution)/shard_map/gather_sets/ppermute | solution.py:28
  34.7 2.1 %collective-permute-done.10 = bf16[144,512]{1,0:T(8,128)(2,1)S(1)} collective-permute-done((bf16[144,512]{1,0:T(8,128)(2,1)S(1)}, bf16[144,512]{1,0:T(8,128)(2,1)S(1)}, u32[]{:S(2)}, u32[]{:S(2)}) %collective-permute-start.10) | collective-permute-done | bytes 147488 | tf_op jit(solution)/shard_map/gather_sets/ppermute | solution.py:28
  37.5 1.5 %collective-permute-done.12 = bf16[144,512]{1,0:T(8,128)(2,1)S(1)} collective-permute-done((bf16[144,512]{1,0:T(8,128)(2,1)S(1)}, bf16[144,512]{1,0:T(8,128)(2,1)S(1)}, u32[]{:S(2)}, u32[]{:S(2)}) %collective-permute-start.12) | collective-permute-done | bytes 147488 | tf_op jit(solution)/shard_map/gather_sets/ppermute | solution.py:28
  39.1 1.5 %collective-permute-start.13 = (bf16[144,512]{1,0:T(8,128)(2,1)S(1)}, bf16[144,512]{1,0:T(8,128)(2,1)S(1)}, u32[]{:S(2)}, u32[]{:S(2)}) collective-permute-start(bf16[144,512]{1,0:T(8,128)(2,1)S(1)} %collective-permute-done.12), channel_id=1, source_target_pairs={{0,2},{2,0},{1,3},{3,1},{4,6},{6,4},{5,7},{7,5},{8,10},{10,8},{9,1... | collective-permute-start | bytes 442376 | tf_op jit(solution)/shard_map/gather_sets/ppermute | solution.py:21
  40.7 3.9 %collective-permute-start.6 = (bf16[4,128,1152]{2,1,0:T(8,128)(2,1)S(1)}, bf16[4,128,1152]{2,1,0:T(8,128)(2,1)S(1)}, u32[]{:S(2)}, u32[]{:S(2)}) collective-permute-start(bf16[4,128,1152]{2,1,0:T(8,128)(2,1)S(1)} %pad_maximum_fusion), channel_id=1, source_target_pairs={{0,64},{64,0},{1,65},{65,1},{2,66},{66,2},{3,67},{67,3},{4,68},{68... | collective-permute-start | bytes 3538952 | tf_op jit(solution)/shard_map/gather_sets/ppermute | solution.py:21
  44.8 2.1 %collective-permute-done.13 = bf16[144,512]{1,0:T(8,128)(2,1)S(1)} collective-permute-done((bf16[144,512]{1,0:T(8,128)(2,1)S(1)}, bf16[144,512]{1,0:T(8,128)(2,1)S(1)}, u32[]{:S(2)}, u32[]{:S(2)}) %collective-permute-start.13) | collective-permute-done | bytes 147488 | tf_op jit(solution)/shard_map/gather_sets/ppermute | solution.py:21
  49.4 1.3 multiply_reduce_fusion.1
  50.7 1.3 copy.11
  53.1 2.2 %fusion.9 = (f32[1024]{0:T(1024)S(1)}, f32[1024]{0:T(1024)S(1)}) fusion(pred[1024]{0:T(1024)(128)(4,1)S(1)} %iota_compare_fusion.5, s32[1024]{0:T(1024)S(1)} %bitcast.109, s32[1024]{0:T(1024)S(1)} %bitcast.111), kind=kLoop, calls=%fused_computation.20 | loop fusion | flops 8386560 | bytes 17408 | tf_op jit(solution)/shard_map/scores/reduce_sum | solution.py:98
  56.6 1.9 %fusion.58 = (f32[1024]{0:T(1024)S(1)}, f32[1024]{0:T(1024)S(1)}, f32[1024,1024]{1,0:T(8,128)S(1)}) fusion(bf16[1024,512]{1,0:T(8,128)(2,1)S(1)} %bitcast.89, f32[1024,512]{0,1:T(8,128)S(1)} %get-tuple-element.48, f32[1024]{0:T(1024)S(1)} %add_sqrt_fusion, pred[1024]{0:T(1024)(128)(4,1)S(1)} %iota_compare_fusion.5), kind=kOutput, calls=%fused_computation.124 | convolution fusion | flops 1081079808 | bytes 7353344 | tf_op jit(solution)/shard_map/scores/dot_general | solution.py:87
  58.6 3.4 %collective-permute-start.14 = (f32[2,2,4,128]{3,2,1,0:T(4,128)S(1)}, f32[2,2,4,128]{3,2,1,0:T(4,128)S(1)}, u32[]{:S(2)}, u32[]{:S(2)}) collective-permute-start(f32[2,2,4,128]{3,2,1,0:T(4,128)S(1)} %pad_maximum_fusion.3), channel_id=1, source_target_pairs={{0,64},{64,0},{1,65},{65,1},{2,66},{66,2},{3,67},{67,3},{4,68},{68... | collective-permute-start | bytes 24584 | tf_op jit(solution)/shard_map/totals/ppermute | solution.py:21
  62.1 2.2 %collective-permute-start.20 = (f32[2,4,2,128]{3,2,1,0:T(2,128)S(1)}, f32[2,4,2,128]{3,2,1,0:T(2,128)S(1)}, u32[]{:S(2)}, u32[]{:S(2)}) collective-permute-start(f32[2,4,2,128]{3,2,1,0:T(2,128)S(1)} %maximum_add_fusion.2), channel_id=1, source_target_pairs={{0,1},{128,129},{1,0},{129,128},{2,3},{130,131},{3,2},{131,130},{4... | collective-permute-start | bytes 24584 | tf_op jit(solution)/shard_map/totals/ppermute | solution.py:28
  65.1 1.8 %collective-permute-start.21 = (f32[2,4,2,128]{3,2,1,0:T(2,128)S(1)}, f32[2,4,2,128]{3,2,1,0:T(2,128)S(1)}, u32[]{:S(2)}, u32[]{:S(2)}) collective-permute-start(f32[2,4,2,128]{3,2,1,0:T(2,128)S(1)} %maximum_add_fusion.2), channel_id=1, source_target_pairs={{0,129},{128,0},{1,128},{129,1},{2,131},{130,2},{3,130},{131,3},{4... | collective-permute-start | bytes 24584 | tf_op jit(solution)/shard_map/totals/ppermute | solution.py:28
  67.3 2.3 %collective-permute-start.17 = (f32[2,2,4,128]{3,2,1,0:T(4,128)S(1)}, f32[2,2,4,128]{3,2,1,0:T(4,128)S(1)}, u32[]{:S(2)}, u32[]{:S(2)}) collective-permute-start(f32[2,2,4,128]{3,2,1,0:T(4,128)S(1)} %maximum_add_fusion), channel_id=1, source_target_pairs={{0,48},{16,0},{32,16},{48,32},{1,49},{17,1},{33,17},{49,33},{2,50}... | collective-permute-start | bytes 24584 | tf_op jit(solution)/shard_map/totals/ppermute | solution.py:21
  69.7 1.3 collective-permute-done.16
  71.1 2.2 %collective-permute-done.15 = f32[2,2,4,128]{3,2,1,0:T(4,128)S(1)} collective-permute-done((f32[2,2,4,128]{3,2,1,0:T(4,128)S(1)}, f32[2,2,4,128]{3,2,1,0:T(4,128)S(1)}, u32[]{:S(2)}, u32[]{:S(2)}) %collective-permute-start.15) | collective-permute-done | bytes 8224 | tf_op jit(solution)/shard_map/totals/ppermute | solution.py:21
  74.5 1.7 %fusion.68 = f32[4,128,512]{2,1,0:T(8,128)} fusion(bf16[4,128,1024]{2,1,0:T(8,128)(2,1)S(1)} %bitcast.88, bf16[1024,512,1]{1,0,2:T(8,128)(2,1)S(1)} %bitcast.90), kind=kOutput, calls=%fused_computation.134 | convolution fusion | flops 536870912 | bytes 3145728 | tf_op jit(solution)/shard_map/pull/dot_general | solution.py:124
  76.9 5.8 %collective-permute-start.22 = (f32[4,128,512]{2,1,0:T(8,128)}, f32[4,128,512]{2,1,0:T(8,128)}, u32[]{:S(2)}, u32[]{:S(2)}) collective-permute-start(f32[4,128,512]{2,1,0:T(8,128)} %fusion.68), channel_id=1, source_target_pairs={{0,64},{64,0},{1,65},{65,1},{2,66},{66,2},{3,67},{67,3},{4,68},{68... | collective-permute-start | bytes 3145736 | tf_op jit(solution)/shard_map/pull/ppermute | solution.py:21
  82.7 2.8 %maximum_multiply_fusion = f32[8,128,512]{2,1,0:T(8,128)} fusion(f32[4,128,512]{2,1,0:T(8,128)} %fusion.68, f32[4,128,512]{2,1,0:T(8,128)S(1)} %fusion.67), kind=kLoop, calls=%fused_computation.15 | loop fusion | flops 1048576 | bytes 4194304 | tf_op jit(solution)/shard_map/head/div | solution.py:137
  85.6 1.9 %copy.10 = f32[1024,512]{0,1:T(8,128)S(1)} copy(f32[1024,512]{1,0:T(8,128)} %bitcast.81) | data formatting | bytes 4194304 | tf_op jit(solution)/shard_map/head/div | solution.py:137
  87.5 2.0 %multiply_reduce_fusion = f32[1024]{0:T(1024)S(1)} fusion(f32[1024,512]{0,1:T(8,128)S(1)} %copy.10, f32[1024,512]{0,1:T(8,128)} %copy-done.3, f32[1024]{0:T(1024)S(1)} %add_sqrt_fusion), kind=kLoop, calls=%fused_computation.17 | loop fusion | flops 1571840 | bytes 4202496 | tf_op jit(solution)/shard_map/head/reduce_sum | solution.py:132
  89.7 2.9 %fusion.10 = f32[1024,512]{1,0:T(8,128)S(1)} fusion(bf16[1024,1152]{1,0:T(8,128)(2,1)} %bitcast.94, f32[1024,512]{0,1:T(8,128)S(1)} %copy.10, f32[1024]{0:T(1024)S(1)} %multiply_reduce_fusion, f32[1024]{0:T(1024)S(1)} %add_sqrt_fusion, f32[1024,512]{0,1:T(8,128)S(1)} %copy-done.4), kind=kOutput, calls=%fused_computation.21 | convolution fusion | flops 1076363264 | bytes 8396800 | tf_op jit(solution)/shard_map/head/dot_general | solution.py:138
  92.7 1.3 copy-done.5
  94.5 1.6 %collective-permute-done.29 = bf16[64,8,512]{2,1,0:T(8,128)(2,1)S(1)} collective-permute-done((bf16[64,8,512]{2,1,0:T(8,128)(2,1)S(1)}, bf16[64,8,512]{2,1,0:T(8,128)(2,1)S(1)}, u32[]{:S(2)}, u32[]{:S(2)}) %collective-permute-start.29) | collective-permute-done | bytes 524320 | tf_op jit(solution)/shard_map/head/ppermute | solution.py:21
  96.1 2.2 %fusion.14 = bf16[64,8,512]{2,1,0:T(8,128)(2,1)} fusion(bf16[64,8,512]{2,1,0:T(8,128)(2,1)S(1)} %collective-permute-done.29, f32[64,2,8,512]{3,2,1,0:T(8,128)} %bitcast.86, s32[]{:T(128)S(6)} %select_n.40), kind=kLoop, calls=%fused_computation.29 | loop fusion | flops 786432 | bytes 2097156 | tf_op jit(solution)/shard_map/head/convert_element_type | solution.py:145
  98.3 5.3 %all-to-all-start = ((bf16[64,8,512]{2,1,0:T(8,128)(2,1)}), bf16[64,8,512]{2,1,0:T(8,128)(2,1)S(1)}, u32[]{:S(2)}, u32[]{:S(2)}) async-start(bf16[64,8,512]{2,1,0:T(8,128)(2,1)} %fusion.14), calls=%async_computation | async-start | bytes 1048576 | tf_op jit(solution)/shard_map/head/all_to_all | solution.py:146
  103.7 1.5 %fusion.59 = (bf16[4,128,512]{2,1,0:T(8,128)(2,1)S(1)}, f32[4,128,512]{2,1,0:T(8,128)S(1)}) fusion(f32[4,128,512]{2,1,0:T(8,128)S(1)} %copy-done.2, f32[4,128,512]{2,1,0:T(8,128)} %collective-permute-done.22), kind=kLoop, calls=%fused_computation.125 | loop fusion | flops 524288 | bytes 3670016 | tf_op jit(solution)/shard_map/convert.2
  105.2 2.5 %collective-permute-start.23 = (bf16[128,512]{1,0:T(8,128)(2,1)S(1)}, bf16[128,512]{1,0:T(8,128)(2,1)S(1)}, u32[]{:S(2)}, u32[]{:S(2)}) collective-permute-start(bf16[128,512]{1,0:T(8,128)(2,1)S(1)} %get-tuple-element.14), channel_id=1, source_target_pairs={{0,48},{16,0},{32,16},{48,32},{1,49},{17,1},{33,17},{49,33},{2,50}... | collective-permute-start | bytes 393224 | tf_op jit(solution)/shard_map/slopes/ppermute | solution.py:21
  108.7 4.0 %collective-permute-done.23 = bf16[128,512]{1,0:T(8,128)(2,1)S(1)} collective-permute-done((bf16[128,512]{1,0:T(8,128)(2,1)S(1)}, bf16[128,512]{1,0:T(8,128)(2,1)S(1)}, u32[]{:S(2)}, u32[]{:S(2)}) %collective-permute-start.23) | collective-permute-done | bytes 131104 | tf_op jit(solution)/shard_map/slopes/ppermute | solution.py:21
  112.7 3.4 %collective-permute-done.24 = bf16[128,512]{1,0:T(8,128)(2,1)S(1)} collective-permute-done((bf16[128,512]{1,0:T(8,128)(2,1)S(1)}, bf16[128,512]{1,0:T(8,128)(2,1)S(1)}, u32[]{:S(2)}, u32[]{:S(2)}) %collective-permute-start.24) | collective-permute-done | bytes 131104 | tf_op jit(solution)/shard_map/slopes/ppermute | solution.py:21
  116.1 5.6 %collective-permute-done.25 = bf16[128,512]{1,0:T(8,128)(2,1)S(1)} collective-permute-done((bf16[128,512]{1,0:T(8,128)(2,1)S(1)}, bf16[128,512]{1,0:T(8,128)(2,1)S(1)}, u32[]{:S(2)}, u32[]{:S(2)}) %collective-permute-start.25) | collective-permute-done | bytes 131104 | tf_op jit(solution)/shard_map/slopes/ppermute | solution.py:21
  122.0 2.9 %collective-permute-start.26 = (bf16[32,512]{1,0:T(8,128)(2,1)S(1)}, bf16[32,512]{1,0:T(8,128)(2,1)S(1)}, u32[]{:S(2)}, u32[]{:S(2)}) collective-permute-start(bf16[32,512]{1,0:T(8,128)(2,1)S(1)} %get-tuple-element.26), channel_id=1, source_target_pairs={{0,12},{4,0},{8,4},{12,8},{1,13},{5,1},{9,5},{13,9},{2,14},{6,2},{... | collective-permute-start | bytes 98312 | tf_op jit(solution)/shard_map/route_back/ppermute | solution.py:21
  124.9 1.5 %collective-permute-start.27 = (bf16[32,512]{1,0:T(8,128)(2,1)S(1)}, bf16[32,512]{1,0:T(8,128)(2,1)S(1)}, u32[]{:S(2)}, u32[]{:S(2)}) collective-permute-start(bf16[32,512]{1,0:T(8,128)(2,1)S(1)} %get-tuple-element.25), channel_id=1, source_target_pairs={{0,8},{4,12},{8,0},{12,4},{1,9},{5,13},{9,1},{13,5},{2,10},{6,14},... | collective-permute-start | bytes 98312 | tf_op jit(solution)/shard_map/route_back/ppermute | solution.py:21
  126.4 1.9 %collective-permute-start.28 = (bf16[32,512]{1,0:T(8,128)(2,1)S(1)}, bf16[32,512]{1,0:T(8,128)(2,1)S(1)}, u32[]{:S(2)}, u32[]{:S(2)}) collective-permute-start(bf16[32,512]{1,0:T(8,128)(2,1)S(1)} %get-tuple-element.24), channel_id=1, source_target_pairs={{0,4},{4,8},{8,12},{12,0},{1,5},{5,9},{9,13},{13,1},{2,6},{6,10},{... | collective-permute-start | bytes 98312 | tf_op jit(solution)/shard_map/route_back/ppermute | solution.py:21
  129.2 2.4 %collective-permute-done.27 = bf16[32,512]{1,0:T(8,128)(2,1)S(1)} collective-permute-done((bf16[32,512]{1,0:T(8,128)(2,1)S(1)}, bf16[32,512]{1,0:T(8,128)(2,1)S(1)}, u32[]{:S(2)}, u32[]{:S(2)}) %collective-permute-start.27) | collective-permute-done | bytes 32800 | tf_op jit(solution)/shard_map/route_back/ppermute | solution.py:21
  131.6 1.4 convolution_convert_fusion.1
  133.0 3.6 %all_gather.3 = f32[16,512]{1,0:T(8,128)S(1)} all-gather(f32[8,512]{1,0:T(8,128)S(1)} %add.178), channel_id=1, replica_groups=mesh['yl'=2,'c'=2,'x'=4,'zh'=4,'zl'=2,'yh'=2] {'c'}, dimensions={0}, use_global_device_ids=true | all-gather | bytes 49152 | tf_op jit(solution)/shard_map/head/all_gather | solution.py:149
  (114 shorter events, 15.9 us)
Async XLA Ops:
  0.6 25.3 %copy-start = (bf16[1024,512]{1,0:T(8,128)(2,1)S(1)}, bf16[1024,512]{1,0:T(8,128)(2,1)}, u32[]{:S(2)}) copy-start(bf16[1024,512]{1,0:T(8,128)(2,1)} %param.7) | copy-start | bytes 3145732
  3.5 11.4 %collective-permute-start = (bf16[32,1152]{1,0:T(8,128)(2,1)S(1)}, bf16[32,1152]{1,0:T(8,128)(2,1)S(1)}, u32[]{:S(2)}, u32[]{:S(2)}) collective-permute-start(bf16[32,1152]{1,0:T(8,128)(2,1)S(1)} %get-tuple-element.22), channel_id=1, source_target_pairs={{0,4},{4,8},{8,12},{12,0},{1,5},{5,9},{9,13},{13,1},{2,6},{6,10},{... | collective-permute-start | bytes 221192 | tf_op jit(solution)/shard_map/route_out/ppermute | solution.py:21
  7.4 9.5 %collective-permute-start.1 = (bf16[32,1152]{1,0:T(8,128)(2,1)S(1)}, bf16[32,1152]{1,0:T(8,128)(2,1)S(1)}, u32[]{:S(2)}, u32[]{:S(2)}) collective-permute-start(bf16[32,1152]{1,0:T(8,128)(2,1)S(1)} %get-tuple-element.21), channel_id=1, source_target_pairs={{0,8},{4,12},{8,0},{12,4},{1,9},{5,13},{9,1},{13,5},{2,10},{6,14},... | collective-permute-start | bytes 221192 | tf_op jit(solution)/shard_map/route_out/ppermute | solution.py:21
  12.6 8.3 %collective-permute-start.2 = (bf16[32,1152]{1,0:T(8,128)(2,1)S(1)}, bf16[32,1152]{1,0:T(8,128)(2,1)S(1)}, u32[]{:S(2)}, u32[]{:S(2)}) collective-permute-start(bf16[32,1152]{1,0:T(8,128)(2,1)S(1)} %get-tuple-element.20), channel_id=1, source_target_pairs={{0,12},{4,0},{8,4},{12,8},{1,13},{5,1},{9,5},{13,9},{2,14},{6,2},{... | collective-permute-start | bytes 221192 | tf_op jit(solution)/shard_map/route_out/ppermute | solution.py:21
  20.9 18.2 %collective-permute-start.3 = (bf16[128,1152]{1,0:T(8,128)(2,1)S(1)}, bf16[128,1152]{1,0:T(8,128)(2,1)S(1)}, u32[]{:S(2)}, u32[]{:S(2)}) collective-permute-start(bf16[128,1152]{1,0:T(8,128)(2,1)S(1)} %get-tuple-element.18), channel_id=1, source_target_pairs={{0,16},{16,32},{32,48},{48,0},{1,17},{17,33},{33,49},{49,1},{2,18}... | collective-permute-start | bytes 884744 | tf_op jit(solution)/shard_map/gather_sets/ppermute | solution.py:21
  22.2 18.4 %collective-permute-start.4 = (bf16[128,1152]{1,0:T(8,128)(2,1)S(1)}, bf16[128,1152]{1,0:T(8,128)(2,1)S(1)}, u32[]{:S(2)}, u32[]{:S(2)}) collective-permute-start(bf16[128,1152]{1,0:T(8,128)(2,1)S(1)} %get-tuple-element.18), channel_id=1, source_target_pairs={{0,32},{16,48},{32,0},{48,16},{1,33},{17,49},{33,1},{49,17},{2,34}... | collective-permute-start | bytes 884744 | tf_op jit(solution)/shard_map/gather_sets/ppermute | solution.py:21
  24.6 15.9 %collective-permute-start.5 = (bf16[128,1152]{1,0:T(8,128)(2,1)S(1)}, bf16[128,1152]{1,0:T(8,128)(2,1)S(1)}, u32[]{:S(2)}, u32[]{:S(2)}) collective-permute-start(bf16[128,1152]{1,0:T(8,128)(2,1)S(1)} %get-tuple-element.18), channel_id=1, source_target_pairs={{0,48},{16,0},{32,16},{48,32},{1,49},{17,1},{33,17},{49,33},{2,50}... | collective-permute-start | bytes 884744 | tf_op jit(solution)/shard_map/gather_sets/ppermute | solution.py:21
  26.5 4.4 %collective-permute-start.7 = (bf16[144,512]{1,0:T(8,128)(2,1)S(1)}, bf16[144,512]{1,0:T(8,128)(2,1)S(1)}, u32[]{:S(2)}, u32[]{:S(2)}) collective-permute-start(bf16[144,512]{1,0:T(8,128)(2,1)S(1)} %pad_maximum_fusion.2), channel_id=1, source_target_pairs={{0,2},{2,0},{1,3},{3,1},{4,6},{6,4},{5,7},{7,5},{8,10},{10,8},{9,1... | collective-permute-start | bytes 442376 | tf_op jit(solution)/shard_map/gather_sets/ppermute | solution.py:21
  26.6 7.2 %collective-permute-start.8 = (bf16[144,512]{1,0:T(8,128)(2,1)S(1)}, bf16[144,512]{1,0:T(8,128)(2,1)S(1)}, u32[]{:S(2)}, u32[]{:S(2)}) collective-permute-start(bf16[144,512]{1,0:T(8,128)(2,1)S(1)} %pad_maximum_fusion.2), channel_id=1, source_target_pairs={{0,128},{128,1},{1,129},{129,0},{2,130},{130,3},{3,131},{131,2},{4... | collective-permute-start | bytes 442376 | tf_op jit(solution)/shard_map/gather_sets/ppermute | solution.py:28
  30.9 5.9 %collective-permute-start.10 = (bf16[144,512]{1,0:T(8,128)(2,1)S(1)}, bf16[144,512]{1,0:T(8,128)(2,1)S(1)}, u32[]{:S(2)}, u32[]{:S(2)}) collective-permute-start(bf16[144,512]{1,0:T(8,128)(2,1)S(1)} %pad_maximum_fusion.2), channel_id=1, source_target_pairs={{0,1},{128,129},{1,0},{129,128},{2,3},{130,131},{3,2},{131,130},{4... | collective-permute-start | bytes 442376 | tf_op jit(solution)/shard_map/gather_sets/ppermute | solution.py:28
  33.9 5.2 %collective-permute-start.12 = (bf16[144,512]{1,0:T(8,128)(2,1)S(1)}, bf16[144,512]{1,0:T(8,128)(2,1)S(1)}, u32[]{:S(2)}, u32[]{:S(2)}) collective-permute-start(bf16[144,512]{1,0:T(8,128)(2,1)S(1)} %pad_maximum_fusion.2), channel_id=1, source_target_pairs={{0,129},{128,0},{1,128},{129,1},{2,131},{130,2},{3,130},{131,3},{4... | collective-permute-start | bytes 442376 | tf_op jit(solution)/shard_map/gather_sets/ppermute | solution.py:28
  36.8 7.9 %collective-permute-start.9 = (bf16[144,512]{1,0:T(8,128)(2,1)S(1)}, bf16[144,512]{1,0:T(8,128)(2,1)S(1)}, u32[]{:S(2)}, u32[]{:S(2)}) collective-permute-start(bf16[144,512]{1,0:T(8,128)(2,1)S(1)} %collective-permute-done.8), channel_id=1, source_target_pairs={{0,2},{2,0},{1,3},{3,1},{4,6},{6,4},{5,7},{7,5},{8,10},{10,8},{9,1... | collective-permute-start | bytes 442376 | tf_op jit(solution)/shard_map/gather_sets/ppermute | solution.py:21
  39.1 5.7 %collective-permute-start.11 = (bf16[144,512]{1,0:T(8,128)(2,1)S(1)}, bf16[144,512]{1,0:T(8,128)(2,1)S(1)}, u32[]{:S(2)}, u32[]{:S(2)}) collective-permute-start(bf16[144,512]{1,0:T(8,128)(2,1)S(1)} %collective-permute-done.10), channel_id=1, source_target_pairs={{0,2},{2,0},{1,3},{3,1},{4,6},{6,4},{5,7},{7,5},{8,10},{10,8},{9,1... | collective-permute-start | bytes 442376 | tf_op jit(solution)/shard_map/gather_sets/ppermute | solution.py:21
  39.1 7.9 %collective-permute-start.13 = (bf16[144,512]{1,0:T(8,128)(2,1)S(1)}, bf16[144,512]{1,0:T(8,128)(2,1)S(1)}, u32[]{:S(2)}, u32[]{:S(2)}) collective-permute-start(bf16[144,512]{1,0:T(8,128)(2,1)S(1)} %collective-permute-done.12), channel_id=1, source_target_pairs={{0,2},{2,0},{1,3},{3,1},{4,6},{6,4},{5,7},{7,5},{8,10},{10,8},{9,1... | collective-permute-start | bytes 442376 | tf_op jit(solution)/shard_map/gather_sets/ppermute | solution.py:21
  40.7 7.4 %collective-permute-start.6 = (bf16[4,128,1152]{2,1,0:T(8,128)(2,1)S(1)}, bf16[4,128,1152]{2,1,0:T(8,128)(2,1)S(1)}, u32[]{:S(2)}, u32[]{:S(2)}) collective-permute-start(bf16[4,128,1152]{2,1,0:T(8,128)(2,1)S(1)} %pad_maximum_fusion), channel_id=1, source_target_pairs={{0,64},{64,0},{1,65},{65,1},{2,66},{66,2},{3,67},{67,3},{4,68},{68... | collective-permute-start | bytes 3538952 | tf_op jit(solution)/shard_map/gather_sets/ppermute | solution.py:21
  48.3 2.4 %copy-start.7 = (bf16[8,128,1152]{2,1,0:T(8,128)(2,1)}, bf16[8,128,1152]{2,1,0:T(8,128)(2,1)S(1)}, u32[]{:S(2)}) copy-start(bf16[8,128,1152]{2,1,0:T(8,128)(2,1)S(1)} %constant_dynamic-update-slice_fusion) | copy-start | bytes 7077892
  50.7 5.3 %copy-start.3 = (f32[1024,512]{0,1:T(8,128)}, f32[1024,512]{0,1:T(8,128)S(1)}, u32[]{:S(2)}) copy-start(f32[1024,512]{0,1:T(8,128)S(1)} %get-tuple-element.48) | copy-start | bytes 6291460
  55.3 1.2 copy-start.6
  58.5 3.5 %collective-permute-start.18 = (f32[2,4,2,128]{3,2,1,0:T(2,128)S(1)}, f32[2,4,2,128]{3,2,1,0:T(2,128)S(1)}, u32[]{:S(2)}, u32[]{:S(2)}) collective-permute-start(f32[2,4,2,128]{3,2,1,0:T(2,128)S(1)} %pad_maximum_fusion.4), channel_id=1, source_target_pairs={{0,2},{2,0},{1,3},{3,1},{4,6},{6,4},{5,7},{7,5},{8,10},{10,8},{9,1... | collective-permute-start | bytes 24584 | tf_op jit(solution)/shard_map/totals/ppermute | solution.py:21
  58.6 8.3 %collective-permute-start.14 = (f32[2,2,4,128]{3,2,1,0:T(4,128)S(1)}, f32[2,2,4,128]{3,2,1,0:T(4,128)S(1)}, u32[]{:S(2)}, u32[]{:S(2)}) collective-permute-start(f32[2,2,4,128]{3,2,1,0:T(4,128)S(1)} %pad_maximum_fusion.3), channel_id=1, source_target_pairs={{0,64},{64,0},{1,65},{65,1},{2,66},{66,2},{3,67},{67,3},{4,68},{68... | collective-permute-start | bytes 24584 | tf_op jit(solution)/shard_map/totals/ppermute | solution.py:21
  62.1 7.6 %collective-permute-start.20 = (f32[2,4,2,128]{3,2,1,0:T(2,128)S(1)}, f32[2,4,2,128]{3,2,1,0:T(2,128)S(1)}, u32[]{:S(2)}, u32[]{:S(2)}) collective-permute-start(f32[2,4,2,128]{3,2,1,0:T(2,128)S(1)} %maximum_add_fusion.2), channel_id=1, source_target_pairs={{0,1},{128,129},{1,0},{129,128},{2,3},{130,131},{3,2},{131,130},{4... | collective-permute-start | bytes 24584 | tf_op jit(solution)/shard_map/totals/ppermute | solution.py:28
  64.3 5.4 %collective-permute-start.19 = (f32[2,4,2,128]{3,2,1,0:T(2,128)S(1)}, f32[2,4,2,128]{3,2,1,0:T(2,128)S(1)}, u32[]{:S(2)}, u32[]{:S(2)}) collective-permute-start(f32[2,4,2,128]{3,2,1,0:T(2,128)S(1)} %maximum_add_fusion.2), channel_id=1, source_target_pairs={{0,128},{128,1},{1,129},{129,0},{2,130},{130,3},{3,131},{131,2},{4... | collective-permute-start | bytes 24584 | tf_op jit(solution)/shard_map/totals/ppermute | solution.py:28
  65.1 4.5 %collective-permute-start.21 = (f32[2,4,2,128]{3,2,1,0:T(2,128)S(1)}, f32[2,4,2,128]{3,2,1,0:T(2,128)S(1)}, u32[]{:S(2)}, u32[]{:S(2)}) collective-permute-start(f32[2,4,2,128]{3,2,1,0:T(2,128)S(1)} %maximum_add_fusion.2), channel_id=1, source_target_pairs={{0,129},{128,0},{1,128},{129,1},{2,131},{130,2},{3,130},{131,3},{4... | collective-permute-start | bytes 24584 | tf_op jit(solution)/shard_map/totals/ppermute | solution.py:28
  67.0 4.1 %collective-permute-start.16 = (f32[2,2,4,128]{3,2,1,0:T(4,128)S(1)}, f32[2,2,4,128]{3,2,1,0:T(4,128)S(1)}, u32[]{:S(2)}, u32[]{:S(2)}) collective-permute-start(f32[2,2,4,128]{3,2,1,0:T(4,128)S(1)} %maximum_add_fusion), channel_id=1, source_target_pairs={{0,32},{16,48},{32,0},{48,16},{1,33},{17,49},{33,1},{49,17},{2,34}... | collective-permute-start | bytes 24584 | tf_op jit(solution)/shard_map/totals/ppermute | solution.py:21
  67.3 3.8 %collective-permute-start.17 = (f32[2,2,4,128]{3,2,1,0:T(4,128)S(1)}, f32[2,2,4,128]{3,2,1,0:T(4,128)S(1)}, u32[]{:S(2)}, u32[]{:S(2)}) collective-permute-start(f32[2,2,4,128]{3,2,1,0:T(4,128)S(1)} %maximum_add_fusion), channel_id=1, source_target_pairs={{0,48},{16,0},{32,16},{48,32},{1,49},{17,1},{33,17},{49,33},{2,50}... | collective-permute-start | bytes 24584 | tf_op jit(solution)/shard_map/totals/ppermute | solution.py:21
  69.6 3.7 %collective-permute-start.15 = (f32[2,2,4,128]{3,2,1,0:T(4,128)S(1)}, f32[2,2,4,128]{3,2,1,0:T(4,128)S(1)}, u32[]{:S(2)}, u32[]{:S(2)}) collective-permute-start(f32[2,2,4,128]{3,2,1,0:T(4,128)S(1)} %maximum_add_fusion), channel_id=1, source_target_pairs={{0,16},{16,32},{32,48},{48,0},{1,17},{17,33},{33,49},{49,1},{2,18}... | collective-permute-start | bytes 24584 | tf_op jit(solution)/shard_map/totals/ppermute | solution.py:21
  76.9 8.7 %copy-start.1 = (f32[4,128,512]{2,1,0:T(8,128)}, f32[4,128,512]{2,1,0:T(8,128)S(1)}, u32[]{:S(2)}) copy-start(f32[4,128,512]{2,1,0:T(8,128)S(1)} %fusion.67) | copy-start | bytes 3145732
  76.9 26.7 %collective-permute-start.22 = (f32[4,128,512]{2,1,0:T(8,128)}, f32[4,128,512]{2,1,0:T(8,128)}, u32[]{:S(2)}, u32[]{:S(2)}) collective-permute-start(f32[4,128,512]{2,1,0:T(8,128)} %fusion.68), channel_id=1, source_target_pairs={{0,64},{64,0},{1,65},{65,1},{2,66},{66,2},{3,67},{67,3},{4,68},{68... | collective-permute-start | bytes 3145736 | tf_op jit(solution)/shard_map/pull/ppermute | solution.py:21
  87.5 2.2 %copy-start.4 = (f32[1024,512]{0,1:T(8,128)S(1)}, f32[1024,512]{0,1:T(8,128)}, u32[]{:S(2)}) copy-start(f32[1024,512]{0,1:T(8,128)} %copy-done.3) | copy-start | bytes 6291460
  92.7 1.4 copy-start.5
  94.0 9.6 %copy-start.2 = (f32[4,128,512]{2,1,0:T(8,128)S(1)}, f32[4,128,512]{2,1,0:T(8,128)}, u32[]{:S(2)}) copy-start(f32[4,128,512]{2,1,0:T(8,128)} %copy-done.1) | copy-start | bytes 3145732
  94.1 2.0 %collective-permute-start.29 = (bf16[64,8,512]{2,1,0:T(8,128)(2,1)S(1)}, bf16[64,8,512]{2,1,0:T(8,128)(2,1)S(1)}, u32[]{:S(2)}, u32[]{:S(2)}) collective-permute-start(bf16[64,8,512]{2,1,0:T(8,128)(2,1)S(1)} %fusion.18), channel_id=1, source_target_pairs={{0,64},{64,0},{1,65},{65,1},{2,66},{66,2},{3,67},{67,3},{4,68},{68... | collective-permute-start | bytes 1572872 | tf_op jit(solution)/shard_map/head/ppermute | solution.py:21
  98.3 30.0 %all-to-all-start = ((bf16[64,8,512]{2,1,0:T(8,128)(2,1)}), bf16[64,8,512]{2,1,0:T(8,128)(2,1)S(1)}, u32[]{:S(2)}, u32[]{:S(2)}) async-start(bf16[64,8,512]{2,1,0:T(8,128)(2,1)} %fusion.14), calls=%async_computation | async-start | bytes 1048576 | tf_op jit(solution)/shard_map/head/all_to_all | solution.py:146
  105.2 7.5 %collective-permute-start.23 = (bf16[128,512]{1,0:T(8,128)(2,1)S(1)}, bf16[128,512]{1,0:T(8,128)(2,1)S(1)}, u32[]{:S(2)}, u32[]{:S(2)}) collective-permute-start(bf16[128,512]{1,0:T(8,128)(2,1)S(1)} %get-tuple-element.14), channel_id=1, source_target_pairs={{0,48},{16,0},{32,16},{48,32},{1,49},{17,1},{33,17},{49,33},{2,50}... | collective-permute-start | bytes 393224 | tf_op jit(solution)/shard_map/slopes/ppermute | solution.py:21
  107.7 8.4 %collective-permute-start.24 = (bf16[128,512]{1,0:T(8,128)(2,1)S(1)}, bf16[128,512]{1,0:T(8,128)(2,1)S(1)}, u32[]{:S(2)}, u32[]{:S(2)}) collective-permute-start(bf16[128,512]{1,0:T(8,128)(2,1)S(1)} %get-tuple-element.16), channel_id=1, source_target_pairs={{0,32},{16,48},{32,0},{48,16},{1,33},{17,49},{33,1},{49,17},{2,34}... | collective-permute-start | bytes 393224 | tf_op jit(solution)/shard_map/slopes/ppermute | solution.py:21
  108.1 13.6 %collective-permute-start.25 = (bf16[128,512]{1,0:T(8,128)(2,1)S(1)}, bf16[128,512]{1,0:T(8,128)(2,1)S(1)}, u32[]{:S(2)}, u32[]{:S(2)}) collective-permute-start(bf16[128,512]{1,0:T(8,128)(2,1)S(1)} %get-tuple-element.15), channel_id=1, source_target_pairs={{0,16},{16,32},{32,48},{48,0},{1,17},{17,33},{33,49},{49,1},{2,18}... | collective-permute-start | bytes 393224 | tf_op jit(solution)/shard_map/slopes/ppermute | solution.py:21
  122.0 7.2 %collective-permute-start.26 = (bf16[32,512]{1,0:T(8,128)(2,1)S(1)}, bf16[32,512]{1,0:T(8,128)(2,1)S(1)}, u32[]{:S(2)}, u32[]{:S(2)}) collective-permute-start(bf16[32,512]{1,0:T(8,128)(2,1)S(1)} %get-tuple-element.26), channel_id=1, source_target_pairs={{0,12},{4,0},{8,4},{12,8},{1,13},{5,1},{9,5},{13,9},{2,14},{6,2},{... | collective-permute-start | bytes 98312 | tf_op jit(solution)/shard_map/route_back/ppermute | solution.py:21
  124.9 6.8 %collective-permute-start.27 = (bf16[32,512]{1,0:T(8,128)(2,1)S(1)}, bf16[32,512]{1,0:T(8,128)(2,1)S(1)}, u32[]{:S(2)}, u32[]{:S(2)}) collective-permute-start(bf16[32,512]{1,0:T(8,128)(2,1)S(1)} %get-tuple-element.25), channel_id=1, source_target_pairs={{0,8},{4,12},{8,0},{12,4},{1,9},{5,13},{9,1},{13,5},{2,10},{6,14},... | collective-permute-start | bytes 98312 | tf_op jit(solution)/shard_map/route_back/ppermute | solution.py:21
  126.4 5.3 %collective-permute-start.28 = (bf16[32,512]{1,0:T(8,128)(2,1)S(1)}, bf16[32,512]{1,0:T(8,128)(2,1)S(1)}, u32[]{:S(2)}, u32[]{:S(2)}) collective-permute-start(bf16[32,512]{1,0:T(8,128)(2,1)S(1)} %get-tuple-element.24), channel_id=1, source_target_pairs={{0,4},{4,8},{8,12},{12,0},{1,5},{5,9},{9,13},{13,1},{2,6},{6,10},{... | collective-permute-start | bytes 98312 | tf_op jit(solution)/shard_map/route_back/ppermute | solution.py:21
  128.4 4.6 %collective-permute-start.30 = (f32[8,512]{1,0:T(8,128)S(1)}, f32[8,512]{1,0:T(8,128)S(1)}, u32[]{:S(2)}, u32[]{:S(2)}) collective-permute-start(f32[8,512]{1,0:T(8,128)S(1)} %convert_reduce_fusion), channel_id=1, source_target_pairs={{0,128},{128,0},{1,129},{129,1},{2,130},{130,2},{3,131},{131,3},{4... | collective-permute-start | bytes 49160 | tf_op jit(solution)/shard_map/head/ppermute | solution.py:21

commit v5 on v3

--- a/solution.py
+++ b/solution.py
@@ -28,6 +28,12 @@
     return lax.ppermute(
         value, ("yl", "yh"), [(seat[y], seat[(y + distance) % 4]) for y in range(4)]
     )
+
+
+def quad(value):
+    other = shift(value, "yl", 2, 1)
+    chips = [lax.all_gather(block, "c", axis=0, tiled=True) for block in (value, other)]
+    return jnp.concatenate(chips, axis=0)
 
 
 def unpack(stack, rows):
@@ -72,7 +78,7 @@
         set_a = jnp.concatenate([across_x, shift(across_x, "c", 2, 1)], axis=0)
         normed_a, labels_a = unpack(set_a, rows)
         normed_b, labels_b = unpack(set_b, rows)
-        chip_rows = lax.all_gather(group_rows, "c", axis=0, tiled=True)
+        quad_rows = quad(group_rows)
     with jax.named_scope("scores"):
         total = normed_a.shape[0]
         scores = (
@@ -123,26 +129,35 @@
     with jax.named_scope("slopes"):
         along = jnp.sum(direction * pull_grad, axis=1, keepdims=True)
         slopes = ((pull_grad - direction * along) / row_norm).astype(bf16)
+    with jax.named_scope("head"):
+        blocks = slopes.reshape(4, share, proj)
+        returned = [shift(blocks[d], "zh", 4, -d) for d in range(4)]
+        quad_slopes = quad(slopes)
+        part = lax.dot_general(
+            quad_rows, quad_slopes, (((0,), (0,)), ((), ())), preferred_element_type=f32
+        ).astype(bf16)
+        part = part.reshape(64, 4, width // 256, proj)
+        seat = 2 * lax.axis_index("c") + lax.axis_index("yl")
+        part = lax.dynamic_index_in_dim(part, seat, axis=1, keepdims=False)
+        part, returned[1], returned[3] = lax.optimization_barrier(
+            (part, returned[1], returned[3])
+        )
+        spread = lax.all_to_all(part, KEY, split_axis=0, concat_axis=0, tiled=True)
+        piece = jnp.sum(spread.astype(f32), axis=0)
+        other = shift(piece, "yl", 2, 1)
+        first = lax.axis_index("yl") == 0
+        pair = jnp.concatenate([jnp.where(first, piece, other), jnp.where(first, other, piece)])
+        grad_head = lax.all_gather(pair, "c", axis=0, tiled=True)
     with jax.named_scope("route_back"):
-        blocks = slopes.reshape(4, share, proj)
-        returned = jnp.concatenate([shift(blocks[d], "zh", 4, -d) for d in range(4)], axis=0)
         own = lax.dot_general(
-            pick, returned, (((0,), (0,)), ((), ())), preferred_element_type=f32
+            pick,
+            jnp.concatenate(returned, axis=0),
+            (((0,), (0,)), ((), ())),
+            preferred_element_type=f32,
         ).astype(bf16)
         grad_embeddings = lax.dot_general(
             own, head_weight, (((1,), (1,)), ((), ())), preferred_element_type=f32
         ).astype(bf16)
-    with jax.named_scope("head"):
-        chip_slopes = lax.all_gather(slopes, "c", axis=0, tiled=True)
-        part = lax.dot_general(
-            chip_rows, chip_slopes, (((0,), (0,)), ((), ())), preferred_element_type=f32
-        ).astype(bf16)
-        part = part.reshape(64, 2, width // 128, proj)
-        part = lax.dynamic_index_in_dim(part, lax.axis_index("c"), axis=1, keepdims=False)
-        spread = lax.all_to_all(part, KEY, split_axis=0, concat_axis=0, tiled=True)
-        piece = jnp.sum(spread.astype(f32), axis=0)
-        piece = piece + shift(piece, "yl", 2, 1)
-        grad_head = lax.all_gather(piece, "c", axis=0, tiled=True)
     return (grad_embeddings, grad_head / loss_scale)
 
 

time: 126 us -> 129 us (1.024)
  waiting for transfers between devices: 39.2 us -> 34.8 us
  blocking collectives: 12 us -> 15.5 us
  starting transfers between devices: 54.8 us -> 57.9 us
    all_gather x3 -> x5, blocking collectives: 12 us -> 15.5 us  [the longest x4 9.77 us: quad(): lax.all_gather(block, 'c', axis=0, tiled=True)]
    all_to_all x1, waiting for transfers between devices: 10.2 us -> 7.02 us  [body(): spread = lax.all_to_all(part, KEY, split_axis=0, concat_axis=0, tiled=True)]
    ppermute x24 -> x26, starting transfers between devices: 38.9 us -> 41.2 us  [shift(): lax.ppermute(value, axis, [(i, (i + distance) % size) for i in range(size)])]
    ppermute x24 -> x26, waiting for transfers between devices: 29 us -> 27.8 us  [shift(): lax.ppermute(value, axis, [(i, (i + distance) % size) for i in range(size)])]
  transfers between devices with their start and end apart: 31 -> 33, of which waited for: 16 -> 16; matrix products, arithmetic and copies ran while one was open for 3% -> 6% of each run, Pallas kernels for 0% -> 0%
where the time goes in v5:
time: 129 us
  starting transfers between devices  57.9 us (45%)
  waiting for transfers between devices  34.8 us (27%)
  blocking collectives  15.5 us (12%)
  matrix products  8.95 us (7%)
  other arithmetic  8.61 us (7%)
  local copies, waits for them, and re-layouts  1.7 us (1%)
    ppermute x26, starting transfers between devices, shift(): lax.ppermute(value, axis, [(i, (i + distance) % size) for i in range(size)])  41.2 us
    ppermute x26, waiting for transfers between devices, shift(): lax.ppermute(value, axis, [(i, (i + distance) % size) for i in range(size)])  27.8 us
    all_gather x4, blocking collectives, quad(): lax.all_gather(block, 'c', axis=0, tiled=True)  9.77 us
    ppermute x6, starting transfers between devices, shift_y(): lax.ppermute(value, ('yl', 'yh'), [(seat[y], seat[(y + distance) % 4]) fo...  9.71 us
    all_to_all x1, waiting for transfers between devices, body(): spread = lax.all_to_all(part, KEY, split_axis=0, concat_axis=0, tiled=True)  7.02 us
    all_to_all x1, starting transfers between devices, body(): spread = lax.all_to_all(part, KEY, split_axis=0, concat_axis=0, tiled=True)  7.01 us
    all_gather x1, blocking collectives, body(): grad_head = lax.all_gather(pair, 'c', axis=0, tiled=True)  5.76 us
    dot_general x2, matrix products, pull_rows(): part = jnp.dot(coefficient, normed_b, preferred_element_type=f32)  3.6 us
  transfers between devices with their start and end apart: 33, of which 16 were waited for; matrix products, arithmetic and copies ran while one was open for 6% of the time, Pallas kernels for 0%

profile of v5, /device:TPU:1, one launch (start us, length us, event | category | flops | bytes accessed | tf_op | source)
XLA Modules:
  0.0 128.7 jit_solution(15035209402641092665)
XLA Ops:
  2.3 1.2 convolution_convert_fusion
  3.5 3.9 %collective-permute-start = (bf16[32,1152]{1,0:T(8,128)(2,1)S(1)}, bf16[32,1152]{1,0:T(8,128)(2,1)S(1)}, u32[]{:S(2)}, u32[]{:S(2)}) collective-permute-start(bf16[32,1152]{1,0:T(8,128)(2,1)S(1)} %get-tuple-element.24), channel_id=1, source_target_pairs={{0,4},{4,8},{8,12},{12,0},{1,5},{5,9},{9,13},{13,1},{2,6},{6,10},{... | collective-permute-start | bytes 221192 | tf_op jit(solution)/shard_map/route_out/ppermute | solution.py:21
  7.4 5.1 %collective-permute-start.1 = (bf16[32,1152]{1,0:T(8,128)(2,1)S(1)}, bf16[32,1152]{1,0:T(8,128)(2,1)S(1)}, u32[]{:S(2)}, u32[]{:S(2)}) collective-permute-start(bf16[32,1152]{1,0:T(8,128)(2,1)S(1)} %get-tuple-element.23), channel_id=1, source_target_pairs={{0,8},{4,12},{8,0},{12,4},{1,9},{5,13},{9,1},{13,5},{2,10},{6,14},... | collective-permute-start | bytes 221192 | tf_op jit(solution)/shard_map/route_out/ppermute | solution.py:21
  12.6 2.4 %collective-permute-start.2 = (bf16[32,1152]{1,0:T(8,128)(2,1)S(1)}, bf16[32,1152]{1,0:T(8,128)(2,1)S(1)}, u32[]{:S(2)}, u32[]{:S(2)}) collective-permute-start(bf16[32,1152]{1,0:T(8,128)(2,1)S(1)} %get-tuple-element.22), channel_id=1, source_target_pairs={{0,12},{4,0},{8,4},{12,8},{1,13},{5,1},{9,5},{13,9},{2,14},{6,2},{... | collective-permute-start | bytes 221192 | tf_op jit(solution)/shard_map/route_out/ppermute | solution.py:21
  14.9 2.0 %collective-permute-done.1 = bf16[32,1152]{1,0:T(8,128)(2,1)S(1)} collective-permute-done((bf16[32,1152]{1,0:T(8,128)(2,1)S(1)}, bf16[32,1152]{1,0:T(8,128)(2,1)S(1)}, u32[]{:S(2)}, u32[]{:S(2)}) %collective-permute-start.1) | collective-permute-done | bytes 73760 | tf_op jit(solution)/shard_map/route_out/ppermute | solution.py:21
  16.9 3.9 %collective-permute-done.2 = bf16[32,1152]{1,0:T(8,128)(2,1)S(1)} collective-permute-done((bf16[32,1152]{1,0:T(8,128)(2,1)S(1)}, bf16[32,1152]{1,0:T(8,128)(2,1)S(1)}, u32[]{:S(2)}, u32[]{:S(2)}) %collective-permute-start.2) | collective-permute-done | bytes 73760 | tf_op jit(solution)/shard_map/route_out/ppermute | solution.py:21
  21.6 1.3 collective-permute-start.3
  22.9 2.5 %collective-permute-start.4 = (bf16[144,512]{1,0:T(8,128)(2,1)S(1)}, bf16[144,512]{1,0:T(8,128)(2,1)S(1)}, u32[]{:S(2)}, u32[]{:S(2)}) collective-permute-start(bf16[144,512]{1,0:T(8,128)(2,1)S(1)} %get-tuple-element.26), channel_id=1, source_target_pairs={{0,32},{16,48},{32,0},{48,16},{1,33},{17,49},{33,1},{49,17},{2,34}... | collective-permute-start | bytes 442376 | tf_op jit(solution)/shard_map/gather_sets/ppermute | solution.py:21
  25.4 1.2 collective-permute-start.5
  26.6 1.3 %collective-permute-start.8 = (bf16[144,512]{1,0:T(8,128)(2,1)S(1)}, bf16[144,512]{1,0:T(8,128)(2,1)S(1)}, u32[]{:S(2)}, u32[]{:S(2)}) collective-permute-start(bf16[144,512]{1,0:T(8,128)(2,1)S(1)} %get-tuple-element.26), channel_id=1, source_target_pairs={{0,128},{128,1},{1,129},{129,0},{2,130},{130,3},{3,131},{131,2},{4... | collective-permute-start | bytes 442376 | tf_op jit(solution)/shard_map/gather_sets/ppermute | solution.py:28
  28.0 2.8 %collective-permute-start.10 = (bf16[144,512]{1,0:T(8,128)(2,1)S(1)}, bf16[144,512]{1,0:T(8,128)(2,1)S(1)}, u32[]{:S(2)}, u32[]{:S(2)}) collective-permute-start(bf16[144,512]{1,0:T(8,128)(2,1)S(1)} %get-tuple-element.26), channel_id=1, source_target_pairs={{0,1},{128,129},{1,0},{129,128},{2,3},{130,131},{3,2},{131,130},{4... | collective-permute-start | bytes 442376 | tf_op jit(solution)/shard_map/gather_sets/ppermute | solution.py:28
  30.8 1.2 collective-permute-done.4
  32.0 2.7 %collective-permute-start.12 = (bf16[144,512]{1,0:T(8,128)(2,1)S(1)}, bf16[144,512]{1,0:T(8,128)(2,1)S(1)}, u32[]{:S(2)}, u32[]{:S(2)}) collective-permute-start(bf16[144,512]{1,0:T(8,128)(2,1)S(1)} %get-tuple-element.26), channel_id=1, source_target_pairs={{0,129},{128,0},{1,128},{129,1},{2,131},{130,2},{3,130},{131,3},{4... | collective-permute-start | bytes 442376 | tf_op jit(solution)/shard_map/gather_sets/ppermute | solution.py:28
  34.8 1.7 %collective-permute-start.6 = (bf16[4,144,512]{2,1,0:T(8,128)(2,1)S(1)}, bf16[4,144,512]{2,1,0:T(8,128)(2,1)S(1)}, u32[]{:S(2)}, u32[]{:S(2)}) collective-permute-start(bf16[4,144,512]{2,1,0:T(8,128)(2,1)S(1)} %pad_maximum_fusion), channel_id=1, source_target_pairs={{0,64},{64,0},{1,65},{65,1},{2,66},{66,2},{3,67},{67,3},{4,68},{68... | collective-permute-start | bytes 1769480 | tf_op jit(solution)/shard_map/gather_sets/ppermute | solution.py:21
  36.7 1.5 %collective-permute-start.11 = (bf16[144,512]{1,0:T(8,128)(2,1)S(1)}, bf16[144,512]{1,0:T(8,128)(2,1)S(1)}, u32[]{:S(2)}, u32[]{:S(2)}) collective-permute-start(bf16[144,512]{1,0:T(8,128)(2,1)S(1)} %collective-permute-done.10), channel_id=1, source_target_pairs={{0,2},{2,0},{1,3},{3,1},{4,6},{6,4},{5,7},{7,5},{8,10},{10,8},{9,1... | collective-permute-start | bytes 442376 | tf_op jit(solution)/shard_map/gather_sets/ppermute | solution.py:21
  38.6 3.5 %collective-permute-done.9 = bf16[144,512]{1,0:T(8,128)(2,1)S(1)} collective-permute-done((bf16[144,512]{1,0:T(8,128)(2,1)S(1)}, bf16[144,512]{1,0:T(8,128)(2,1)S(1)}, u32[]{:S(2)}, u32[]{:S(2)}) %collective-permute-start.9) | collective-permute-done | bytes 147488 | tf_op jit(solution)/shard_map/gather_sets/ppermute | solution.py:21
  42.1 3.1 %collective-permute-done.11 = bf16[144,512]{1,0:T(8,128)(2,1)S(1)} collective-permute-done((bf16[144,512]{1,0:T(8,128)(2,1)S(1)}, bf16[144,512]{1,0:T(8,128)(2,1)S(1)}, u32[]{:S(2)}, u32[]{:S(2)}) %collective-permute-start.11) | collective-permute-done | bytes 147488 | tf_op jit(solution)/shard_map/gather_sets/ppermute | solution.py:21
  45.3 3.1 %collective-permute-done.13 = bf16[144,512]{1,0:T(8,128)(2,1)S(1)} collective-permute-done((bf16[144,512]{1,0:T(8,128)(2,1)S(1)}, bf16[144,512]{1,0:T(8,128)(2,1)S(1)}, u32[]{:S(2)}, u32[]{:S(2)}) %collective-permute-start.13) | collective-permute-done | bytes 147488 | tf_op jit(solution)/shard_map/gather_sets/ppermute | solution.py:21
  48.7 2.2 %fusion.9 = (f32[1024]{0:T(1024)S(1)}, f32[1024]{0:T(1024)S(1)}) fusion(pred[1024]{0:T(1024)(128)(4,1)S(1)} %iota_compare_fusion.5, s32[1024]{0:T(1024)S(1)} %bitcast.97, s32[1024]{0:T(1024)S(1)} %bitcast.99), kind=kLoop, calls=%fused_computation.16 | loop fusion | flops 8386560 | bytes 17408 | tf_op jit(solution)/shard_map/scores/reduce_sum | solution.py:96
  51.6 1.6 %fusion.58 = (f32[1024]{0:T(1024)S(1)}, f32[1024]{0:T(1024)S(1)}, f32[1024,1024]{1,0:T(8,128)S(1)}) fusion(bf16[1024,512]{1,0:T(8,128)(2,1)S(1)} %bitcast.79, bf16[1024,512]{1,0:T(8,128)(2,1)S(1)} %bitcast.76, pred[1024]{0:T(1024)(128)(4,1)S(1)} %iota_compare_fusion.5), kind=kOutput, calls=%fused_computation.122 | convolution fusion | flops 1080031232 | bytes 6300672 | tf_op jit(solution)/shard_map/scores/dot_general | solution.py:85
  53.3 1.1 collective-permute-start.14
  54.4 1.4 %collective-permute-done.18 = f32[2,4,2,128]{3,2,1,0:T(2,128)S(1)} collective-permute-done((f32[2,4,2,128]{3,2,1,0:T(2,128)S(1)}, f32[2,4,2,128]{3,2,1,0:T(2,128)S(1)}, u32[]{:S(2)}, u32[]{:S(2)}) %collective-permute-start.18) | collective-permute-done | bytes 8224 | tf_op jit(solution)/shard_map/totals/ppermute | solution.py:21
  56.0 1.0 collective-permute-start.19
  57.0 1.7 %collective-permute-start.21 = (f32[2,4,2,128]{3,2,1,0:T(2,128)S(1)}, f32[2,4,2,128]{3,2,1,0:T(2,128)S(1)}, u32[]{:S(2)}, u32[]{:S(2)}) collective-permute-start(f32[2,4,2,128]{3,2,1,0:T(2,128)S(1)} %maximum_add_fusion.2), channel_id=1, source_target_pairs={{0,129},{128,0},{1,128},{129,1},{2,131},{130,2},{3,130},{131,3},{4... | collective-permute-start | bytes 24584 | tf_op jit(solution)/shard_map/totals/ppermute | solution.py:28
  58.7 1.8 %collective-permute-start.16 = (f32[2,2,4,128]{3,2,1,0:T(4,128)S(1)}, f32[2,2,4,128]{3,2,1,0:T(4,128)S(1)}, u32[]{:S(2)}, u32[]{:S(2)}) collective-permute-start(f32[2,2,4,128]{3,2,1,0:T(4,128)S(1)} %maximum_add_fusion), channel_id=1, source_target_pairs={{0,32},{16,48},{32,0},{48,16},{1,33},{17,49},{33,1},{49,17},{2,34}... | collective-permute-start | bytes 24584 | tf_op jit(solution)/shard_map/totals/ppermute | solution.py:21
  61.0 1.0 collective-permute-start.15
  63.1 1.7 %collective-permute-done.15 = f32[2,2,4,128]{3,2,1,0:T(4,128)S(1)} collective-permute-done((f32[2,2,4,128]{3,2,1,0:T(4,128)S(1)}, f32[2,2,4,128]{3,2,1,0:T(4,128)S(1)}, u32[]{:S(2)}, u32[]{:S(2)}) %collective-permute-start.15) | collective-permute-done | bytes 8224 | tf_op jit(solution)/shard_map/totals/ppermute | solution.py:21
  64.8 1.0 fusion.5
  65.9 1.7 %fusion.67 = f32[4,128,512]{2,1,0:T(8,128)} fusion(bf16[4,128,1024]{2,1,0:T(8,128)(2,1)S(1)} %bitcast.75, bf16[1024,512,1]{1,0,2:T(8,128)(2,1)S(1)} %bitcast.77), kind=kOutput, calls=%fused_computation.131 | convolution fusion | flops 536870912 | bytes 3145728 | tf_op jit(solution)/shard_map/pull/dot_general | solution.py:122
  67.5 5.5 %collective-permute-start.22 = (f32[4,128,512]{2,1,0:T(8,128)}, f32[4,128,512]{2,1,0:T(8,128)}, u32[]{:S(2)}, u32[]{:S(2)}) collective-permute-start(f32[4,128,512]{2,1,0:T(8,128)} %fusion.67), channel_id=1, source_target_pairs={{0,64},{64,0},{1,65},{65,1},{2,66},{66,2},{3,67},{67,3},{4,68},{68... | collective-permute-start | bytes 3145736 | tf_op jit(solution)/shard_map/pull/ppermute | solution.py:21
  73.2 2.5 %all_gather.15 = bf16[256,1024]{1,0:T(8,128)(2,1)S(1)} all-gather(bf16[128,1024]{1,0:T(8,128)(2,1)S(1)} %slice.231), channel_id=1, replica_groups=mesh['yl'=2,'c'=2,'x'=4,'zh'=4,'zl'=2,'yh'=2] {'c'}, dimensions={0}, use_global_device_ids=true | all-gather | bytes 786432 | tf_op jit(solution)/shard_map/gather_sets/all_gather | solution.py:35
  75.7 1.9 %fusion.66 = f32[4,128,512]{2,1,0:T(8,128)S(1)} fusion(bf16[4,128,1024]{2,1,0:T(8,128)(2,1)S(1)} %bitcast.74, bf16[1024,512,1]{1,0,2:T(8,128)(2,1)} %bitcast.78), kind=kOutput, calls=%fused_computation.130 | convolution fusion | flops 536870912 | bytes 3145728 | tf_op jit(solution)/shard_map/pull/dot_general | solution.py:122
  77.7 1.5 %fusion.59 = (bf16[4,128,512]{2,1,0:T(8,128)(2,1)S(1)}, f32[4,128,512]{2,1,0:T(8,128)S(1)}) fusion(f32[4,128,512]{2,1,0:T(8,128)S(1)} %fusion.66, f32[4,128,512]{2,1,0:T(8,128)} %collective-permute-done.22), kind=kLoop, calls=%fused_computation.123 | loop fusion | flops 524288 | bytes 3670016 | tf_op jit(solution)/shard_map/convert.2
  79.5 1.0 collective-permute-start.24
  81.1 2.6 %all_gather.16 = bf16[256,1024]{1,0:T(8,128)(2,1)S(1)} all-gather(bf16[128,1024]{1,0:T(8,128)(2,1)S(1)} %collective-permute-done.26), channel_id=1, replica_groups=mesh['yl'=2,'c'=2,'x'=4,'zh'=4,'zl'=2,'yh'=2] {'c'}, dimensions={0}, use_global_device_ids=true | all-gather | bytes 786432 | tf_op jit(solution)/shard_map/gather_sets/all_gather | solution.py:35
  84.2 1.6 %collective-permute-done.24 = bf16[128,512]{1,0:T(8,128)(2,1)S(1)} collective-permute-done((bf16[128,512]{1,0:T(8,128)(2,1)S(1)}, bf16[128,512]{1,0:T(8,128)(2,1)S(1)}, u32[]{:S(2)}, u32[]{:S(2)}) %collective-permute-start.24) | collective-permute-done | bytes 131104 | tf_op jit(solution)/shard_map/pull/ppermute | solution.py:21
  85.8 3.5 %collective-permute-done.25 = bf16[128,512]{1,0:T(8,128)(2,1)S(1)} collective-permute-done((bf16[128,512]{1,0:T(8,128)(2,1)S(1)}, bf16[128,512]{1,0:T(8,128)(2,1)S(1)}, u32[]{:S(2)}, u32[]{:S(2)}) %collective-permute-start.25) | collective-permute-done | bytes 131104 | tf_op jit(solution)/shard_map/pull/ppermute | solution.py:21
  89.7 1.2 collective-permute-start.27
  90.8 3.1 %collective-permute-start.28 = (bf16[32,512]{1,0:T(8,128)(2,1)S(1)}, bf16[32,512]{1,0:T(8,128)(2,1)S(1)}, u32[]{:S(2)}, u32[]{:S(2)}) collective-permute-start(bf16[32,512]{1,0:T(8,128)(2,1)S(1)} %get-tuple-element.30), channel_id=1, source_target_pairs={{0,12},{4,0},{8,4},{12,8},{1,13},{5,1},{9,5},{13,9},{2,14},{6,2},{... | collective-permute-start | bytes 98312 | tf_op jit(solution)/shard_map/head/ppermute | solution.py:21
  94.0 2.7 %all_gather.17 = bf16[256,512]{1,0:T(8,128)(2,1)S(1)} all-gather(bf16[128,512]{1,0:T(8,128)(2,1)S(1)} %divide_convert_fusion), channel_id=1, replica_groups=mesh['yl'=2,'c'=2,'x'=4,'zh'=4,'zl'=2,'yh'=2] {'c'}, dimensions={0}, use_global_device_ids=true | all-gather | bytes 393216 | tf_op jit(solution)/shard_map/head/all_gather | solution.py:35
  96.6 2.0 %all_gather.18 = bf16[256,512]{1,0:T(8,128)(2,1)S(1)} all-gather(bf16[128,512]{1,0:T(8,128)(2,1)S(1)} %collective-permute-done.27), channel_id=1, replica_groups=mesh['yl'=2,'c'=2,'x'=4,'zh'=4,'zl'=2,'yh'=2] {'c'}, dimensions={0}, use_global_device_ids=true | all-gather | bytes 393216 | tf_op jit(solution)/shard_map/head/all_gather | solution.py:35
  99.7 0.8 dynamic-slice_bitcast_fusion
  100.5 7.0 %all-to-all-start = ((bf16[64,4,512]{2,1,0:T(4,128)(2,1)}), bf16[64,4,512]{2,1,0:T(4,128)(2,1)S(1)}, u32[]{:S(2)}, u32[]{:S(2)}) async-start(bf16[64,4,512]{2,1,0:T(4,128)(2,1)} %dynamic-slice_bitcast_fusion), calls=%async_computation | async-start | bytes 524288 | tf_op jit(solution)/shard_map/head/all_to_all | solution.py:145
  107.5 5.0 %collective-permute-start.30 = (bf16[32,512]{1,0:T(8,128)(2,1)S(1)}, bf16[32,512]{1,0:T(8,128)(2,1)S(1)}, u32[]{:S(2)}, u32[]{:S(2)}) collective-permute-start(bf16[32,512]{1,0:T(8,128)(2,1)S(1)} %get-tuple-element.28), channel_id=1, source_target_pairs={{0,8},{4,12},{8,0},{12,4},{1,9},{5,13},{9,1},{13,5},{2,10},{6,14},... | collective-permute-start | bytes 98312 | tf_op jit(solution)/shard_map/head/ppermute | solution.py:21
  112.5 7.0 %all-to-all-done = bf16[64,4,512]{2,1,0:T(4,128)(2,1)S(1)} async-done(((bf16[64,4,512]{2,1,0:T(4,128)(2,1)}), bf16[64,4,512]{2,1,0:T(4,128)(2,1)S(1)}, u32[]{:S(2)}, u32[]{:S(2)}) %all-to-all-start) | async-done | bytes 262176 | tf_op jit(solution)/shard_map/head/all_to_all | solution.py:145
  119.9 1.4 %convolution_convert_fusion.2 = bf16[128,1024]{1,0:T(8,128)(2,1)} fusion(bf16[1024,512]{1,0:T(8,128)(2,1)S(1)} %copy-done, bf16[32,512]{1,0:T(8,128)(2,1)S(1)} %collective-permute-done.29, bf16[32,512]{1,0:T(8,128)(2,1)S(1)} %collective-permute-done.30, bf16[32,512]{1,0:T(8,128)(2,1)S(1)} %collective-permute-done.28, ...), kind=kOutput, calls=%fused_computation.18 | convolution fusion | flops 151732224 | bytes 1442304 | tf_op jit(solution)/shard_map/route_back/dot_general | solution.py:158
  121.3 1.0 collective-permute-done.31
  122.3 5.8 %all_gather.19 = f32[16,512]{1,0:T(8,128)S(1)} all-gather(f32[8,512]{1,0:T(8,128)S(1)} %pad_maximum_fusion.3), channel_id=1, replica_groups=mesh['yl'=2,'c'=2,'x'=4,'zh'=4,'zl'=2,'yh'=2] {'c'}, dimensions={0}, use_global_device_ids=true | all-gather | bytes 49152 | tf_op jit(solution)/shard_map/head/all_gather | solution.py:150
  (103 shorter events, 9.7 us)
Async XLA Ops:
  0.6 20.2 %copy-start = (bf16[1024,512]{1,0:T(8,128)(2,1)S(1)}, bf16[1024,512]{1,0:T(8,128)(2,1)}, u32[]{:S(2)}) copy-start(bf16[1024,512]{1,0:T(8,128)(2,1)} %param.7) | copy-start | bytes 3145732
  3.5 11.4 %collective-permute-start = (bf16[32,1152]{1,0:T(8,128)(2,1)S(1)}, bf16[32,1152]{1,0:T(8,128)(2,1)S(1)}, u32[]{:S(2)}, u32[]{:S(2)}) collective-permute-start(bf16[32,1152]{1,0:T(8,128)(2,1)S(1)} %get-tuple-element.24), channel_id=1, source_target_pairs={{0,4},{4,8},{8,12},{12,0},{1,5},{5,9},{9,13},{13,1},{2,6},{6,10},{... | collective-permute-start | bytes 221192 | tf_op jit(solution)/shard_map/route_out/ppermute | solution.py:21
  7.4 9.5 %collective-permute-start.1 = (bf16[32,1152]{1,0:T(8,128)(2,1)S(1)}, bf16[32,1152]{1,0:T(8,128)(2,1)S(1)}, u32[]{:S(2)}, u32[]{:S(2)}) collective-permute-start(bf16[32,1152]{1,0:T(8,128)(2,1)S(1)} %get-tuple-element.23), channel_id=1, source_target_pairs={{0,8},{4,12},{8,0},{12,4},{1,9},{5,13},{9,1},{13,5},{2,10},{6,14},... | collective-permute-start | bytes 221192 | tf_op jit(solution)/shard_map/route_out/ppermute | solution.py:21
  12.6 8.3 %collective-permute-start.2 = (bf16[32,1152]{1,0:T(8,128)(2,1)S(1)}, bf16[32,1152]{1,0:T(8,128)(2,1)S(1)}, u32[]{:S(2)}, u32[]{:S(2)}) collective-permute-start(bf16[32,1152]{1,0:T(8,128)(2,1)S(1)} %get-tuple-element.22), channel_id=1, source_target_pairs={{0,12},{4,0},{8,4},{12,8},{1,13},{5,1},{9,5},{13,9},{2,14},{6,2},{... | collective-permute-start | bytes 221192 | tf_op jit(solution)/shard_map/route_out/ppermute | solution.py:21
  21.6 6.3 %collective-permute-start.3 = (bf16[144,512]{1,0:T(8,128)(2,1)S(1)}, bf16[144,512]{1,0:T(8,128)(2,1)S(1)}, u32[]{:S(2)}, u32[]{:S(2)}) collective-permute-start(bf16[144,512]{1,0:T(8,128)(2,1)S(1)} %get-tuple-element.26), channel_id=1, source_target_pairs={{0,16},{16,32},{32,48},{48,0},{1,17},{17,33},{33,49},{49,1},{2,18}... | collective-permute-start | bytes 442376 | tf_op jit(solution)/shard_map/gather_sets/ppermute | solution.py:21
  22.9 9.1 %collective-permute-start.4 = (bf16[144,512]{1,0:T(8,128)(2,1)S(1)}, bf16[144,512]{1,0:T(8,128)(2,1)S(1)}, u32[]{:S(2)}, u32[]{:S(2)}) collective-permute-start(bf16[144,512]{1,0:T(8,128)(2,1)S(1)} %get-tuple-element.26), channel_id=1, source_target_pairs={{0,32},{16,48},{32,0},{48,16},{1,33},{17,49},{33,1},{49,17},{2,34}... | collective-permute-start | bytes 442376 | tf_op jit(solution)/shard_map/gather_sets/ppermute | solution.py:21
  25.4 9.4 %collective-permute-start.5 = (bf16[144,512]{1,0:T(8,128)(2,1)S(1)}, bf16[144,512]{1,0:T(8,128)(2,1)S(1)}, u32[]{:S(2)}, u32[]{:S(2)}) collective-permute-start(bf16[144,512]{1,0:T(8,128)(2,1)S(1)} %get-tuple-element.26), channel_id=1, source_target_pairs={{0,48},{16,0},{32,16},{48,32},{1,49},{17,1},{33,17},{49,33},{2,50}... | collective-permute-start | bytes 442376 | tf_op jit(solution)/shard_map/gather_sets/ppermute | solution.py:21
  26.5 11.7 %collective-permute-start.7 = (bf16[144,512]{1,0:T(8,128)(2,1)S(1)}, bf16[144,512]{1,0:T(8,128)(2,1)S(1)}, u32[]{:S(2)}, u32[]{:S(2)}) collective-permute-start(bf16[144,512]{1,0:T(8,128)(2,1)S(1)} %get-tuple-element.26), channel_id=1, source_target_pairs={{0,2},{2,0},{1,3},{3,1},{4,6},{6,4},{5,7},{7,5},{8,10},{10,8},{9,1... | collective-permute-start | bytes 442376 | tf_op jit(solution)/shard_map/gather_sets/ppermute | solution.py:21
  26.6 10.0 %collective-permute-start.8 = (bf16[144,512]{1,0:T(8,128)(2,1)S(1)}, bf16[144,512]{1,0:T(8,128)(2,1)S(1)}, u32[]{:S(2)}, u32[]{:S(2)}) collective-permute-start(bf16[144,512]{1,0:T(8,128)(2,1)S(1)} %get-tuple-element.26), channel_id=1, source_target_pairs={{0,128},{128,1},{1,129},{129,0},{2,130},{130,3},{3,131},{131,2},{4... | collective-permute-start | bytes 442376 | tf_op jit(solution)/shard_map/gather_sets/ppermute | solution.py:28
  28.0 8.7 %collective-permute-start.10 = (bf16[144,512]{1,0:T(8,128)(2,1)S(1)}, bf16[144,512]{1,0:T(8,128)(2,1)S(1)}, u32[]{:S(2)}, u32[]{:S(2)}) collective-permute-start(bf16[144,512]{1,0:T(8,128)(2,1)S(1)} %get-tuple-element.26), channel_id=1, source_target_pairs={{0,1},{128,129},{1,0},{129,128},{2,3},{130,131},{3,2},{131,130},{4... | collective-permute-start | bytes 442376 | tf_op jit(solution)/shard_map/gather_sets/ppermute | solution.py:28
  32.0 6.3 %collective-permute-start.12 = (bf16[144,512]{1,0:T(8,128)(2,1)S(1)}, bf16[144,512]{1,0:T(8,128)(2,1)S(1)}, u32[]{:S(2)}, u32[]{:S(2)}) collective-permute-start(bf16[144,512]{1,0:T(8,128)(2,1)S(1)} %get-tuple-element.26), channel_id=1, source_target_pairs={{0,129},{128,0},{1,128},{129,1},{2,131},{130,2},{3,130},{131,3},{4... | collective-permute-start | bytes 442376 | tf_op jit(solution)/shard_map/gather_sets/ppermute | solution.py:28
  34.8 13.7 %collective-permute-start.6 = (bf16[4,144,512]{2,1,0:T(8,128)(2,1)S(1)}, bf16[4,144,512]{2,1,0:T(8,128)(2,1)S(1)}, u32[]{:S(2)}, u32[]{:S(2)}) collective-permute-start(bf16[4,144,512]{2,1,0:T(8,128)(2,1)S(1)} %pad_maximum_fusion), channel_id=1, source_target_pairs={{0,64},{64,0},{1,65},{65,1},{2,66},{66,2},{3,67},{67,3},{4,68},{68... | collective-permute-start | bytes 1769480 | tf_op jit(solution)/shard_map/gather_sets/ppermute | solution.py:21
  36.6 5.5 %collective-permute-start.9 = (bf16[144,512]{1,0:T(8,128)(2,1)S(1)}, bf16[144,512]{1,0:T(8,128)(2,1)S(1)}, u32[]{:S(2)}, u32[]{:S(2)}) collective-permute-start(bf16[144,512]{1,0:T(8,128)(2,1)S(1)} %collective-permute-done.8), channel_id=1, source_target_pairs={{0,2},{2,0},{1,3},{3,1},{4,6},{6,4},{5,7},{7,5},{8,10},{10,8},{9,1... | collective-permute-start | bytes 442376 | tf_op jit(solution)/shard_map/gather_sets/ppermute | solution.py:21
  36.7 8.6 %collective-permute-start.11 = (bf16[144,512]{1,0:T(8,128)(2,1)S(1)}, bf16[144,512]{1,0:T(8,128)(2,1)S(1)}, u32[]{:S(2)}, u32[]{:S(2)}) collective-permute-start(bf16[144,512]{1,0:T(8,128)(2,1)S(1)} %collective-permute-done.10), channel_id=1, source_target_pairs={{0,2},{2,0},{1,3},{3,1},{4,6},{6,4},{5,7},{7,5},{8,10},{10,8},{9,1... | collective-permute-start | bytes 442376 | tf_op jit(solution)/shard_map/gather_sets/ppermute | solution.py:21
  38.3 10.2 %collective-permute-start.13 = (bf16[144,512]{1,0:T(8,128)(2,1)S(1)}, bf16[144,512]{1,0:T(8,128)(2,1)S(1)}, u32[]{:S(2)}, u32[]{:S(2)}) collective-permute-start(bf16[144,512]{1,0:T(8,128)(2,1)S(1)} %collective-permute-done.12), channel_id=1, source_target_pairs={{0,2},{2,0},{1,3},{3,1},{4,6},{6,4},{5,7},{7,5},{8,10},{10,8},{9,1... | collective-permute-start | bytes 442376 | tf_op jit(solution)/shard_map/gather_sets/ppermute | solution.py:21
  48.5 17.3 %copy-start.1 = (bf16[8,128,512]{2,1,0:T(8,128)(2,1)}, bf16[8,128,512]{2,1,0:T(8,128)(2,1)S(1)}, u32[]{:S(2)}) copy-start(bf16[8,128,512]{2,1,0:T(8,128)(2,1)S(1)} %slice.233) | copy-start | bytes 3145732
  53.2 2.6 %collective-permute-start.18 = (f32[2,4,2,128]{3,2,1,0:T(2,128)S(1)}, f32[2,4,2,128]{3,2,1,0:T(2,128)S(1)}, u32[]{:S(2)}, u32[]{:S(2)}) collective-permute-start(f32[2,4,2,128]{3,2,1,0:T(2,128)S(1)} %pad_maximum_fusion.5), channel_id=1, source_target_pairs={{0,2},{2,0},{1,3},{3,1},{4,6},{6,4},{5,7},{7,5},{8,10},{10,8},{9,1... | collective-permute-start | bytes 24584 | tf_op jit(solution)/shard_map/totals/ppermute | solution.py:21
  53.3 5.4 %collective-permute-start.14 = (f32[2,2,4,128]{3,2,1,0:T(4,128)S(1)}, f32[2,2,4,128]{3,2,1,0:T(4,128)S(1)}, u32[]{:S(2)}, u32[]{:S(2)}) collective-permute-start(f32[2,2,4,128]{3,2,1,0:T(4,128)S(1)} %pad_maximum_fusion.4), channel_id=1, source_target_pairs={{0,64},{64,0},{1,65},{65,1},{2,66},{66,2},{3,67},{67,3},{4,68},{68... | collective-permute-start | bytes 24584 | tf_op jit(solution)/shard_map/totals/ppermute | solution.py:21
  55.9 6.2 %collective-permute-start.20 = (f32[2,4,2,128]{3,2,1,0:T(2,128)S(1)}, f32[2,4,2,128]{3,2,1,0:T(2,128)S(1)}, u32[]{:S(2)}, u32[]{:S(2)}) collective-permute-start(f32[2,4,2,128]{3,2,1,0:T(2,128)S(1)} %maximum_add_fusion.2), channel_id=1, source_target_pairs={{0,1},{128,129},{1,0},{129,128},{2,3},{130,131},{3,2},{131,130},{4... | collective-permute-start | bytes 24584 | tf_op jit(solution)/shard_map/totals/ppermute | solution.py:28
  56.0 5.1 %collective-permute-start.19 = (f32[2,4,2,128]{3,2,1,0:T(2,128)S(1)}, f32[2,4,2,128]{3,2,1,0:T(2,128)S(1)}, u32[]{:S(2)}, u32[]{:S(2)}) collective-permute-start(f32[2,4,2,128]{3,2,1,0:T(2,128)S(1)} %maximum_add_fusion.2), channel_id=1, source_target_pairs={{0,128},{128,1},{1,129},{129,0},{2,130},{130,3},{3,131},{131,2},{4... | collective-permute-start | bytes 24584 | tf_op jit(solution)/shard_map/totals/ppermute | solution.py:28
  57.0 5.0 %collective-permute-start.21 = (f32[2,4,2,128]{3,2,1,0:T(2,128)S(1)}, f32[2,4,2,128]{3,2,1,0:T(2,128)S(1)}, u32[]{:S(2)}, u32[]{:S(2)}) collective-permute-start(f32[2,4,2,128]{3,2,1,0:T(2,128)S(1)} %maximum_add_fusion.2), channel_id=1, source_target_pairs={{0,129},{128,0},{1,128},{129,1},{2,131},{130,2},{3,130},{131,3},{4... | collective-permute-start | bytes 24584 | tf_op jit(solution)/shard_map/totals/ppermute | solution.py:28
  58.7 4.1 %collective-permute-start.16 = (f32[2,2,4,128]{3,2,1,0:T(4,128)S(1)}, f32[2,2,4,128]{3,2,1,0:T(4,128)S(1)}, u32[]{:S(2)}, u32[]{:S(2)}) collective-permute-start(f32[2,2,4,128]{3,2,1,0:T(4,128)S(1)} %maximum_add_fusion), channel_id=1, source_target_pairs={{0,32},{16,48},{32,0},{48,16},{1,33},{17,49},{33,1},{49,17},{2,34}... | collective-permute-start | bytes 24584 | tf_op jit(solution)/shard_map/totals/ppermute | solution.py:21
  60.5 2.5 %collective-permute-start.17 = (f32[2,2,4,128]{3,2,1,0:T(4,128)S(1)}, f32[2,2,4,128]{3,2,1,0:T(4,128)S(1)}, u32[]{:S(2)}, u32[]{:S(2)}) collective-permute-start(f32[2,2,4,128]{3,2,1,0:T(4,128)S(1)} %maximum_add_fusion), channel_id=1, source_target_pairs={{0,48},{16,0},{32,16},{48,32},{1,49},{17,1},{33,17},{49,33},{2,50}... | collective-permute-start | bytes 24584 | tf_op jit(solution)/shard_map/totals/ppermute | solution.py:21
  61.0 3.7 %collective-permute-start.15 = (f32[2,2,4,128]{3,2,1,0:T(4,128)S(1)}, f32[2,2,4,128]{3,2,1,0:T(4,128)S(1)}, u32[]{:S(2)}, u32[]{:S(2)}) collective-permute-start(f32[2,2,4,128]{3,2,1,0:T(4,128)S(1)} %maximum_add_fusion), channel_id=1, source_target_pairs={{0,16},{16,32},{32,48},{48,0},{1,17},{17,33},{33,49},{49,1},{2,18}... | collective-permute-start | bytes 24584 | tf_op jit(solution)/shard_map/totals/ppermute | solution.py:21
  67.5 10.1 %collective-permute-start.22 = (f32[4,128,512]{2,1,0:T(8,128)}, f32[4,128,512]{2,1,0:T(8,128)}, u32[]{:S(2)}, u32[]{:S(2)}) collective-permute-start(f32[4,128,512]{2,1,0:T(8,128)} %fusion.67), channel_id=1, source_target_pairs={{0,64},{64,0},{1,65},{65,1},{2,66},{66,2},{3,67},{67,3},{4,68},{68... | collective-permute-start | bytes 3145736 | tf_op jit(solution)/shard_map/pull/ppermute | solution.py:21
  73.1 8.0 %collective-permute-start.26 = (bf16[128,1024]{1,0:T(8,128)(2,1)S(1)}, bf16[128,1024]{1,0:T(8,128)(2,1)S(1)}, u32[]{:S(2)}, u32[]{:S(2)}) collective-permute-start(bf16[128,1024]{1,0:T(8,128)(2,1)S(1)} %slice.231), channel_id=1, source_target_pairs={{0,128},{128,0},{1,129},{129,1},{2,130},{130,2},{3,131},{131,3},{4... | collective-permute-start | bytes 786440 | tf_op jit(solution)/shard_map/gather_sets/ppermute | solution.py:21
  79.2 5.0 %collective-permute-start.23 = (bf16[128,512]{1,0:T(8,128)(2,1)S(1)}, bf16[128,512]{1,0:T(8,128)(2,1)S(1)}, u32[]{:S(2)}, u32[]{:S(2)}) collective-permute-start(bf16[128,512]{1,0:T(8,128)(2,1)S(1)} %get-tuple-element.18), channel_id=1, source_target_pairs={{0,48},{16,0},{32,16},{48,32},{1,49},{17,1},{33,17},{49,33},{2,50}... | collective-permute-start | bytes 393224 | tf_op jit(solution)/shard_map/pull/ppermute | solution.py:21
  79.5 6.3 %collective-permute-start.24 = (bf16[128,512]{1,0:T(8,128)(2,1)S(1)}, bf16[128,512]{1,0:T(8,128)(2,1)S(1)}, u32[]{:S(2)}, u32[]{:S(2)}) collective-permute-start(bf16[128,512]{1,0:T(8,128)(2,1)S(1)} %get-tuple-element.20), channel_id=1, source_target_pairs={{0,32},{16,48},{32,0},{48,16},{1,33},{17,49},{33,1},{49,17},{2,34}... | collective-permute-start | bytes 393224 | tf_op jit(solution)/shard_map/pull/ppermute | solution.py:21
  80.5 8.9 %collective-permute-start.25 = (bf16[128,512]{1,0:T(8,128)(2,1)S(1)}, bf16[128,512]{1,0:T(8,128)(2,1)S(1)}, u32[]{:S(2)}, u32[]{:S(2)}) collective-permute-start(bf16[128,512]{1,0:T(8,128)(2,1)S(1)} %get-tuple-element.19), channel_id=1, source_target_pairs={{0,16},{16,32},{32,48},{48,0},{1,17},{17,33},{33,49},{49,1},{2,18}... | collective-permute-start | bytes 393224 | tf_op jit(solution)/shard_map/pull/ppermute | solution.py:21
  89.7 7.0 %collective-permute-start.27 = (bf16[128,512]{1,0:T(8,128)(2,1)S(1)}, bf16[128,512]{1,0:T(8,128)(2,1)S(1)}, u32[]{:S(2)}, u32[]{:S(2)}) collective-permute-start(bf16[128,512]{1,0:T(8,128)(2,1)S(1)} %divide_convert_fusion), channel_id=1, source_target_pairs={{0,128},{128,0},{1,129},{129,1},{2,130},{130,2},{3,131},{131,3},{4... | collective-permute-start | bytes 393224 | tf_op jit(solution)/shard_map/head/ppermute | solution.py:21
  90.8 9.7 %collective-permute-start.28 = (bf16[32,512]{1,0:T(8,128)(2,1)S(1)}, bf16[32,512]{1,0:T(8,128)(2,1)S(1)}, u32[]{:S(2)}, u32[]{:S(2)}) collective-permute-start(bf16[32,512]{1,0:T(8,128)(2,1)S(1)} %get-tuple-element.30), channel_id=1, source_target_pairs={{0,12},{4,0},{8,4},{12,8},{1,13},{5,1},{9,5},{13,9},{2,14},{6,2},{... | collective-permute-start | bytes 98312 | tf_op jit(solution)/shard_map/head/ppermute | solution.py:21
  94.0 6.5 %collective-permute-start.29 = (bf16[32,512]{1,0:T(8,128)(2,1)S(1)}, bf16[32,512]{1,0:T(8,128)(2,1)S(1)}, u32[]{:S(2)}, u32[]{:S(2)}) collective-permute-start(bf16[32,512]{1,0:T(8,128)(2,1)S(1)} %get-tuple-element.29), channel_id=1, source_target_pairs={{0,4},{4,8},{8,12},{12,0},{1,5},{5,9},{9,13},{13,1},{2,6},{6,10},{... | collective-permute-start | bytes 98312 | tf_op jit(solution)/shard_map/head/ppermute | solution.py:21
  100.5 19.0 %all-to-all-start = ((bf16[64,4,512]{2,1,0:T(4,128)(2,1)}), bf16[64,4,512]{2,1,0:T(4,128)(2,1)S(1)}, u32[]{:S(2)}, u32[]{:S(2)}) async-start(bf16[64,4,512]{2,1,0:T(4,128)(2,1)} %dynamic-slice_bitcast_fusion), calls=%async_computation | async-start | bytes 524288 | tf_op jit(solution)/shard_map/head/all_to_all | solution.py:145
  107.5 12.4 %collective-permute-start.30 = (bf16[32,512]{1,0:T(8,128)(2,1)S(1)}, bf16[32,512]{1,0:T(8,128)(2,1)S(1)}, u32[]{:S(2)}, u32[]{:S(2)}) collective-permute-start(bf16[32,512]{1,0:T(8,128)(2,1)S(1)} %get-tuple-element.28), channel_id=1, source_target_pairs={{0,8},{4,12},{8,0},{12,4},{1,9},{5,13},{9,1},{13,5},{2,10},{6,14},... | collective-permute-start | bytes 98312 | tf_op jit(solution)/shard_map/head/ppermute | solution.py:21
  119.7 2.6 %collective-permute-start.31 = (f32[4,512]{1,0:T(4,128)S(1)}, f32[4,512]{1,0:T(4,128)S(1)}, u32[]{:S(2)}, u32[]{:S(2)}) collective-permute-start(f32[4,512]{1,0:T(4,128)S(1)} %convert_reduce_fusion), channel_id=1, source_target_pairs={{0,128},{128,0},{1,129},{129,1},{2,130},{130,2},{3,131},{131,3},{4... | collective-permute-start | bytes 24584 | tf_op jit(solution)/shard_map/head/ppermute | solution.py:21
